TPU v7x, 256 devices: a whole 4x4x8 slice. The times are simulated.
256 devices in a mesh: band: 8 (over y, core), sub: 32 (over x, z).
Axes of the slice: x: 4, y: 4, z: 8, core: 2. Of those that a mesh axis runs over, the one named last changes fastest.
Arguments:
- background: float32 [64, 4, 768, 1536], P('band', None, 'sub'), may hold values from -18 to 18
- obs_columns: float32 [64, 4, 131072], P('band', None, 'sub'), may hold values from -18 to 18
- obs_owner: int32 [131072, 1], P('sub'), may hold values from 0 to 31; in each aligned block of 4096 rows (0 to 4095, 4096 to 8191, ...) at most 256 rows name the same one
- obs_cell: int32 [131072], P('sub'), may hold values from 0 to 36863
- lat_length: float32 [64, 4, 768], P('band'), may hold values from 1 to 2200
- lon_length: float32 [64, 4], P('band'), may hold values from 2 to 48
- vert_length: float32 [64, 4], P('band'), may hold values from 1 to 720
Outputs:
- filtered: float32 [64, 4, 768, 1536], P('band', None, 'sub')
Inputs may be any that keep to these rules, and one draw needn't show every extreme that they name: `obs_owner`: among the 4096 observations of one device no subdomain is named more than 256 times, and in every draw some device names some subdomain exactly 256 times.
All inputs are finite; a program needn't handle non-finite values.
Results may differ from a plain program's by a relative error of at most 0.0003.
Values sent between devices are 32-bit elements; how exact they have to be, the bound alone decides.
A program may use at most 128 MiB of HBM per device.

v0:
```python
import jax
import jax.numpy as jnp
from jax import lax
from jax.sharding import PartitionSpec as P

highest = lax.Precision.HIGHEST


def prefix(part, axis, combine, identity, reverse):
    count = lax.axis_size(axis)
    place = lax.axis_index(axis)
    ahead = count - 1 - place if reverse else place
    gathered = jax.tree.map(lambda a: lax.all_gather(a, axis), part)
    state = jax.tree.map(lambda a, e: jnp.zeros_like(a) + jnp.asarray(e, a.dtype), part, identity)

    def one(turn, state):
        source = count - 1 - turn if reverse else turn
        return combine(
            state, jax.tree.map(lambda a: lax.dynamic_index_in_dim(a, source, 0, False), gathered)
        )

    return lax.fori_loop(0, ahead, one, state)


def combine(earlier, later):
    return (earlier[0] * later[0], later[0] * earlier[1] + later[1])


def row_sweep(values, decays, reverse):
    group_count, scale_length, column_count = values.shape
    block_len = min(scale_length, 128)
    block_count = scale_length // block_len
    blocked = values.reshape(group_count, block_count, block_len, column_count)
    decay_blocks = decays.reshape(group_count, block_count, block_len)
    log_decay = jnp.log(decay_blocks)
    inclusive = jnp.cumsum(log_decay, axis=-1)
    exclusive = inclusive - log_decay
    position = jnp.arange(block_len)
    if reverse:
        log_gap = exclusive[..., None, :] - exclusive[..., :, None]
        lower_mask = position[None, :] >= position[:, None]
        entry_weight = jnp.exp(inclusive[..., -1:] - exclusive)
    else:
        log_gap = inclusive[..., :, None] - inclusive[..., None, :]
        lower_mask = position[:, None] >= position[None, :]
        entry_weight = jnp.exp(inclusive)
    weights = (
        jnp.where(lower_mask, jnp.exp(jnp.minimum(log_gap, 0.0)), 0.0)
        * (1.0 - decay_blocks)[..., None, :]
    )
    local_part = jnp.einsum("knij,knjc->knic", weights, blocked, precision=highest)
    pieces = [None] * block_count
    carry_state = jnp.zeros((group_count, column_count), jnp.float32)
    visit_order = range(block_count - 1, -1, -1) if reverse else range(block_count)
    for block_index in visit_order:
        piece_value = (
            local_part[:, block_index]
            + entry_weight[:, block_index, :, None] * carry_state[:, None, :]
        )
        pieces[block_index] = piece_value
        carry_state = piece_value[:, 0] if reverse else piece_value[:, -1]
    return jnp.concatenate(pieces, axis=1)


def cycle_sweep(values, decays, reverse):
    group_count, row_count, column_count = values.shape
    block_len = 128
    block_count = column_count // block_len
    log_decay = jnp.log(decays)
    position = jnp.arange(block_len, dtype=jnp.float32)
    if reverse:
        column_gap = position[None, :] - position[:, None]
    else:
        column_gap = position[:, None] - position[None, :]
    weights = jnp.where(
        column_gap[None] >= 0.0,
        jnp.exp(log_decay[:, None, None] * jnp.maximum(column_gap, 0.0)[None]),
        0.0,
    )
    weights = weights * (1.0 - decays)[:, None, None]
    blocked = values.reshape(group_count, row_count, block_count, block_len)
    local_part = jnp.einsum("krnj,kij->krni", blocked, weights, precision=highest)
    block_decay = jnp.exp(log_decay * block_len)[:, None]
    full_turn = (1.0 - jnp.exp(log_decay * column_count))[:, None]
    starts = [None] * block_count
    carry_state = jnp.zeros((group_count, row_count), jnp.float32)
    if reverse:
        edge_value = local_part[..., 0]
        for block_index in range(block_count - 1, -1, -1):
            starts[block_index] = carry_state
            carry_state = block_decay * carry_state + edge_value[:, :, block_index]
        wrapped = carry_state / full_turn
        incoming = jnp.stack(
            [
                starts[block_index]
                + jnp.exp(log_decay * block_len * (block_count - 1 - block_index))[:, None]
                * wrapped
                for block_index in range(block_count)
            ],
            axis=2,
        )
        within = jnp.exp(log_decay[:, None] * (block_len - position)[None, :])
    else:
        edge_value = local_part[..., -1]
        for block_index in range(block_count):
            starts[block_index] = carry_state
            carry_state = block_decay * carry_state + edge_value[:, :, block_index]
        wrapped = carry_state / full_turn
        incoming = jnp.stack(
            [
                starts[block_index]
                + jnp.exp(log_decay * block_len * block_index)[:, None] * wrapped
                for block_index in range(block_count)
            ],
            axis=2,
        )
        within = jnp.exp(log_decay[:, None] * (position + 1.0)[None, :])
    result = local_part + within[:, None, None, :] * incoming[..., None]
    return result.reshape(group_count, row_count, column_count)


def latitude_filter(values, decays):
    for reverse in (False, True, False, True):
        values = row_sweep(values, decays, reverse)
    return values


def longitude_filter(values, decays):
    for reverse in (False, True, False, True):
        values = cycle_sweep(values, decays, reverse)
    return values


def level_chain(values, decays, reverse):
    level_count = values.shape[0]
    visit_order = range(level_count - 1, -1, -1) if reverse else range(level_count)
    carry_state = jnp.zeros_like(values[0])
    level_gain = jnp.ones((values.shape[1],), jnp.float32)
    outputs = [None] * level_count
    carried = [None] * level_count
    for level_index in visit_order:
        factor = decays[level_index][:, None, None]
        carry_state = factor * carry_state + (1.0 - factor) * values[level_index]
        level_gain = level_gain * decays[level_index]
        outputs[level_index] = carry_state
        carried[level_index] = level_gain
    total_decay = level_gain[:, None, None]
    identity = (jnp.ones_like(total_decay), jnp.zeros_like(carry_state))
    incoming = prefix((total_decay, carry_state), "band", combine, identity, reverse)[1]
    return jnp.stack(
        [
            outputs[level_index] + carried[level_index][:, None, None] * incoming
            for level_index in range(level_count)
        ]
    )


def route_slots(owners, sub_count, capacity):
    matches = (owners[:, None] == jnp.arange(sub_count, dtype=jnp.int32)[None, :]).astype(jnp.int32)
    ranks = jnp.sum((jnp.cumsum(matches, axis=0) - 1) * matches, axis=1)
    return owners * capacity + ranks


def fill_slots(obs_values, obs_cell, slots, sub_count, capacity):
    group_count = obs_values.shape[0]
    sent_values = (
        jnp.zeros((group_count, sub_count * capacity), jnp.float32).at[:, slots].set(obs_values)
    )
    sent_cells = jnp.zeros((sub_count * capacity,), jnp.int32).at[slots].set(obs_cell)
    return (
        sent_values.reshape(group_count, sub_count, capacity),
        sent_cells.reshape(sub_count, capacity),
    )


def deposit(target, obs_values, cells):
    group_count = target.shape[0]
    flat = target.reshape(group_count, -1)
    flat = flat.at[:, cells.reshape(-1)].add(obs_values.reshape(group_count, -1))
    return flat.reshape(target.shape)


def per_device(background, obs_columns, obs_owner, obs_cell, lat_length, lon_length, vert_length):
    level_count, var_count, row_count, lon_count = background.shape
    sub_count = lax.axis_size("sub")
    sub_index = lax.axis_index("sub")
    group_count = level_count * var_count
    lat_count = row_count * sub_count
    tile_field = background.reshape(group_count, row_count, lon_count)
    obs_values = obs_columns.reshape(group_count, -1)
    owners = obs_owner[:, 0]
    capacity = 2 * owners.shape[0] // sub_count
    lat_decay = jnp.exp(-1.0 / lat_length).reshape(group_count, lat_count)
    lon_decay = jnp.exp(-1.0 / lon_length).reshape(group_count)
    slots = route_slots(owners, sub_count, capacity)
    sent_values, sent_cells = fill_slots(obs_values, obs_cell, slots, sub_count, capacity)
    got_values = lax.all_to_all(sent_values, "sub", split_axis=1, concat_axis=1, tiled=True)
    got_cells = lax.all_to_all(sent_cells, "sub", split_axis=0, concat_axis=0, tiled=True)
    tile_field = deposit(tile_field, got_values, got_cells)
    own_lat = lax.dynamic_slice_in_dim(lat_decay, sub_index, 1, 0)
    own_lon = lax.dynamic_slice_in_dim(lon_decay, sub_index, 1, 0)
    level_slab = latitude_filter(
        lax.all_to_all(tile_field, "sub", split_axis=0, concat_axis=1, tiled=True), own_lat
    )
    level_slab = longitude_filter(level_slab, own_lon)
    tile_field = lax.all_to_all(level_slab, "sub", split_axis=1, concat_axis=0, tiled=True)
    result = tile_field.reshape(level_count, var_count, row_count, lon_count)
    vert_decay = jnp.exp(-1.0 / vert_length)
    result = level_chain(result, vert_decay, False)
    result = level_chain(result, vert_decay, True)
    return result


def solution(mesh):
    placed = (
        P("band", None, "sub", None),
        P("band", None, "sub"),
        P("sub", None),
        P("sub"),
        P("band", None, None),
        P("band", None),
        P("band", None),
    )
    return jax.shard_map(
        per_device,
        mesh=mesh,
        in_specs=placed,
        out_specs=P("band", None, "sub", None),
        check_vma=False,
    )
```

profile of v0, /device:TPU:1, one launch (start us, length us, event | category | flops | bytes accessed | tf_op | source)
XLA Modules:
  0.0 639.2 jit_solution(11833946562720952195)
XLA Ops:
  7.3 9.2 %reduce-window.6 = s32[32,32,128]{2,1,0:T(8,128)S(1)} reduce-window(s32[32,32,128]{2,1,0:T(8,128)S(1)} %fusion.55, s32[]{:T(128)} %constant.117.clone.1), window={size=1x1x128 pad=0_0x0_0x127_0}, to_apply=%region_1.2 | reduce-window | flops 16646144 | bytes 1048580 | tf_op jit(solution)/shard_map/reduce-window
  19.6 16.3 %scatter_custom_fusion = s32[8192]{0:T(1024)} fusion(s32[4096]{0:T(1024)S(1)} %bitcast.433, s32[4096]{0:T(1024)} %param.14, s32[]{:T(128)} %constant.117.clone.1), kind=kCustom, calls=%fused_computation.248 | custom fusion | bytes 33280 | tf_op jit(solution)/shard_map/scatter | solution.py:169
  35.8 11.9 %all-to-all-start = ((s32[32,1,256]{2,1,0:T(1,128)}), s32[32,1,256]{2,1,0:T(1,128)S(1)}, u32[]{:S(2)}, u32[]{:S(2)}) async-start(s32[32,1,256]{2,1,0:T(1,128)} %bitcast.10), calls=%async_computation | async-start | bytes 65536 | tf_op jit(solution)/shard_map/all_to_all | solution.py:198
  49.5 12.9 %scatter_custom_fusion.1 = f32[32,8192]{0,1:T(8,128)} fusion(s32[4096]{0:T(1024)S(1)} %bitcast.434, f32[32,4096]{0,1:T(8,128)S(1)} %copy.99, f32[]{:T(128)} %constant.114.clone.1), kind=kCustom, calls=%fused_computation.27 | custom fusion | bytes 3145732 | tf_op jit(solution)/shard_map/scatter | solution.py:167
  62.4 3.6 copy.100
  66.0 9.5 %all-to-all-start.1 = ((f32[32,32,256]{2,0,1:T(8,128)}), f32[32,32,256]{2,0,1:T(8,128)S(1)}, u32[]{:S(2)}, u32[]{:S(2)}) async-start(f32[32,32,256]{2,0,1:T(8,128)} %copy.100), calls=%async_computation.1 | async-start | bytes 2097152 | tf_op jit(solution)/shard_map/all_to_all | solution.py:197
  75.5 7.3 %copy.146 = f32[4,8,24,1536]{3,1,2,0:T(8,128)} copy(f32[4,8,24,1536]{3,2,1,0:T(8,128)} %bitcast.395) | data formatting | bytes 9437184
  82.8 11.1 %copy.102 = f32[32,36864]{0,1:T(8,128)} copy(f32[32,36864]{1,0:T(8,128)} %bitcast.375) | data formatting | bytes 9437184 | tf_op jit(solution)/shard_map/reshape;reshape | solution.py:178
  94.0 6.2 all-to-all-done.1
  100.3 2.7 copy.103
  103.0 52.7 %scatter_fusion = f32[32,36864]{0,1:T(8,128)} fusion(f32[32,36864]{0,1:T(8,128)} %copy.102, s32[8192]{0:T(1024)S(1)} %bitcast.419, f32[8192,32]{1,0:T(8,128)} %copy.103), kind=kCustom, calls=%fused_computation.2 | custom fusion | flops 262144 | bytes 3178496 | tf_op jit(solution)/shard_map/scatter-add | solution.py:179
  155.7 13.6 %copy.104 = f32[32,24,1536]{2,1,0:T(8,128)} copy(f32[32,24,1536]{0,2,1:T(8,128)} %bitcast.372) | data formatting | bytes 9437184 | tf_op jit(solution)/shard_map/reshape | solution.py:180
  169.3 20.6 %all-to-all-start.2 = ((f32[32,24,1536]{2,1,0:T(8,128)}), f32[32,24,1536]{2,1,0:T(8,128)}, u32[]{:S(2)}, u32[]{:S(2)}) async-start(f32[32,24,1536]{2,1,0:T(8,128)} %copy.104), calls=%async_computation.2 | async-start | bytes 9437184 | tf_op jit(solution)/shard_map/all_to_all | solution.py:203
  193.3 103.8 %all-to-all-done.2 = f32[32,24,1536]{2,1,0:T(8,128)} async-done(((f32[32,24,1536]{2,1,0:T(8,128)}), f32[32,24,1536]{2,1,0:T(8,128)}, u32[]{:S(2)}, u32[]{:S(2)}) %all-to-all-start.2) | async-done | bytes 4718624 | tf_op jit(solution)/shard_map/all_to_all | solution.py:203
  297.2 6.7 %convolution_bitcast_fusion.3 = f32[1,6,128,1536]{3,2,1,0:T(8,128)S(1)} fusion(f32[6,128,1536]{2,1,0:T(8,128)} %bitcast.17, f32[6,128]{1,0:T(8,128)S(1)} %bitcast.411, f32[6,128]{1,0:T(8,128)S(1)} %bitcast.421, pred[128,128]{1,0:T(8,128)(4,1)S(1)} %iota_compare_fusion.2), kind=kOutput, calls=%fused_computation.20 | convolution fusion | flops 1812332544 | bytes 9459712 | tf_op jit(solution)/shard_map/knij,knjc->knic/dot_general | solution.py:51
  305.1 4.7 convolution_bitcast_fusion.2
  311.5 4.7 convolution_bitcast_fusion.1
  317.4 4.9 convolution_bitcast_fusion
  322.3 2.6 fusion.140
  324.9 2.3 copy.105
  327.2 2.3 copy.106
  329.5 2.3 copy.107
  331.8 2.3 copy.108
  335.2 1.4 copy.110
  351.8 4.8 fusion.79
  357.0 5.4 fusion.6
  362.4 3.4 dot_general.51
  366.1 5.2 fusion.3
  371.2 3.8 dot_general.53
  375.4 5.2 fusion
  380.6 3.4 dot_general.55
  384.3 2.7 multiply_add_fusion
  387.0 12.2 %copy.121 = f32[1,768,1536]{2,0,1:T(1,128)} copy(f32[1,768,1536]{1,2,0:T(8,128)} %bitcast.374) | data formatting | bytes 9437184 | tf_op jit(solution)/shard_map/reshape | solution.py:119
  399.3 6.7 %all-to-all-start.3 = ((f32[1,768,1536]{2,0,1:T(1,128)}), f32[1,768,1536]{2,0,1:T(1,128)}, u32[]{:S(2)}, u32[]{:S(2)}) async-start(f32[1,768,1536]{2,0,1:T(1,128)} %copy.121), calls=%async_computation.3 | async-start | bytes 9437184 | tf_op jit(solution)/shard_map/all_to_all | solution.py:206
  407.7 101.7 %all-to-all-done.3 = f32[1,768,1536]{2,0,1:T(1,128)} async-done(((f32[1,768,1536]{2,0,1:T(1,128)}), f32[1,768,1536]{2,0,1:T(1,128)}, u32[]{:S(2)}, u32[]{:S(2)}) %all-to-all-start.3) | async-done | bytes 4718624 | tf_op jit(solution)/shard_map/all_to_all | solution.py:206
  510.6 4.4 fusion.139
  516.2 1.6 fusion.40
  519.0 17.0 %all_gather.16 = f32[8,4,1,1]{1,3,2,0:T(1,128)} all-gather(f32[1,4,1,1]{1,3,2,0:T(1,128)S(1)} %get-tuple-element.255), channel_id=1, replica_groups=mesh['band'=8,'sub'=32] {'band'}, dimensions={0}, use_global_device_ids=true | all-gather | bytes 144 | tf_op jit(solution)/shard_map/all_gather | solution.py:13
  536.0 1.9 copy.137
  538.0 1.9 copy.138
  542.7 15.7 %all-gather.4.cloned.1.call-done = f32[8,4,24,1536]{3,2,1,0:T(8,128)} async-done(((f32[1,4,24,1536]{3,2,1,0:T(8,128)}), f32[8,4,24,1536]{3,2,1,0:T(8,128)}) %all-gather.4.cloned.1.call-update) | async-done | bytes 4718608 | tf_op jit(solution)/shard_map/all_gather | solution.py:13
  558.4 2.1 while.26
  560.6 4.5 multiply_add_fusion.1
  565.1 18.6 %all_gather.18 = f32[8,4,1,1]{1,3,2,0:T(1,128)} all-gather(f32[1,4,1,1]{1,3,2,0:T(1,128)} %get-tuple-element.254), channel_id=1, replica_groups=mesh['band'=8,'sub'=32] {'band'}, dimensions={0}, use_global_device_ids=true | all-gather | bytes 144 | tf_op jit(solution)/shard_map/all_gather | solution.py:13
  583.7 28.9 %all-gather.6.cloned.1.call-done = f32[32,24,1536]{2,1,0:T(8,128)} async-done(((f32[4,24,1536]{2,1,0:T(8,128)}), f32[32,24,1536]{2,1,0:T(8,128)}) %all-gather.6.cloned.1.call-update) | async-done | bytes 4718608 | tf_op jit(solution)/shard_map/all_gather | solution.py:13
  612.7 11.5 %while.27 = (s32[]{:T(128)}, f32[4,24,1536]{2,1,0:T(8,128)S(1)}, s32[]{:T(128)}, f32[8,4,1,1]{1,3,2,0:T(1,128)}, f32[8,4,24,1536]{3,2,1,0:T(8,128)}, /*index=5*/s32[]{:T(128)}, s32[]{:T(128)}, s32[]{:T(128)}, s32[]{:T(128)}) while((s32[]{:T(128)}, f32[4,24,1536]{2,1,0:T(8,128)S(1)}, s32[]{:T(128)}, f32[8,4,1,1]{1,3,2,0:T(1,128)}, ...), condition=%wide.region_10.11_spmd, body=%wide.region_9.10_spmd.sunk | while | flops 294918 | bytes 1769667 | solution.py:22
  625.7 1.5 bitcast_dynamic-update-slice_fusion.6
  628.8 2.2 copy-done.5
  (255 shorter events, 53.4 us)
Async XLA Ops:
  35.8 30.2 %all-to-all-start = ((s32[32,1,256]{2,1,0:T(1,128)}), s32[32,1,256]{2,1,0:T(1,128)S(1)}, u32[]{:S(2)}, u32[]{:S(2)}) async-start(s32[32,1,256]{2,1,0:T(1,128)} %bitcast.10), calls=%async_computation | async-start | bytes 65536 | tf_op jit(solution)/shard_map/all_to_all | solution.py:198
  66.0 34.2 %all-to-all-start.1 = ((f32[32,32,256]{2,0,1:T(8,128)}), f32[32,32,256]{2,0,1:T(8,128)S(1)}, u32[]{:S(2)}, u32[]{:S(2)}) async-start(f32[32,32,256]{2,0,1:T(8,128)} %copy.100), calls=%async_computation.1 | async-start | bytes 2097152 | tf_op jit(solution)/shard_map/all_to_all | solution.py:197
  169.3 20.6 %copy-start.4 = (f32[8,4,768]{2,1,0:T(4,128)S(1)}, f32[8,4,768]{2,1,0:T(4,128)}, u32[]{:S(2)}) copy-start(f32[8,4,768]{2,1,0:T(4,128)} %param.15) | copy-start | bytes 294916
  169.3 20.7 %copy-start.36 = (f32[8,4]{0,1:T(4,128)S(1)}, f32[8,4]{0,1:T(4,128)}, u32[]{:S(2)}) copy-start(f32[8,4]{0,1:T(4,128)} %param.16) | copy-start | bytes 388
  169.3 127.8 %all-to-all-start.2 = ((f32[32,24,1536]{2,1,0:T(8,128)}), f32[32,24,1536]{2,1,0:T(8,128)}, u32[]{:S(2)}, u32[]{:S(2)}) async-start(f32[32,24,1536]{2,1,0:T(8,128)} %copy.104), calls=%async_computation.2 | async-start | bytes 9437184 | tf_op jit(solution)/shard_map/all_to_all | solution.py:203
  399.3 6.8 %copy-start.37 = (f32[8,4]{0,1:T(4,128)S(1)}, f32[8,4]{0,1:T(4,128)}, u32[]{:S(2)}) copy-start(f32[8,4]{0,1:T(4,128)} %param.17) | copy-start | bytes 388
  399.3 110.1 %all-to-all-start.3 = ((f32[1,768,1536]{2,0,1:T(1,128)}), f32[1,768,1536]{2,0,1:T(1,128)}, u32[]{:S(2)}, u32[]{:S(2)}) async-start(f32[1,768,1536]{2,0,1:T(1,128)} %copy.121), calls=%async_computation.3 | async-start | bytes 9437184 | tf_op jit(solution)/shard_map/all_to_all | solution.py:206
  406.0 152.4 %all-gather.4.cloned.1.call-start = ((), (), s32[]{:S(2)}) async-start(), calls=%async_computation.4 | async-start | bytes 5308416 | tf_op jit(solution)/shard_map/all_gather | solution.py:13
  406.3 0.6 copy-start.6
  406.3 0.6 copy-start.9
  406.3 0.6 copy-start.12
  406.4 0.6 copy-start.16
  406.4 0.6 copy-start.18
  406.4 0.6 copy-start.21
  509.4 6.7 %copy-start.7 = (f32[4]{0:T(128)S(1)}, f32[4]{0:T(128)}, u32[]{:S(2)}) copy-start(f32[4]{0:T(128)} %copy-done.6) | copy-start | bytes 52
  509.4 6.7 %copy-start.10 = (f32[4]{0:T(128)S(1)}, f32[4]{0:T(128)}, u32[]{:S(2)}) copy-start(f32[4]{0:T(128)} %copy-done.9) | copy-start | bytes 52
  509.4 6.7 %copy-start.13 = (f32[4]{0:T(128)S(1)}, f32[4]{0:T(128)}, u32[]{:S(2)}) copy-start(f32[4]{0:T(128)} %copy-done.12) | copy-start | bytes 52
  509.4 6.7 %copy-start.17 = (f32[4]{0:T(128)S(1)}, f32[4]{0:T(128)}, u32[]{:S(2)}) copy-start(f32[4]{0:T(128)} %copy-done.16) | copy-start | bytes 52
  509.4 6.7 %copy-start.19 = (f32[4]{0:T(128)S(1)}, f32[4]{0:T(128)}, u32[]{:S(2)}) copy-start(f32[4]{0:T(128)} %copy-done.18) | copy-start | bytes 52
  509.4 6.7 %copy-start.22 = (f32[4]{0:T(128)S(1)}, f32[4]{0:T(128)}, u32[]{:S(2)}) copy-start(f32[4]{0:T(128)} %get-tuple-element.273) | copy-start | bytes 52
  509.4 6.7 %copy-start.24 = (f32[4]{0:T(128)S(1)}, f32[4]{0:T(128)}, u32[]{:S(2)}) copy-start(f32[4]{0:T(128)} %get-tuple-element.275) | copy-start | bytes 52
  509.4 6.7 %copy-start.26 = (f32[4]{0:T(128)S(1)}, f32[4]{0:T(128)}, u32[]{:S(2)}) copy-start(f32[4]{0:T(128)} %get-tuple-element.277) | copy-start | bytes 52
  509.4 6.7 %copy-start.29 = (f32[4]{0:T(128)S(1)}, f32[4]{0:T(128)}, u32[]{:S(2)}) copy-start(f32[4]{0:T(128)} %get-tuple-element.274) | copy-start | bytes 52
  509.4 6.7 %copy-start.30 = (f32[4]{0:T(128)S(1)}, f32[4]{0:T(128)}, u32[]{:S(2)}) copy-start(f32[4]{0:T(128)} %get-tuple-element.276) | copy-start | bytes 52
  509.5 6.7 %copy-start.31 = (f32[4]{0:T(128)S(1)}, f32[4]{0:T(128)}, u32[]{:S(2)}) copy-start(f32[4]{0:T(128)} %get-tuple-element.278) | copy-start | bytes 52
  509.5 6.7 %copy-start.32 = (f32[4]{0:T(128)S(1)}, f32[4]{0:T(128)}, u32[]{:S(2)}) copy-start(f32[4]{0:T(128)} %get-tuple-element.279) | copy-start | bytes 52
  515.0 0.8 copy-start.1
  515.0 1.0 copy-start.2
  517.8 94.8 %all-gather.6.cloned.1.call-start = ((), (), s32[]{:S(2)}) async-start(), calls=%async_computation.5 | async-start | bytes 5308416 | tf_op jit(solution)/shard_map/all_gather | solution.py:13
  624.2 3.0 copy-start
  624.2 3.0 copy-start.39
  624.2 3.1 copy-start.3
  624.2 3.1 copy-start.11
  624.3 3.1 copy-start.25
  624.3 3.1 copy-start.28
  624.3 3.1 copy-start.35
  624.3 3.4 copy-start.38
  625.6 2.2 copy-start.8
  625.6 2.2 copy-start.14
  625.6 2.2 copy-start.15
  625.6 2.2 copy-start.20
  625.6 2.2 copy-start.23
  625.6 2.2 copy-start.27
  625.6 2.2 copy-start.34
  627.2 1.2 copy-start.33
  628.8 2.2 copy-start.5
Sparse Core Ops, SparseCore 0:
  517.9 40.4 all-gather.3
  565.2 47.3 all-gather.5
where the time goes:
time: 647 us; the launch traced here: 639 us
  waiting for transfers between devices  256 us (40%)
  local copies, waits for them, and re-layouts  138 us (21%)
  other arithmetic  102 us (16%)
  starting transfers between devices  48.7 us (8%)
  matrix products  41.7 us (6%)
  blocking collectives  35.6 us (6%)
  between operations  16.8 us (3%)
    all_to_all x1, waiting for transfers between devices, per_device(): lax.all_to_all(tile_field, 'sub', split_axis=0, concat_axis=1, tiled=True)  104 us
    all_to_all x1, waiting for transfers between devices, per_device(): lax.all_to_all(level_slab, 'sub', split_axis=1, concat_axis=0, tiled=True)  102 us
    scatter-add x1, other arithmetic, deposit(): flat.at[:, cells.reshape(-1)].add(obs_values.reshape(group_count, -1))  52.7 us
    all_gather x2, waiting for transfers between devices, prefix(): gathered = jax.tree.map(lambda a: lax.all_gather(a, axis), part)  44.6 us
    all_gather x2, blocking collectives, prefix(): gathered = jax.tree.map(lambda a: lax.all_gather(a, axis), part)  35.6 us
    dot_general x4, matrix products, row_sweep(): jnp.einsum('knij,knjc->knic', weights, blocked, precision=highest)  21.1 us
    all_to_all x1, starting transfers between devices, per_device(): lax.all_to_all(tile_field, 'sub', split_axis=0, concat_axis=1, tiled=True)  20.6 us
    dot_general x4, matrix products, cycle_sweep(): jnp.einsum('krnj,kij->krni', blocked, weights, precision=highest)  20.6 us
  transfers between devices with their start and end apart: 6, of which 5 were waited for; matrix products, arithmetic and copies ran while one was open for 7% of the time, Pallas kernels for 0%

commit v1 on v0

v1 whole, which is shorter than its diff:
```python
import functools

import jax
import jax.numpy as jnp
from jax import lax
from jax.experimental import pallas as pl
from jax.experimental.pallas import tpu as pltpu
from jax.sharding import PartitionSpec as P

LANE = 128
f32 = jnp.float32
bf16 = jnp.bfloat16


def vmem(mib):
    return pltpu.CompilerParams(vmem_limit_bytes=mib << 20)


def cost(flops, moved):
    return pl.CostEstimate(flops=flops, bytes_accessed=moved, transcendentals=0)


def route_slots(owners, sub_count, capacity):
    count = owners.shape[0]
    block = 128
    owner_block = owners.reshape(count // block, block)
    match = (owner_block[:, :, None] == jnp.arange(sub_count, dtype=jnp.int32)).astype(bf16)
    position = jnp.arange(block)
    lower = (position[:, None] > position[None, :]).astype(bf16)
    ahead = jnp.einsum("ij,bjo->bio", lower, match, preferred_element_type=f32)
    totals = jnp.sum(match.astype(f32), axis=1)
    base = jnp.cumsum(totals, axis=0) - totals
    rank = jnp.sum((ahead + base[:, None, :]) * match.astype(f32), axis=2)
    return owners * capacity + rank.reshape(count).astype(jnp.int32)


def pack_kernel(slots, cells, zeros, values, packed, sent_cells, rows, big, sem):
    clear = pltpu.make_async_copy(zeros, sent_cells, sem)
    clear.start()
    count = values.shape[1]
    total = big.shape[0]

    @pl.loop(0, total // 64)
    def _(i):
        big[pl.ds(pl.multiple_of(i * 64, 64), 64), :] = jnp.zeros((64, LANE), f32)

    for j in range(count // LANE):
        part = values[:, j * LANE : (j + 1) * LANE]
        rows[j * LANE : (j + 1) * LANE, :] = jnp.concatenate([part] * 4, axis=0).T
    clear.wait()

    step = 16

    @pl.loop(0, count // step)
    def _(i):
        for u in range(step):
            j = i * step + u
            slot = slots[j]
            big[pl.ds(slot, 1), :] = rows[pl.ds(j, 1), :]
            sent_cells[slot] = cells[j]

    quarter = lax.broadcasted_iota(jnp.int32, (64, LANE), 1) // 32

    @pl.loop(0, total // 256)
    def _(d):
        start = pl.multiple_of(d * 256, 256)
        out = big[pl.ds(start, 64), :]
        for k in range(1, 4):
            out = jnp.where(quarter == k, big[pl.ds(start + 64 * k, 64), :], out)
        packed[pl.ds(pl.multiple_of(d * 64, 64), 64), :] = out


def pack(slots, cells, values, total):
    count = values.shape[1]
    smem = pl.BlockSpec(memory_space=pltpu.SMEM)
    return pl.pallas_call(
        pack_kernel,
        out_shape=(
            jax.ShapeDtypeStruct((total // 4, LANE), f32),
            jax.ShapeDtypeStruct((total,), jnp.int32),
        ),
        in_specs=[smem, smem, pl.BlockSpec(memory_space=pl.ANY), pl.BlockSpec(memory_space=pltpu.VMEM)],
        out_specs=(pl.BlockSpec(memory_space=pltpu.VMEM), smem),
        scratch_shapes=[
            pltpu.VMEM((count, LANE), f32),
            pltpu.VMEM((total, LANE), f32),
            pltpu.SemaphoreType.DMA,
        ],
        compiler_params=vmem(32),
        cost_estimate=cost(0, 4 << 20),
        name="pack",
    )(slots, cells, jnp.zeros((total,), jnp.int32), values)


def deposit_kernel(places, got, field, spread, f1, f2, f3, masks):
    total = spread.shape[0]
    chains = [field, f1, f2, f3]
    depth = field.shape[0]

    @pl.loop(0, depth // 64)
    def _(i):
        at = pl.ds(pl.multiple_of(i * 64, 64), 64)
        for chain in chains:
            chain[at, :] = jnp.zeros((64, LANE), f32)

    lane_quarter = lax.broadcasted_iota(jnp.int32, (8, LANE), 1) // 32
    masks[...] = (lane_quarter == lax.broadcasted_iota(jnp.int32, (8, LANE), 0)).astype(f32)
    quarter = lax.broadcasted_iota(jnp.int32, (64, LANE), 1) // 32

    @pl.loop(0, total // 256)
    def _(d):
        part = got[pl.ds(pl.multiple_of(d * 64, 64), 64), :]
        for k in range(4):
            one = jnp.where(quarter == k, part, 0.0)
            one = one + pltpu.roll(one, 32, 1)
            one = one + pltpu.roll(one, 64, 1)
            spread[pl.ds(pl.multiple_of(d * 256 + k * 64, 64), 64), :] = one

    step = 4

    @pl.loop(0, total // (4 * step))
    def _(i):
        for u in range(step):
            loads = []
            for c in range(4):
                j = (i * step + u) * 4 + c
                place = places[j]
                row = lax.shift_right_logical(place, 2)
                mask = masks[pl.ds(place & 3, 1), :]
                loads.append((row, spread[pl.ds(j, 1), :] * mask))
            olds = [chains[c][pl.ds(loads[c][0], 1), :] for c in range(4)]
            for c in range(4):
                chains[c][pl.ds(loads[c][0], 1), :] = olds[c] + loads[c][1]

    @pl.loop(0, depth // 64)
    def _(i):
        at = pl.ds(pl.multiple_of(i * 64, 64), 64)
        field[at, :] = (field[at, :] + f1[at, :]) + (f2[at, :] + f3[at, :])


def deposit(places, got, depth):
    total = places.shape[0]
    return pl.pallas_call(
        deposit_kernel,
        out_shape=jax.ShapeDtypeStruct((depth, LANE), f32),
        in_specs=[pl.BlockSpec(memory_space=pltpu.SMEM), pl.BlockSpec(memory_space=pltpu.VMEM)],
        out_specs=pl.BlockSpec(memory_space=pltpu.VMEM),
        scratch_shapes=[pltpu.VMEM((total, LANE), f32)]
        + [pltpu.VMEM((depth, LANE), f32)] * 3
        + [pltpu.VMEM((8, LANE), f32)],
        compiler_params=vmem(40),
        cost_estimate=cost(0, 16 << 20),
        name="deposit",
    )(places, got)


def lat_sweeps(rows, decay, starts):
    count = len(rows)
    ends = []
    for sweep in range(4):
        order = range(count) if sweep % 2 == 0 else range(count - 1, -1, -1)
        state = starts[sweep]
        out = [None] * count
        for r in order:
            state = rows[r] + decay(r) * (state - rows[r])
            out[r] = state
        ends.append(state)
        rows = out
    return rows, ends


def lat_moments_kernel(row_count, groups, field, background, decay, forced, moments):
    ct = pl.program_id(0)
    tiles = background.shape[1] // LANE
    for rr in range(row_count // 4):
        turned = field[rr].T
        for q in range(4):
            for o in range(groups // 8):
                at = pl.ds(o * 8 * row_count + rr * 4 + q, 8, stride=row_count)
                first = q * groups + o * 8
                forced[at, :] = background[at, :] + turned[first : first + 8, :]
    zero = jnp.zeros((8, LANE), f32)
    for o in range(groups // 8):
        rows = [
            forced[pl.ds(o * 8 * row_count + r, 8, stride=row_count), :] for r in range(row_count)
        ]
        _, ends = lat_sweeps(
            rows, lambda r: decay[r * groups + o * 8 : r * groups + o * 8 + 8, :], [zero] * 4
        )
        per_group = moments.shape[0] // groups
        for k in range(4):
            start = o * 8 * per_group + k * (per_group // 4) + ct
            moments[pl.ds(start, 8, stride=per_group), :] = ends[k]


def lat_moments(field, background, decay, row_count, groups):
    rows, columns = background.shape
    tiles = columns // LANE
    block = pl.BlockSpec((rows, LANE), lambda i: (0, i))
    whole = pl.BlockSpec((rows, LANE), lambda i: (0, 0))
    return pl.pallas_call(
        functools.partial(lat_moments_kernel, row_count, groups),
        grid=(tiles,),
        out_shape=(
            jax.ShapeDtypeStruct(background.shape, f32),
            jax.ShapeDtypeStruct((groups * 4 * tiles, LANE), f32),
        ),
        in_specs=[pl.BlockSpec((row_count // 4, LANE, LANE), lambda i: (0, i, 0)), block, whole],
        out_specs=(block, pl.BlockSpec((groups * 4 * tiles, LANE), lambda i: (0, 0))),
        compiler_params=vmem(32),
        cost_estimate=cost(0, 16 << 20),
        name="lat_moments",
    )(field.reshape(row_count // 4, columns, LANE), background, decay)


def lon_weights(length, columns):
    blocks = columns // LANE
    length = length[:, None, None]
    kappa = jnp.tanh(0.5 / length)
    beta = kappa * kappa
    alpha = beta / jnp.tanh(1.0 / length)
    i = jnp.arange(LANE, dtype=f32)

    def power(n):
        return jnp.exp(-n / length)

    gap = jnp.abs(i[:, None] - i[None, :])[None]
    local = (alpha + beta * gap) * power(gap)
    up, down = i[None, :, None], (LANE - 1.0) - i[None, :, None]
    sums = jnp.concatenate(
        [power(down), down * power(down), power(up), up * power(up)], axis=2
    )
    sums = jnp.pad(sums, ((0, 0), (0, 0), (0, LANE - 4)))
    first = jnp.concatenate([local, sums], axis=2)
    index = jnp.arange(LANE)
    src, dst = index[:, None], index[None, :]
    source, target = src // 4, dst // 4
    backward = (src % 4) >= 2
    steps = jnp.where(backward, source - target - 1, target - source - 1) % blocks
    gap = (LANE * steps).astype(f32)[None]
    turn = power(float(columns))
    left = -jnp.expm1(-float(columns) / length)
    same = power(gap) / left
    cross = (gap + columns * turn / left) * same
    used = (source < blocks) & (target < blocks)
    mix = jnp.where((used & (src % 4 == dst % 4))[None], same, 0.0)
    mix = jnp.where((used & (src % 2 == 0) & (dst % 4 == src % 4 + 1))[None], cross, mix)
    near, far = i[None, None, :] + 1.0, LANE - i[None, None, :]
    back = jnp.concatenate(
        [
            (alpha + beta * near) * power(near),
            beta * power(near),
            (alpha + beta * far) * power(far),
            beta * power(far),
        ],
        axis=1,
    )
    back = jnp.pad(back, ((0, 0), (0, LANE - 4), (0, 0)))
    return first, mix, back


def split(x):
    high = x.astype(bf16)
    return high, (x - high.astype(f32)).astype(bf16)


def dot3(x, w):
    xh, xl = split(x)
    wh, wl = split(w)

    def dot(a, b):
        return jnp.dot(a, b, preferred_element_type=f32)

    return dot(xh, wh) + (dot(xh, wl) + dot(xl, wh))


def lon_apply(x, first, mix, back):
    count, columns = x.shape
    blocks = columns // LANE
    stacked = jnp.concatenate([x[:, b * LANE : (b + 1) * LANE] for b in range(blocks)], axis=0)
    both = dot3(stacked, first)
    local, sums = both[:, :LANE], both[:, LANE:]
    line = sums[:count]
    for b in range(1, blocks):
        line = line + pltpu.roll(sums[b * count : (b + 1) * count], 4 * b, 1)
    states = dot3(line, mix)
    spread = jnp.concatenate(
        [states] + [pltpu.roll(states, LANE - 4 * b, 1) for b in range(1, blocks)], axis=0
    )
    out = local + dot3(spread, back)
    return jnp.concatenate([out[b * count : (b + 1) * count] for b in range(blocks)], axis=1)


def lon_kernel(x, first, mix, back, out):
    out[...] = lon_apply(x[...], first[0], mix[0], back[0])


def lon_filter(x, weights, row_count):
    rows, columns = x.shape
    block = pl.BlockSpec((row_count, columns), lambda i: (i, 0))
    return pl.pallas_call(
        lon_kernel,
        grid=(rows // row_count,),
        out_shape=jax.ShapeDtypeStruct(x.shape, f32),
        in_specs=[
            block,
            pl.BlockSpec((1, LANE, 2 * LANE), lambda i: (i, 0, 0)),
            pl.BlockSpec((1, LANE, LANE), lambda i: (i, 0, 0)),
            pl.BlockSpec((1, LANE, LANE), lambda i: (i, 0, 0)),
        ],
        out_specs=block,
        compiler_params=vmem(32),
        cost_estimate=cost(6 * rows * columns * 3 * LANE, 60 << 20),
        name="lon",
    )(x, *weights)


def hub_kernel(decay, moments, first, mix, back, states, work):
    blocks = 32
    depth = moments.shape[0] // blocks
    tiles = depth // 4
    count = decay.shape[0]
    coef = [decay[r : r + 1, :] for r in range(count)]

    def forward(rows):
        state, out = jnp.zeros((1, LANE), f32), []
        for r in range(count):
            state = rows[r] + coef[r] * (state - rows[r])
            out.append(state)
        return out

    def backward(rows):
        state, out = jnp.zeros((1, LANE), f32), [None] * count
        for r in range(count - 1, -1, -1):
            state = rows[r] + coef[r] * (state - rows[r])
            out[r] = state
        return out

    state, down = jnp.ones((1, LANE), f32), []
    for r in range(count):
        state = coef[r] * state
        down.append(state)
    full = state
    state, up = jnp.ones((1, LANE), f32), [None] * count
    for r in range(count - 1, -1, -1):
        state = coef[r] * state
        up[r] = state
    bp = backward(down)
    fbp = forward(bp)
    bfbp = backward(fbp)
    fq = forward(up)
    bfq = backward(fq)
    t21, t31, t41, t32, t42 = bp[0], fbp[-1], bfbp[0], fq[-1], bfq[0]

    def at(table, d):
        return jnp.broadcast_to(table[:, d : d + 1], (tiles, LANE))

    def moment(d, k):
        return moments[d * depth + k * tiles : d * depth + (k + 1) * tiles, :]

    def put(d, k, value):
        for t in range(tiles):
            work[k * blocks + d, t * LANE : (t + 1) * LANE] = value[t]

    zero = jnp.zeros((tiles, LANE), f32)
    s = [[None] * blocks for _ in range(4)]
    carry = zero
    for d in range(blocks):
        s[0][d] = carry
        carry = at(full, d) * carry + moment(d, 0)
    carry = zero
    for d in range(blocks - 1, -1, -1):
        s[1][d] = carry
        carry = at(full, d) * carry + (moment(d, 1) + at(t21, d) * s[0][d])
    carry = zero
    for d in range(blocks):
        s[2][d] = carry
        carry = at(full, d) * carry + (
            moment(d, 2) + at(t31, d) * s[0][d] + at(t32, d) * s[1][d]
        )
    carry = zero
    for d in range(blocks - 1, -1, -1):
        s[3][d] = carry
        carry = at(full, d) * carry + (
            moment(d, 3) + at(t41, d) * s[0][d] + at(t42, d) * s[1][d] + at(t21, d) * s[2][d]
        )
    for k in range(4):
        for d in range(blocks):
            put(d, k, s[k][d])
    done = lon_apply(work[...], first[0], mix[0], back[0])
    for k in range(4):
        for d in range(blocks):
            row = done[k * blocks + d : k * blocks + d + 1]
            for t in range(tiles):
                base = d * depth + k * tiles + t
                states[base : base + 1, :] = row[:, t * LANE : (t + 1) * LANE]


def hub(decay, moments, weights):
    depth = moments.shape[0] // 32
    return pl.pallas_call(
        hub_kernel,
        out_shape=jax.ShapeDtypeStruct(moments.shape, f32),
        in_specs=[pl.BlockSpec(memory_space=pltpu.VMEM)] * 5,
        out_specs=pl.BlockSpec(memory_space=pltpu.VMEM),
        scratch_shapes=[pltpu.VMEM((128, depth // 4 * LANE), f32)],
        compiler_params=vmem(32),
        cost_estimate=cost(0, 4 << 20),
        name="hub",
    )(decay, moments, *weights)


def level_sweeps(rows, decay, starts):
    count = len(rows)
    ends = []
    for sweep in range(2):
        order = range(count) if sweep == 0 else range(count - 1, -1, -1)
        state = starts[sweep]
        out = [None] * count
        for r in order:
            state = rows[r] + decay(r) * (state - rows[r])
            out[r] = state
        ends.append(state)
        rows = out
    return rows, ends


def lat_states_kernel(row_count, groups, variables, x, decay, states, vert, out, sums):
    ct = pl.program_id(0)
    per_group = states.shape[0] // groups
    for o in range(groups // 8):
        rows = [x[pl.ds(o * 8 * row_count + r, 8, stride=row_count), :] for r in range(row_count)]
        starts = [
            states[pl.ds(o * 8 * per_group + k * (per_group // 4) + ct, 8, stride=per_group), :]
            for k in range(4)
        ]
        rows, _ = lat_sweeps(
            rows, lambda r: decay[r * groups + o * 8 : r * groups + o * 8 + 8, :], starts
        )
        for r in range(row_count):
            out[pl.ds(o * 8 * row_count + r, 8, stride=row_count), :] = rows[r]
    zero = jnp.zeros((8, LANE), f32)
    levels = groups // variables
    for var in range(variables):
        for t in range(row_count // 8):
            rows = []
            for lev in range(levels):
                base = (lev * variables + var) * row_count + t * 8
                rows.append(out[base : base + 8, :])
            _, ends = level_sweeps(rows, lambda lev: vert[lev * variables + var], [zero, zero])
            for k in range(2):
                sums[var, 0, k, 0, t * 8 : t * 8 + 8, :] = ends[k]


def lat_states(x, decay, states, vert, row_count, groups, variables):
    rows, columns = x.shape
    tiles = columns // LANE
    half = tiles // 2
    block = pl.BlockSpec((rows, LANE), lambda i: (0, i))
    return pl.pallas_call(
        functools.partial(lat_states_kernel, row_count, groups, variables),
        grid=(tiles,),
        out_shape=(
            jax.ShapeDtypeStruct(x.shape, f32),
            jax.ShapeDtypeStruct((variables, 2, 2, half, row_count, LANE), f32),
        ),
        in_specs=[
            block,
            pl.BlockSpec((rows, LANE), lambda i: (0, 0)),
            pl.BlockSpec(states.shape, lambda i: (0, 0)),
            pl.BlockSpec(memory_space=pltpu.SMEM),
        ],
        out_specs=(
            block,
            pl.BlockSpec(
                (variables, 1, 2, 1, row_count, LANE),
                lambda i: (0, i // half, 0, i % half, 0, 0),
            ),
        ),
        compiler_params=vmem(32),
        cost_estimate=cost(0, 12 << 20),
        name="lat_states",
    )(x, decay, states, vert)


def level_hub_kernel(coef, sums, states):
    bands = sums.shape[0]
    depth = sums.shape[2]
    for t in range(depth // 8):
        at = slice(t * 8, t * 8 + 8)
        state = jnp.zeros((8, LANE), f32)
        entering = []
        for b in range(bands):
            entering.append(state)
            states[b, 0, at, :] = state
            state = coef[0, b] * state + sums[b, 0, at, :]
        state = jnp.zeros((8, LANE), f32)
        for b in range(bands - 1, -1, -1):
            states[b, 1, at, :] = state
            state = coef[0, b] * state + (sums[b, 1, at, :] + coef[1, b] * entering[b])


def level_hub(coef, sums):
    return pl.pallas_call(
        level_hub_kernel,
        out_shape=jax.ShapeDtypeStruct(sums.shape, f32),
        in_specs=[pl.BlockSpec(memory_space=pltpu.SMEM), pl.BlockSpec(memory_space=pltpu.VMEM)],
        out_specs=pl.BlockSpec(memory_space=pltpu.VMEM),
        compiler_params=vmem(16),
        cost_estimate=cost(0, 3 << 20),
        name="level_hub",
    )(coef, sums)


def level_states_kernel(row_count, groups, variables, x, vert, states, out):
    levels = groups // variables
    for var in range(variables):
        for t in range(row_count // 8):
            spots = [
                slice((lev * variables + var) * row_count + t * 8, (lev * variables + var) * row_count + t * 8 + 8)
                for lev in range(levels)
            ]
            rows = [x[spot, :] for spot in spots]
            starts = [states[var, 0, k, 0, t * 8 : t * 8 + 8, :] for k in range(2)]
            rows, _ = level_sweeps(rows, lambda lev: vert[lev * variables + var], starts)
            for lev in range(levels):
                out[spots[lev], :] = rows[lev]


def level_states(x, vert, states, row_count, groups, variables):
    rows, columns = x.shape
    tiles = columns // LANE
    half = tiles // 2
    block = pl.BlockSpec((rows, LANE), lambda i: (0, i))
    return pl.pallas_call(
        functools.partial(level_states_kernel, row_count, groups, variables),
        grid=(tiles,),
        out_shape=jax.ShapeDtypeStruct(x.shape, f32),
        in_specs=[
            block,
            pl.BlockSpec(memory_space=pltpu.SMEM),
            pl.BlockSpec(
                (variables, 1, 2, 1, row_count, LANE),
                lambda i: (0, i // half, 0, i % half, 0, 0),
            ),
        ],
        out_specs=block,
        compiler_params=vmem(32),
        cost_estimate=cost(0, 11 << 20),
        name="level_states",
    )(x, vert, states)


def level_coefficients(decays):
    levels = decays.shape[1]
    state, down = jnp.ones_like(decays[:, 0]), []
    for r in range(levels):
        state = decays[:, r] * state
        down.append(state)
    full = state
    state = jnp.zeros_like(full)
    for r in range(levels - 1, -1, -1):
        state = down[r] + decays[:, r] * (state - down[r])
    return jnp.stack([full, state])


def per_device(background, obs_columns, obs_owner, obs_cell, lat_length, lon_length, vert_length):
    level_count, var_count, row_count, lon_count = background.shape
    sub_count = lax.axis_size("sub")
    band_count = lax.axis_size("band")
    sub_index = lax.axis_index("sub")
    band_index = lax.axis_index("band")
    groups = level_count * var_count
    tiles = lon_count // LANE
    tile_field = background.reshape(groups * row_count, lon_count)
    obs_values = obs_columns.reshape(groups, -1)
    owners = obs_owner[:, 0]
    capacity = 2 * owners.shape[0] // sub_count

    slots = route_slots(owners, sub_count, capacity)
    row, column = obs_cell // lon_count, obs_cell % lon_count
    place = ((row // 4) * lon_count + column) * 4 + row % 4
    packed, sent = pack(slots, place, obs_values, sub_count * capacity)
    got = lax.all_to_all(
        packed.reshape(sub_count, capacity // 4, LANE), "sub", 0, 0, tiled=True
    )
    places = lax.all_to_all(sent.reshape(sub_count, capacity), "sub", 0, 0, tiled=True)

    all_vert = lax.all_gather(vert_length, "band")
    vert_decay = jnp.exp(-1.0 / vert_length).reshape(groups)
    own_var = band_index // 2
    hub_vert = lax.dynamic_index_in_dim(jnp.exp(-1.0 / all_vert), own_var, 2, False)
    coef = level_coefficients(hub_vert)

    lat_all = jnp.exp(-1.0 / lat_length).reshape(groups, sub_count, row_count)
    own_lat = lax.dynamic_index_in_dim(lat_all, sub_index, 1, False)
    decay = jnp.broadcast_to(own_lat.T.reshape(row_count * groups, 1), (row_count * groups, LANE))
    hub_lat = lax.dynamic_index_in_dim(lat_all, sub_index, 0, False)
    hub_lat = jnp.pad(hub_lat.T, ((0, 0), (0, LANE - sub_count)))

    lengths = lon_length.reshape(groups)
    weights = lon_weights(lengths, lon_count)
    own_weights = [lax.dynamic_slice_in_dim(w, sub_index, 1, 0) for w in weights]

    field = deposit(places.reshape(-1), got.reshape(-1, LANE), groups * row_count * lon_count // LANE)
    forced, moments = lat_moments(field, tile_field, decay, row_count, groups)
    moments = lax.all_to_all(
        moments.reshape(sub_count, 4 * tiles, LANE), "sub", 0, 0, tiled=True
    )
    smooth = lon_filter(forced, weights, row_count)
    states = hub(hub_lat, moments.reshape(-1, LANE), own_weights)
    states = lax.all_to_all(states.reshape(sub_count, 4 * tiles, LANE), "sub", 0, 0, tiled=True)
    smooth, sums = lat_states(
        smooth, decay, states.reshape(-1, LANE), vert_decay, row_count, groups, var_count
    )
    depth = tiles // 2 * row_count
    sums = lax.all_to_all(
        sums.reshape(band_count, 2, depth, LANE), "band", 0, 0, tiled=True
    )
    entering = level_hub(coef, sums)
    entering = lax.all_to_all(entering, "band", 0, 0, tiled=True)
    result = level_states(
        smooth,
        vert_decay,
        entering.reshape(var_count, 2, 2, tiles // 2, row_count, LANE),
        row_count,
        groups,
        var_count,
    )
    return result.reshape(background.shape)


def solution(mesh):
    placed = (
        P("band", None, "sub", None),
        P("band", None, "sub"),
        P("sub", None),
        P("sub"),
        P("band", None, None),
        P("band", None),
        P("band", None),
    )
    return jax.shard_map(
        per_device,
        mesh=mesh,
        in_specs=placed,
        out_specs=P("band", None, "sub", None),
        check_vma=False,
    )
```

time: 647 us -> 249 us (0.38); the launches traced: 639 us -> 248 us
  waiting for transfers between devices: 256 us -> 39.2 us
  local copies, waits for them, and re-layouts: 138 us -> 28.3 us
  other arithmetic: 102 us -> 8.86 us
  Pallas kernels: 0 us -> 89.4 us
  matrix products: 41.7 us -> 1.07 us
  between operations: 16.8 us -> 0.47 us
  starting transfers between devices: 48.7 us -> 39.2 us
    all_to_all x4 -> x5, waiting for transfers between devices: 212 us -> 39.2 us  [the longest x1 19.6 us: per_device(): lax.all_to_all(packed.reshape(sub_count, capacity // 4, LANE), 'sub', 0,...]
    pallas_call x0 -> x8, Pallas kernels: none -> 89.4 us  [the longest x1 27.5 us: lon_filter(): pl.pallas_call(lon_kernel, grid=(rows // row_count,), out_shape=jax.Shape...]
    scatter-add x1 -> x0, other arithmetic: 52.7 us -> none  [deposit(): flat.at[:, cells.reshape(-1)].add(obs_values.reshape(group_count, -1))]
    all_gather x2 -> x0, waiting for transfers between devices: 44.6 us -> none  [prefix(): gathered = jax.tree.map(lambda a: lax.all_gather(a, axis), part)]
    dot_general x8 -> x1, matrix products: 41.7 us -> 1.07 us  [route_slots(): ahead = jnp.einsum('ij,bjo->bio', lower, match, preferred_element_type=f32)]
    reshape x9 -> x3, local copies, waits for them, and re-layouts: 34.2 us -> 1.67 us  [the longest x1 1.22 us: per_device(): obs_values = obs_columns.reshape(groups, -1)]
    scatter x2 -> x0, local copies, waits for them, and re-layouts: 29.1 us -> none  [the longest x1 16.3 us: fill_slots(): jnp.zeros((sub_count * capacity,), jnp.int32).at[slots].set(obs_cell)]
    all_to_all x0 -> x1, blocking collectives: none -> 20.2 us  [per_device(): entering = lax.all_to_all(entering, 'band', 0, 0, tiled=True)]
  transfers between devices with their start and end apart: 6 -> 5, of which waited for: 5 -> 3; matrix products, arithmetic and copies ran while one was open for 7% -> 4% of each run, Pallas kernels for 0% -> 11%
where the time goes in v1:
time: 249 us; the launch traced here: 248 us
  Pallas kernels  89.4 us (36%)
  blocking collectives  42 us (17%)
  starting transfers between devices  39.2 us (16%)
  waiting for transfers between devices  39.2 us (16%)
  local copies, waits for them, and re-layouts  28.3 us (11%)
  other arithmetic  8.86 us (4%)
    pallas_call x1, Pallas kernels, lon_filter(): pl.pallas_call(lon_kernel, grid=(rows // row_count,), out_shape=jax.Shape...  27.5 us
    pallas_call x1, Pallas kernels, deposit(): pl.pallas_call(deposit_kernel, out_shape=jax.ShapeDtypeStruct((depth, LAN...  26.2 us
    unnamed x45, local copies, waits for them, and re-layouts  23.6 us
    all_gather x1, blocking collectives, per_device(): all_vert = lax.all_gather(vert_length, 'band')  21.8 us
    all_to_all x1, blocking collectives, per_device(): entering = lax.all_to_all(entering, 'band', 0, 0, tiled=True)  20.2 us
    all_to_all x1, waiting for transfers between devices, per_device(): lax.all_to_all(packed.reshape(sub_count, capacity // 4, LANE), 'sub', 0,...  19.6 us
    all_to_all x1, starting transfers between devices, per_device(): lax.all_to_all(sent.reshape(sub_count, capacity), 'sub', 0, 0, tiled=True)  11.9 us
    all_to_all x1, waiting for transfers between devices, per_device(): lax.all_to_all(moments.reshape(sub_count, 4 * tiles, LANE), 'sub', 0, 0,...  11.6 us
  transfers between devices with their start and end apart: 5, of which 3 were waited for; matrix products, arithmetic and copies ran while one was open for 4% of the time, Pallas kernels for 11%

profile of v1, /device:TPU:1, one launch (start us, length us, event | category | flops | bytes accessed | tf_op | source)
XLA Modules:
  0.0 248.4 jit_solution(17618005358346399998)
XLA Ops:
  0.0 0.8 broadcast_multiply_fusion.1
  0.8 0.9 convert_reduce_fusion
  1.8 1.1 fusion.4
  2.8 1.2 reshape.1411.values
  4.1 0.8 fusion.20
  4.8 11.0 %pack.1 = (f32[2048,128]{1,0:T(8,128)}, s32[8192]{0:T(1024)}) custom-call(s32[4096]{0:T(1024)S(1)} %get-tuple-element.52.slots, s32[4096]{0:T(1024)S(1)} %get-tuple-element.51.cells, s32[8192]{0:T(1024)S(1)} %broadcast_in_dim.33.zeros, f32[32,4096]{1,0:T(8,128)S(1)} %reshape.1411.values), custom_call_target="tpu_custom_call" | custom-call | bytes 4194304 | tf_op jit(solution)/shard_map/pack/pallas_call | solution.py:76
  15.9 11.9 %all-to-all-start = ((s32[32,1,256]{2,1,0:T(1,128)}), s32[32,1,256]{2,1,0:T(1,128)S(1)}, u32[]{:S(2)}, u32[]{:S(2)}) async-start(s32[32,1,256]{2,1,0:T(1,128)} %bitcast.5), calls=%async_computation | async-start | bytes 65536 | tf_op jit(solution)/shard_map/all_to_all | solution.py:587
  28.0 0.4 reshape.1417
  28.6 8.0 %all-to-all-done = s32[32,1,256]{2,1,0:T(1,128)S(1)} async-done(((s32[32,1,256]{2,1,0:T(1,128)}), s32[32,1,256]{2,1,0:T(1,128)S(1)}, u32[]{:S(2)}, u32[]{:S(2)}) %all-to-all-start) | async-done | bytes 32800 | tf_op jit(solution)/shard_map/all_to_all | solution.py:587
  36.5 3.9 %all-to-all-start.1 = ((f32[32,64,128]{2,1,0:T(8,128)}), f32[32,64,128]{2,1,0:T(8,128)S(1)}, u32[]{:S(2)}, u32[]{:S(2)}) async-start(f32[32,64,128]{2,1,0:T(8,128)} %bitcast.7), calls=%async_computation.1 | async-start | bytes 2097152 | tf_op jit(solution)/shard_map/all_to_all | solution.py:584
  40.7 2.0 copy.26
  42.8 0.6 multiply_divide_fusion
  43.5 0.2 add_multiply_fusion.1
  43.6 0.3 select_maximum_fusion.1.back
  43.9 0.5 exponential-minus-one_negate_fusion
  44.4 0.7 fusion.14
  45.3 19.6 %all-to-all-done.1 = f32[32,64,128]{2,1,0:T(8,128)S(1)} async-done(((f32[32,64,128]{2,1,0:T(8,128)}), f32[32,64,128]{2,1,0:T(8,128)S(1)}, u32[]{:S(2)}, u32[]{:S(2)}) %all-to-all-start.1) | async-done | bytes 1048608 | tf_op jit(solution)/shard_map/all_to_all | solution.py:584
  64.9 26.2 %deposit.1 = f32[9216,128]{1,0:T(8,128)S(1)} custom-call(s32[8192]{0:T(1024)S(1)} %bitcast.162, f32[2048,128]{1,0:T(8,128)S(1)} %bitcast.156), custom_call_target="tpu_custom_call" | custom-call | bytes 16777216 | tf_op jit(solution)/shard_map/deposit/pallas_call | solution.py:143
  91.1 0.2 broadcast_in_dim.38.decay
  91.3 2.3 copy-done.6
  93.6 7.4 %lat_moments.1 = (f32[768,1536]{1,0:T(8,128)S(1)}, f32[1536,128]{1,0:T(8,128)S(1)}) custom-call(f32[6,1536,128]{2,1,0:T(8,128)S(1)} %bitcast.153, f32[768,1536]{1,0:T(8,128)S(1)} %bitcast.154, f32[768,128]{1,0:T(8,128)S(1)} %broadcast_in_dim.38.decay), custom_call_target="tpu_custom_call" | custom-call | bytes 16777216 | tf_op jit(solution)/shard_map/lat_moments/pallas_call | solution.py:201
  101.1 2.2 copy-done.9
  103.3 0.9 copy-done.13
  104.2 8.5 %all-to-all-start.2 = ((f32[32,48,128]{2,1,0:T(8,128)}), f32[32,48,128]{2,1,0:T(8,128)S(1)}, u32[]{:S(2)}, u32[]{:S(2)}) async-start(f32[32,48,128]{2,1,0:T(8,128)} %bitcast.161), calls=%async_computation.2 | async-start | bytes 1572864 | tf_op jit(solution)/shard_map/all_to_all | solution.py:607
  112.8 0.9 fusion.16
  113.6 2.3 select_select_fusion
  116.0 1.3 copy-done.4
  117.3 0.4 select_maximum_fusion.first
  117.8 2.0 copy-done.2
  119.8 11.6 %all-to-all-done.2 = f32[32,48,128]{2,1,0:T(8,128)S(1)} async-done(((f32[32,48,128]{2,1,0:T(8,128)}), f32[32,48,128]{2,1,0:T(8,128)S(1)}, u32[]{:S(2)}, u32[]{:S(2)}) %all-to-all-start.2) | async-done | bytes 786464 | tf_op jit(solution)/shard_map/all_to_all | solution.py:607
  131.4 2.9 %hub.1 = f32[1536,128]{1,0:T(8,128)S(1)} custom-call(f32[24,128]{1,0:T(8,128)S(1)} %pad.14.decay, f32[1536,128]{1,0:T(8,128)S(1)} %bitcast.157, f32[1,128,256]{2,1,0:T(8,128)S(1)} %constant_dynamic-slice_fusion.3.first, f32[1,128,128]{2,1,0:T(8,128)S(1)} %constant_dynamic-slice_fusion.2.mix, f32[1,128,128]{2,1,0:T(8,128)S(1)} %constant_dynamic-slice_fusion.1.back), custom_call_target="tpu_custom_call" | custom-call | bytes 4194304 | tf_op jit(solution)/shard_map/hub/pallas_call | solution.py:401
  134.3 0.9 copy-done.11
  135.2 7.9 %all-to-all-start.3 = ((f32[32,48,128]{2,1,0:T(8,128)}), f32[32,48,128]{2,1,0:T(8,128)S(1)}, u32[]{:S(2)}, u32[]{:S(2)}) async-start(f32[32,48,128]{2,1,0:T(8,128)} %bitcast.159), calls=%async_computation.3 | async-start | bytes 1572864 | tf_op jit(solution)/shard_map/all_to_all | solution.py:612
  143.3 2.2 copy-done.3
  145.5 1.6 copy-done.5
  147.1 2.3 copy-done.10
  149.5 27.5 %lon.1.x = f32[768,1536]{1,0:T(8,128)S(1)} custom-call(f32[768,1536]{1,0:T(8,128)S(1)} %copy-done.10, f32[32,128,256]{2,1,0:T(8,128)S(1)} %copy-done.3, f32[32,128,128]{2,1,0:T(8,128)S(1)} %copy-done.5, f32[32,128,128]{2,1,0:T(8,128)S(1)} %select_maximum_fusion.1.back), custom_call_target="tpu_custom_call" | custom-call | flops 2717908992 | bytes 62914560 | tf_op jit(solution)/shard_map/lon/pallas_call | solution.py:301
  177.0 2.2 copy-done
  179.2 2.3 copy-done.1
  181.5 7.4 %lat_states.1 = (f32[768,1536]{1,0:T(8,128)S(1)}, f32[4,2,2,6,24,128]{5,4,3,2,1,0:T(8,128)S(1)}) custom-call(f32[768,1536]{1,0:T(8,128)S(1)} %copy-done.1, f32[768,128]{1,0:T(8,128)S(1)} %broadcast_in_dim.38.decay, f32[1536,128]{1,0:T(8,128)S(1)} %bitcast.158, f32[32]{0:T(128)S(1)} %reshape.1422.vert), custom_call_target="tpu_custom_call" | custom-call | bytes 12582912 | tf_op jit(solution)/shard_map/lat_states/pallas_call | solution.py:460
  189.0 2.2 copy-done.7
  191.1 1.0 copy-done.12
  192.2 7.0 %all-to-all-start.4 = ((f32[8,2,144,128]{3,2,1,0:T(8,128)}), f32[8,2,144,128]{3,2,1,0:T(8,128)S(1)}, u32[]{:S(2)}, u32[]{:S(2)}) async-start(f32[8,2,144,128]{3,2,1,0:T(8,128)} %bitcast.160), calls=%async_computation.4 | async-start | bytes 2359296 | tf_op jit(solution)/shard_map/all_to_all | solution.py:617
  199.1 21.8 %all-gather.1 = f32[8,8,4]{1,2,0:T(4,128)S(1)} all-gather(f32[1,8,4]{1,2,0:T(4,128)S(1)} %bitcast.169), channel_id=2, replica_groups=mesh['band'=8,'sub'=32] {'band'}, dimensions={0}, use_global_device_ids=true | all-gather | bytes 1152 | tf_op jit(solution)/shard_map/all_gather | solution.py:589
  220.9 0.3 slice_reduce_fusion.7
  221.3 0.7 level_hub.1
  222.0 20.2 %all_to_all.34 = f32[8,2,144,128]{3,2,1,0:T(8,128)S(1)} all-to-all(f32[8,2,144,128]{3,2,1,0:T(8,128)S(1)} %level_hub.1), channel_id=1, replica_groups=mesh['band'=8,'sub'=32] {'band'}, dimensions={0} | all-to-all | bytes 2359296 | tf_op jit(solution)/shard_map/all_to_all | solution.py:621
  242.2 6.3 %level_states.1 = f32[768,1536]{1,0:T(8,128)} custom-call(f32[768,1536]{1,0:T(8,128)S(1)} %copy-done.8, f32[32]{0:T(128)S(1)} %reshape.1422.vert, f32[4,2,2,6,24,128]{5,4,3,2,1,0:T(8,128)S(1)} %bitcast.155), custom_call_target="tpu_custom_call" | custom-call | bytes 11534336 | tf_op jit(solution)/shard_map/level_states/pallas_call | solution.py:535
  (68 shorter events, 1.3 us)
Async XLA Ops:
  0.0 27.8 %copy-start.21 = (f32[8,4]{0,1:T(4,128)S(1)}, f32[8,4]{0,1:T(4,128)}, u32[]{:S(2)}) copy-start(f32[8,4]{0,1:T(4,128)} %param.12) | copy-start | bytes 388
  0.0 28.0 %copy-start.15 = (f32[8,4,768]{2,1,0:T(4,128)S(1)}, f32[8,4,768]{2,1,0:T(4,128)}, u32[]{:S(2)}) copy-start(f32[8,4,768]{2,1,0:T(4,128)} %param.11) | copy-start | bytes 294916
  15.9 20.6 %all-to-all-start = ((s32[32,1,256]{2,1,0:T(1,128)}), s32[32,1,256]{2,1,0:T(1,128)S(1)}, u32[]{:S(2)}, u32[]{:S(2)}) async-start(s32[32,1,256]{2,1,0:T(1,128)} %bitcast.5), calls=%async_computation | async-start | bytes 65536 | tf_op jit(solution)/shard_map/all_to_all | solution.py:587
  36.5 28.4 %all-to-all-start.1 = ((f32[32,64,128]{2,1,0:T(8,128)}), f32[32,64,128]{2,1,0:T(8,128)S(1)}, u32[]{:S(2)}, u32[]{:S(2)}) async-start(f32[32,64,128]{2,1,0:T(8,128)} %bitcast.7), calls=%async_computation.1 | async-start | bytes 2097152 | tf_op jit(solution)/shard_map/all_to_all | solution.py:584
  40.5 4.7 %copy-start.20 = (pred[128]{0:T(512)(128)(4,1)}, pred[128]{0:T(512)(128)(4,1)S(1)}, u32[]{:S(2)}) copy-start(pred[128]{0:T(512)(128)(4,1)S(1)} %broadcast_compare_fusion.1) | copy-start | bytes 388
  42.7 48.4 %copy-start.16 = (s32[128]{0:T(128)}, s32[128]{0:T(128)S(1)}, u32[]{:S(2)}) copy-start(s32[128]{0:T(128)S(1)} %get-tuple-element.48) | copy-start | bytes 1540
  43.4 47.7 %copy-start.18 = (f32[32]{0:T(128)}, f32[32]{0:T(128)S(1)}, u32[]{:S(2)}) copy-start(f32[32]{0:T(128)S(1)} %get-tuple-element.44) | copy-start | bytes 388
  43.4 47.7 %copy-start.19 = (f32[32]{0:T(128)}, f32[32]{0:T(128)S(1)}, u32[]{:S(2)}) copy-start(f32[32]{0:T(128)S(1)} %get-tuple-element.43) | copy-start | bytes 388
  91.3 2.3 copy-start.6
  101.1 2.2 copy-start.9
  103.3 0.9 copy-start.13
  104.2 27.2 %all-to-all-start.2 = ((f32[32,48,128]{2,1,0:T(8,128)}), f32[32,48,128]{2,1,0:T(8,128)S(1)}, u32[]{:S(2)}, u32[]{:S(2)}) async-start(f32[32,48,128]{2,1,0:T(8,128)} %bitcast.161), calls=%async_computation.2 | async-start | bytes 1572864 | tf_op jit(solution)/shard_map/all_to_all | solution.py:607
  113.6 3.7 %copy-start.14 = (f32[32,128,4]{2,1,0:T(8,128)S(1)}, f32[32,128,4]{2,1,0:T(8,128)}, u32[]{:S(2)}) copy-start(f32[32,128,4]{2,1,0:T(8,128)} %copy.26) | copy-start | bytes 196612
  116.0 1.4 copy-start.4
  117.8 25.4 %copy-start.17 = (f32[8,4]{0,1:T(4,128)S(1)}, f32[8,4]{0,1:T(4,128)}, u32[]{:S(2)}) copy-start(f32[8,4]{0,1:T(4,128)} %param.13) | copy-start | bytes 388
  117.8 2.0 copy-start.2
  134.3 0.9 copy-start.11
  135.2 43.9 %all-to-all-start.3 = ((f32[32,48,128]{2,1,0:T(8,128)}), f32[32,48,128]{2,1,0:T(8,128)S(1)}, u32[]{:S(2)}, u32[]{:S(2)}) async-start(f32[32,48,128]{2,1,0:T(8,128)} %bitcast.159), calls=%async_computation.3 | async-start | bytes 1572864 | tf_op jit(solution)/shard_map/all_to_all | solution.py:612
  143.3 2.2 copy-start.3
  145.5 1.6 copy-start.5
  147.1 2.3 copy-start.10
  177.0 2.2 copy-start
  179.1 2.3 copy-start.1
  188.9 2.2 copy-start.7
  191.1 1.0 copy-start.12
  192.2 29.1 %all-to-all-start.4 = ((f32[8,2,144,128]{3,2,1,0:T(8,128)}), f32[8,2,144,128]{3,2,1,0:T(8,128)S(1)}, u32[]{:S(2)}, u32[]{:S(2)}) async-start(f32[8,2,144,128]{3,2,1,0:T(8,128)} %bitcast.160), calls=%async_computation.4 | async-start | bytes 2359296 | tf_op jit(solution)/shard_map/all_to_all | solution.py:617
  221.3 20.9 %copy-start.8 = (f32[768,1536]{1,0:T(8,128)S(1)}, f32[768,1536]{1,0:T(8,128)}, u32[]{:S(2)}) copy-start(f32[768,1536]{1,0:T(8,128)} %copy-done.7) | copy-start | bytes 14155780

commit v2 on v1

--- a/solution.py
+++ b/solution.py
@@ -86,72 +86,10 @@
             pltpu.VMEM((total, LANE), f32),
             pltpu.SemaphoreType.DMA,
         ],
-        compiler_params=vmem(32),
+        compiler_params=vmem(60),
         cost_estimate=cost(0, 4 << 20),
         name="pack",
     )(slots, cells, jnp.zeros((total,), jnp.int32), values)
-
-
-def deposit_kernel(places, got, field, spread, f1, f2, f3, masks):
-    total = spread.shape[0]
-    chains = [field, f1, f2, f3]
-    depth = field.shape[0]
-
-    @pl.loop(0, depth // 64)
-    def _(i):
-        at = pl.ds(pl.multiple_of(i * 64, 64), 64)
-        for chain in chains:
-            chain[at, :] = jnp.zeros((64, LANE), f32)
-
-    lane_quarter = lax.broadcasted_iota(jnp.int32, (8, LANE), 1) // 32
-    masks[...] = (lane_quarter == lax.broadcasted_iota(jnp.int32, (8, LANE), 0)).astype(f32)
-    quarter = lax.broadcasted_iota(jnp.int32, (64, LANE), 1) // 32
-
-    @pl.loop(0, total // 256)
-    def _(d):
-        part = got[pl.ds(pl.multiple_of(d * 64, 64), 64), :]
-        for k in range(4):
-            one = jnp.where(quarter == k, part, 0.0)
-            one = one + pltpu.roll(one, 32, 1)
-            one = one + pltpu.roll(one, 64, 1)
-            spread[pl.ds(pl.multiple_of(d * 256 + k * 64, 64), 64), :] = one
-
-    step = 4
-
-    @pl.loop(0, total // (4 * step))
-    def _(i):
-        for u in range(step):
-            loads = []
-            for c in range(4):
-                j = (i * step + u) * 4 + c
-                place = places[j]
-                row = lax.shift_right_logical(place, 2)
-                mask = masks[pl.ds(place & 3, 1), :]
-                loads.append((row, spread[pl.ds(j, 1), :] * mask))
-            olds = [chains[c][pl.ds(loads[c][0], 1), :] for c in range(4)]
-            for c in range(4):
-                chains[c][pl.ds(loads[c][0], 1), :] = olds[c] + loads[c][1]
-
-    @pl.loop(0, depth // 64)
-    def _(i):
-        at = pl.ds(pl.multiple_of(i * 64, 64), 64)
-        field[at, :] = (field[at, :] + f1[at, :]) + (f2[at, :] + f3[at, :])
-
-
-def deposit(places, got, depth):
-    total = places.shape[0]
-    return pl.pallas_call(
-        deposit_kernel,
-        out_shape=jax.ShapeDtypeStruct((depth, LANE), f32),
-        in_specs=[pl.BlockSpec(memory_space=pltpu.SMEM), pl.BlockSpec(memory_space=pltpu.VMEM)],
-        out_specs=pl.BlockSpec(memory_space=pltpu.VMEM),
-        scratch_shapes=[pltpu.VMEM((total, LANE), f32)]
-        + [pltpu.VMEM((depth, LANE), f32)] * 3
-        + [pltpu.VMEM((8, LANE), f32)],
-        compiler_params=vmem(40),
-        cost_estimate=cost(0, 16 << 20),
-        name="deposit",
-    )(places, got)
 
 
 def lat_sweeps(rows, decay, starts):
@@ -169,48 +107,117 @@
     return rows, ends
 
 
-def lat_moments_kernel(row_count, groups, field, background, decay, forced, moments):
-    ct = pl.program_id(0)
-    tiles = background.shape[1] // LANE
-    for rr in range(row_count // 4):
-        turned = field[rr].T
-        for q in range(4):
-            for o in range(groups // 8):
-                at = pl.ds(o * 8 * row_count + rr * 4 + q, 8, stride=row_count)
-                first = q * groups + o * 8
-                forced[at, :] = background[at, :] + turned[first : first + 8, :]
-    zero = jnp.zeros((8, LANE), f32)
-    for o in range(groups // 8):
-        rows = [
-            forced[pl.ds(o * 8 * row_count + r, 8, stride=row_count), :] for r in range(row_count)
-        ]
-        _, ends = lat_sweeps(
-            rows, lambda r: decay[r * groups + o * 8 : r * groups + o * 8 + 8, :], [zero] * 4
-        )
+CHAINS = 8
+
+
+def forced_kernel(row_count, groups, places, got, quarters, background, decay, forced, moments, spread, *chains):
+    step_id = pl.program_id(0)
+    total = spread.shape[0]
+    depth = chains[0].shape[0]
+    sources = got.shape[0]
+
+    @pl.when(step_id == 0)
+    def _():
+        @pl.loop(0, depth // 64)
+        def _(i):
+            at = pl.ds(pl.multiple_of(i * 64, 64), 64)
+            for chain in chains:
+                chain[at, :] = jnp.zeros((64, LANE), f32)
+
+        lane = lax.broadcasted_iota(jnp.int32, (8, LANE), 1) // 32
+        pick = (lane == lax.broadcasted_iota(jnp.int32, (8, LANE), 0)).astype(bf16)
+        quarter = lax.broadcasted_iota(jnp.int32, (64, LANE), 1) // 32
+        wanted = quarter.astype(f32)
+
+        def turns(x):
+            return [x] + [pltpu.roll(x, 32 * k, 1) for k in range(1, 4)]
+
+        def repeat(turned, k):
+            out = turned[(3 - k) % 4]
+            for q in range(3):
+                out = jnp.where(quarter == q, turned[(q - k) % 4], out)
+            return out
+
+        @pl.loop(0, sources)
+        def _(d):
+            part = turns(got[d, :64, :])
+            mark = turns(
+                lax.dot_general(
+                    quarters[d].astype(bf16), pick, (((0,), (0,)), ((), ())), preferred_element_type=f32
+                )
+            )
+            for k in range(4):
+                one = jnp.where(repeat(mark, k) == wanted, repeat(part, k), 0.0)
+                spread[pl.ds(pl.multiple_of(d * 256 + k * 64, 64), 64), :] = one
+
+        step = 4
+
+        @pl.loop(0, total // (CHAINS * step))
+        def _(i):
+            for u in range(step):
+                spots = [(i * step + u) * CHAINS + c for c in range(CHAINS)]
+                where = [pl.ds(places[j], 1) for j in spots]
+                adds = [spread[pl.ds(j, 1), :] for j in spots]
+                olds = [chains[c][where[c], :] for c in range(CHAINS)]
+                for c in range(CHAINS):
+                    chains[c][where[c], :] = olds[c] + adds[c]
+
+    @pl.when(step_id > 0)
+    def _():
+        ct = step_id - 1
+        columns = depth // (row_count // 4)
+        for rr in range(row_count // 4):
+            at = pl.ds(pl.multiple_of(rr * columns + ct * LANE, LANE), LANE)
+            parts = [chain[at, :] for chain in chains]
+            while len(parts) > 1:
+                parts = [a + b for a, b in zip(parts[::2], parts[1::2])]
+            turned = parts[0].T
+            for q in range(4):
+                for o in range(groups // 8):
+                    at = pl.ds(o * 8 * row_count + rr * 4 + q, 8, stride=row_count)
+                    first = q * groups + o * 8
+                    forced[at, :] = background[at, :] + turned[first : first + 8, :]
+        zero = jnp.zeros((8, LANE), f32)
         per_group = moments.shape[0] // groups
-        for k in range(4):
-            start = o * 8 * per_group + k * (per_group // 4) + ct
-            moments[pl.ds(start, 8, stride=per_group), :] = ends[k]
-
-
-def lat_moments(field, background, decay, row_count, groups):
+        for o in range(groups // 8):
+            rows = [
+                forced[pl.ds(o * 8 * row_count + r, 8, stride=row_count), :]
+                for r in range(row_count)
+            ]
+            _, ends = lat_sweeps(
+                rows, lambda r: decay[r * groups + o * 8 : r * groups + o * 8 + 8, :], [zero] * 4
+            )
+            for k in range(4):
+                start = o * 8 * per_group + k * (per_group // 4) + ct
+                moments[pl.ds(start, 8, stride=per_group), :] = ends[k]
+
+
+def force(places, got, quarters, background, decay, row_count, groups):
     rows, columns = background.shape
     tiles = columns // LANE
-    block = pl.BlockSpec((rows, LANE), lambda i: (0, i))
-    whole = pl.BlockSpec((rows, LANE), lambda i: (0, 0))
+    total = places.shape[0]
+    depth = rows * columns // LANE
+    block = pl.BlockSpec((rows, LANE), lambda i: (0, jnp.maximum(i - 1, 0)))
     return pl.pallas_call(
-        functools.partial(lat_moments_kernel, row_count, groups),
-        grid=(tiles,),
+        functools.partial(forced_kernel, row_count, groups),
+        grid=(tiles + 1,),
         out_shape=(
             jax.ShapeDtypeStruct(background.shape, f32),
             jax.ShapeDtypeStruct((groups * 4 * tiles, LANE), f32),
         ),
-        in_specs=[pl.BlockSpec((row_count // 4, LANE, LANE), lambda i: (0, i, 0)), block, whole],
+        in_specs=[
+            pl.BlockSpec(memory_space=pltpu.SMEM),
+            pl.BlockSpec(got.shape, lambda i: (0, 0, 0), pipeline_mode=pl.Buffered(1)),
+            pl.BlockSpec(quarters.shape, lambda i: (0, 0, 0), pipeline_mode=pl.Buffered(1)),
+            block,
+            pl.BlockSpec((rows, LANE), lambda i: (0, 0), pipeline_mode=pl.Buffered(1)),
+        ],
         out_specs=(block, pl.BlockSpec((groups * 4 * tiles, LANE), lambda i: (0, 0))),
-        compiler_params=vmem(32),
+        scratch_shapes=[pltpu.VMEM((total, LANE), f32)] + [pltpu.VMEM((depth, LANE), f32)] * CHAINS,
+        compiler_params=vmem(60),
         cost_estimate=cost(0, 16 << 20),
-        name="lat_moments",
-    )(field.reshape(row_count // 4, columns, LANE), background, decay)
+        name="force",
+    )(places, got, quarters, background, decay)
 
 
 def lon_weights(length, columns):
@@ -256,22 +263,20 @@
         axis=1,
     )
     back = jnp.pad(back, ((0, 0), (0, LANE - 4), (0, 0)))
-    return first, mix, back
-
-
-def split(x):
+    return thirds(first), thirds(mix), thirds(back)
+
+
+def thirds(w):
+    high = lax.reduce_precision(w, 8, 7)
+    low = (w - high).astype(bf16)
+    high = high.astype(bf16)
+    return jnp.concatenate([high, high, low], axis=1)
+
+
+def dot3(x, w):
     high = x.astype(bf16)
-    return high, (x - high.astype(f32)).astype(bf16)
-
-
-def dot3(x, w):
-    xh, xl = split(x)
-    wh, wl = split(w)
-
-    def dot(a, b):
-        return jnp.dot(a, b, preferred_element_type=f32)
-
-    return dot(xh, wh) + (dot(xh, wl) + dot(xl, wh))
+    low = (x - high.astype(f32)).astype(bf16)
+    return jnp.dot(jnp.concatenate([high, low, high], axis=1), w, preferred_element_type=f32)
 
 
 def lon_apply(x, first, mix, back):
@@ -292,25 +297,29 @@
 
 
 def lon_kernel(x, first, mix, back, out):
-    out[...] = lon_apply(x[...], first[0], mix[0], back[0])
-
-
-def lon_filter(x, weights, row_count):
+    count = x.shape[0] // first.shape[0]
+    for g in range(first.shape[0]):
+        at = slice(g * count, (g + 1) * count)
+        out[at, :] = lon_apply(x[at, :], first[g], mix[g], back[g])
+
+
+def lon_filter(x, weights, row_count, half):
     rows, columns = x.shape
-    block = pl.BlockSpec((row_count, columns), lambda i: (i, 0))
+    per_step = 4
+    steps = rows // row_count // per_step // 2
+    block = pl.BlockSpec((per_step * row_count, columns), lambda i: (i + half * steps, 0))
     return pl.pallas_call(
         lon_kernel,
-        grid=(rows // row_count,),
-        out_shape=jax.ShapeDtypeStruct(x.shape, f32),
-        in_specs=[
-            block,
-            pl.BlockSpec((1, LANE, 2 * LANE), lambda i: (i, 0, 0)),
-            pl.BlockSpec((1, LANE, LANE), lambda i: (i, 0, 0)),
-            pl.BlockSpec((1, LANE, LANE), lambda i: (i, 0, 0)),
+        grid=(steps,),
+        out_shape=jax.ShapeDtypeStruct((rows // 2, columns), f32),
+        in_specs=[block]
+        + [
+            pl.BlockSpec((per_step,) + w.shape[1:], lambda i: (i + half * steps, 0, 0))
+            for w in weights
         ],
-        out_specs=block,
-        compiler_params=vmem(32),
-        cost_estimate=cost(6 * rows * columns * 3 * LANE, 60 << 20),
+        out_specs=pl.BlockSpec((per_step * row_count, columns), lambda i: (i, 0)),
+        compiler_params=vmem(60),
+        cost_estimate=cost(3 * rows * columns * 3 * LANE, 30 << 20),
         name="lon",
     )(x, *weights)
 
@@ -404,7 +413,7 @@
         in_specs=[pl.BlockSpec(memory_space=pltpu.VMEM)] * 5,
         out_specs=pl.BlockSpec(memory_space=pltpu.VMEM),
         scratch_shapes=[pltpu.VMEM((128, depth // 4 * LANE), f32)],
-        compiler_params=vmem(32),
+        compiler_params=vmem(60),
         cost_estimate=cost(0, 4 << 20),
         name="hub",
     )(decay, moments, *weights)
@@ -425,11 +434,14 @@
     return rows, ends
 
 
-def lat_states_kernel(row_count, groups, variables, x, decay, states, vert, out, sums):
+def lat_states_kernel(row_count, groups, variables, low, high, decay, states, vert, coef, out, sums):
     ct = pl.program_id(0)
     per_group = states.shape[0] // groups
+    half = low.shape[0]
     for o in range(groups // 8):
-        rows = [x[pl.ds(o * 8 * row_count + r, 8, stride=row_count), :] for r in range(row_count)]
+        base = o * 8 * row_count
+        x, first = (low, base) if base < half else (high, base - half)
+        rows = [x[pl.ds(first + r, 8, stride=row_count), :] for r in range(row_count)]
         starts = [
             states[pl.ds(o * 8 * per_group + k * (per_group // 4) + ct, 8, stride=per_group), :]
             for k in range(4)
@@ -438,9 +450,12 @@
             rows, lambda r: decay[r * groups + o * 8 : r * groups + o * 8 + 8, :], starts
         )
         for r in range(row_count):
-            out[pl.ds(o * 8 * row_count + r, 8, stride=row_count), :] = rows[r]
+            out[pl.ds(base + r, 8, stride=row_count), :] = rows[r]
     zero = jnp.zeros((8, LANE), f32)
     levels = groups // variables
+    halves = pl.num_programs(0) // 2
+    depth = halves * row_count
+    size = sums.shape[0] // (2 * variables)
     for var in range(variables):
         for t in range(row_count // 8):
             rows = []
@@ -449,67 +464,77 @@
                 rows.append(out[base : base + 8, :])
             _, ends = level_sweeps(rows, lambda lev: vert[lev * variables + var], [zero, zero])
             for k in range(2):
-                sums[var, 0, k, 0, t * 8 : t * 8 + 8, :] = ends[k]
-
-
-def lat_states(x, decay, states, vert, row_count, groups, variables):
-    rows, columns = x.shape
+                start = (var * 2 + ct // halves) * size + k * depth + (ct % halves) * row_count + t * 8
+                sums[pl.ds(pl.multiple_of(start, 8), 8), :] = ends[k]
+
+    @pl.when(ct == 0)
+    def _():
+        for target in range(2 * variables):
+            start = target * size + 2 * depth
+            sums[start : start + 8, :] = coef[target // 2]
+
+
+def lat_states(low, high, decay, states, vert, coef, row_count, groups, variables):
+    rows, columns = 2 * low.shape[0], low.shape[1]
     tiles = columns // LANE
-    half = tiles // 2
+    part = pl.BlockSpec((rows // 2, LANE), lambda i: (0, i))
     block = pl.BlockSpec((rows, LANE), lambda i: (0, i))
+    size = 2 * variables * (tiles * row_count + 8)
     return pl.pallas_call(
         functools.partial(lat_states_kernel, row_count, groups, variables),
         grid=(tiles,),
         out_shape=(
-            jax.ShapeDtypeStruct(x.shape, f32),
-            jax.ShapeDtypeStruct((variables, 2, 2, half, row_count, LANE), f32),
+            jax.ShapeDtypeStruct((rows, columns), f32),
+            jax.ShapeDtypeStruct((size, LANE), f32),
         ),
         in_specs=[
-            block,
+            part,
+            part,
             pl.BlockSpec((rows, LANE), lambda i: (0, 0)),
             pl.BlockSpec(states.shape, lambda i: (0, 0)),
             pl.BlockSpec(memory_space=pltpu.SMEM),
+            pl.BlockSpec(coef.shape, lambda i: (0, 0, 0)),
         ],
-        out_specs=(
-            block,
-            pl.BlockSpec(
-                (variables, 1, 2, 1, row_count, LANE),
-                lambda i: (0, i // half, 0, i % half, 0, 0),
-            ),
-        ),
-        compiler_params=vmem(32),
+        out_specs=(block, pl.BlockSpec((size, LANE), lambda i: (0, 0))),
+        compiler_params=vmem(60),
         cost_estimate=cost(0, 12 << 20),
         name="lat_states",
-    )(x, decay, states, vert)
-
-
-def level_hub_kernel(coef, sums, states):
+    )(low, high, decay, states, vert, coef)
+
+
+def level_hub_kernel(sums, states):
     bands = sums.shape[0]
-    depth = sums.shape[2]
+    depth = states.shape[2]
+    full = [jnp.broadcast_to(sums[b, 2 * depth : 2 * depth + 1, :], (8, LANE)) for b in range(bands)]
+    both = [
+        jnp.broadcast_to(sums[b, 2 * depth + 1 : 2 * depth + 2, :], (8, LANE)) for b in range(bands)
+    ]
     for t in range(depth // 8):
         at = slice(t * 8, t * 8 + 8)
+        later = slice(depth + t * 8, depth + t * 8 + 8)
         state = jnp.zeros((8, LANE), f32)
         entering = []
         for b in range(bands):
             entering.append(state)
             states[b, 0, at, :] = state
-            state = coef[0, b] * state + sums[b, 0, at, :]
+            state = full[b] * state + sums[b, at, :]
         state = jnp.zeros((8, LANE), f32)
         for b in range(bands - 1, -1, -1):
             states[b, 1, at, :] = state
-            state = coef[0, b] * state + (sums[b, 1, at, :] + coef[1, b] * entering[b])
-
-
-def level_hub(coef, sums):
+            state = full[b] * state + (sums[b, later, :] + both[b] * entering[b])
+
+
+def level_hub(sums):
+    bands, size, _ = sums.shape
     return pl.pallas_call(
         level_hub_kernel,
-        out_shape=jax.ShapeDtypeStruct(sums.shape, f32),
-        in_specs=[pl.BlockSpec(memory_space=pltpu.SMEM), pl.BlockSpec(memory_space=pltpu.VMEM)],
+        out_shape=jax.ShapeDtypeStruct((bands, 2, (size - 8) // 2, LANE), f32),
+        in_specs=[pl.BlockSpec(memory_space=pltpu.VMEM)],
         out_specs=pl.BlockSpec(memory_space=pltpu.VMEM),
-        compiler_params=vmem(16),
+        compiler_params=vmem(60),
         cost_estimate=cost(0, 3 << 20),
         name="level_hub",
-    )(coef, sums)
+    )(sums)
 
 
 def level_states_kernel(row_count, groups, variables, x, vert, states, out):
@@ -545,23 +570,25 @@
             ),
         ],
         out_specs=block,
-        compiler_params=vmem(32),
+        compiler_params=vmem(60),
         cost_estimate=cost(0, 11 << 20),
         name="level_states",
     )(x, vert, states)
 
 
 def level_coefficients(decays):
-    levels = decays.shape[1]
-    state, down = jnp.ones_like(decays[:, 0]), []
+    levels = decays.shape[0]
+    state, down = jnp.ones_like(decays[0]), []
     for r in range(levels):
-        state = decays[:, r] * state
+        state = decays[r] * state
         down.append(state)
     full = state
     state = jnp.zeros_like(full)
     for r in range(levels - 1, -1, -1):
-        state = down[r] + decays[:, r] * (state - down[r])
-    return jnp.stack([full, state])
+        state = down[r] + decays[r] * (state - down[r])
+    both = jnp.stack([full, state], axis=1)
+    both = jnp.pad(both, ((0, 0), (0, 6)))
+    return jnp.broadcast_to(both[:, :, None], both.shape + (LANE,))
 
 
 def per_device(background, obs_columns, obs_owner, obs_cell, lat_length, lon_length, vert_length):
@@ -569,7 +596,6 @@
     sub_count = lax.axis_size("sub")
     band_count = lax.axis_size("band")
     sub_index = lax.axis_index("sub")
-    band_index = lax.axis_index("band")
     groups = level_count * var_count
     tiles = lon_count // LANE
     tile_field = background.reshape(groups * row_count, lon_count)
@@ -581,16 +607,20 @@
     row, column = obs_cell // lon_count, obs_cell % lon_count
     place = ((row // 4) * lon_count + column) * 4 + row % 4
     packed, sent = pack(slots, place, obs_values, sub_count * capacity)
-    got = lax.all_to_all(
-        packed.reshape(sub_count, capacity // 4, LANE), "sub", 0, 0, tiled=True
-    )
-    places = lax.all_to_all(sent.reshape(sub_count, capacity), "sub", 0, 0, tiled=True)
-
-    all_vert = lax.all_gather(vert_length, "band")
-    vert_decay = jnp.exp(-1.0 / vert_length).reshape(groups)
-    own_var = band_index // 2
-    hub_vert = lax.dynamic_index_in_dim(jnp.exp(-1.0 / all_vert), own_var, 2, False)
-    coef = level_coefficients(hub_vert)
+    lines = capacity // LANE
+    message = jnp.concatenate(
+        [
+            packed.reshape(sub_count, capacity // 4, LANE),
+            sent.astype(f32).reshape(sub_count, lines, LANE),
+            jnp.zeros((sub_count, 8 - lines, LANE), f32),
+        ],
+        axis=1,
+    )
+    got = lax.all_to_all(message, "sub", 0, 0, tiled=True)
+
+    vert_decay = jnp.exp(-1.0 / vert_length)
+    coef = level_coefficients(vert_decay)
+    vert_decay = vert_decay.reshape(groups)
 
     lat_all = jnp.exp(-1.0 / lat_length).reshape(groups, sub_count, row_count)
     own_lat = lax.dynamic_index_in_dim(lat_all, sub_index, 1, False)
@@ -602,23 +632,26 @@
     weights = lon_weights(lengths, lon_count)
     own_weights = [lax.dynamic_slice_in_dim(w, sub_index, 1, 0) for w in weights]
 
-    field = deposit(places.reshape(-1), got.reshape(-1, LANE), groups * row_count * lon_count // LANE)
-    forced, moments = lat_moments(field, tile_field, decay, row_count, groups)
+    places = got[:, capacity // 4 : capacity // 4 + lines, :].reshape(-1).astype(jnp.int32)
+    quarters = (places & 3).astype(f32).reshape(sub_count, 4, capacity // 4)
+    quarters = jnp.pad(quarters, ((0, 0), (0, 4), (0, 0)))
+    forced, moments = force(places >> 2, got, quarters, tile_field, decay, row_count, groups)
     moments = lax.all_to_all(
         moments.reshape(sub_count, 4 * tiles, LANE), "sub", 0, 0, tiled=True
     )
-    smooth = lon_filter(forced, weights, row_count)
+    low = lon_filter(forced, weights, row_count, 0)
+    moments, low = lax.optimization_barrier((moments, low))
     states = hub(hub_lat, moments.reshape(-1, LANE), own_weights)
+    states, forced = lax.optimization_barrier((states, forced))
     states = lax.all_to_all(states.reshape(sub_count, 4 * tiles, LANE), "sub", 0, 0, tiled=True)
+    high = lon_filter(forced, weights, row_count, 1)
     smooth, sums = lat_states(
-        smooth, decay, states.reshape(-1, LANE), vert_decay, row_count, groups, var_count
-    )
-    depth = tiles // 2 * row_count
+        low, high, decay, states.reshape(-1, LANE), vert_decay, coef, row_count, groups, var_count
+    )
     sums = lax.all_to_all(
-        sums.reshape(band_count, 2, depth, LANE), "band", 0, 0, tiled=True
-    )
-    entering = level_hub(coef, sums)
-    entering = lax.all_to_all(entering, "band", 0, 0, tiled=True)
+        sums.reshape(band_count, -1, LANE), "band", 0, 0, tiled=True
+    )
+    entering = lax.all_to_all(level_hub(sums), "band", 0, 0, tiled=True)
     result = level_states(
         smooth,
         vert_decay,

time: 249 us -> 235 us (0.944)
  waiting for transfers between devices: 39.2 us -> 26.3 us
  local copies, waits for them, and re-layouts: 28.3 us -> 17 us
  starting transfers between devices: 39.2 us -> 30 us
  blocking collectives: 42 us -> 48.6 us
  other arithmetic: 8.86 us -> 15.4 us
  Pallas kernels: 89.4 us -> 94.4 us
    all_to_all x1 -> x2, blocking collectives: 20.2 us -> 48.6 us  [the longest x1 26.9 us: per_device(): lax.all_to_all(sums.reshape(band_count, -1, LANE), 'band', 0, 0, tiled=True)]
    all_gather x1 -> x0, blocking collectives: 21.8 us -> none  [per_device(): all_vert = lax.all_gather(vert_length, 'band')]
    unnamed x45 -> x20, local copies, waits for them, and re-layouts: 23.6 us -> 5.34 us
    all_to_all x1, waiting for transfers between devices: 11.6 us -> 0.01 us  [per_device(): lax.all_to_all(moments.reshape(sub_count, 4 * tiles, LANE), 'sub', 0, 0,...]
    all_to_all x3 -> x1, starting transfers between devices: 22.8 us -> 12.1 us  [per_device(): got = lax.all_to_all(message, 'sub', 0, 0, tiled=True)]
    all_to_all x3 -> x1, waiting for transfers between devices: 27.6 us -> 19.7 us  [per_device(): got = lax.all_to_all(message, 'sub', 0, 0, tiled=True)]
    convert_element_type x0 -> x5, other arithmetic: none -> 7.01 us  [the longest x3 4.7 us: thirds(): high = high.astype(bf16)]
    all_to_all x1, waiting for transfers between devices: 0.01 us -> 6.64 us  [per_device(): lax.all_to_all(states.reshape(sub_count, 4 * tiles, LANE), 'sub', 0, 0, t...]
  transfers between devices with their start and end apart: 5 -> 3, of which waited for: 3 -> 2; matrix products, arithmetic and copies ran while one was open for 4% -> 6% of each run, Pallas kernels for 11% -> 9%
where the time goes in v2:
time: 235 us; the launch traced here: 233 us
  Pallas kernels  94.4 us (40%)
  blocking collectives  48.6 us (21%)
  starting transfers between devices  30 us (13%)
  waiting for transfers between devices  26.3 us (11%)
  local copies, waits for them, and re-layouts  17 us (7%)
  other arithmetic  15.4 us (7%)
    pallas_call x1, Pallas kernels, force(): pl.pallas_call(functools.partial(forced_kernel, row_count, groups), grid=...  33.5 us
    all_to_all x1, blocking collectives, per_device(): lax.all_to_all(sums.reshape(band_count, -1, LANE), 'band', 0, 0, tiled=True)  26.9 us
    all_to_all x1, blocking collectives, per_device(): entering = lax.all_to_all(level_hub(sums), 'band', 0, 0, tiled=True)  21.8 us
    pallas_call x2, Pallas kernels, lon_filter(): pl.pallas_call(lon_kernel, grid=(steps,), out_shape=jax.ShapeDtypeStruct(...  21.3 us
    all_to_all x1, waiting for transfers between devices, per_device(): got = lax.all_to_all(message, 'sub', 0, 0, tiled=True)  19.7 us
    all_to_all x1, starting transfers between devices, per_device(): got = lax.all_to_all(message, 'sub', 0, 0, tiled=True)  12.1 us
    pallas_call x1, Pallas kernels, lat_states(): pl.pallas_call(functools.partial(lat_states_kernel, row_count, groups, va...  11.9 us
    pallas_call x1, Pallas kernels, pack(): pl.pallas_call(pack_kernel, out_shape=(jax.ShapeDtypeStruct((total // 4,...  11.1 us
  transfers between devices with their start and end apart: 3, of which 2 were waited for; matrix products, arithmetic and copies ran while one was open for 6% of the time, Pallas kernels for 9%

profile of v2, /device:TPU:1, one launch (start us, length us, event | category | flops | bytes accessed | tf_op | source)
XLA Modules:
  0.0 233.1 jit_solution(16335093545632735465)
XLA Ops:
  0.0 0.7 broadcast_multiply_fusion.1
  0.7 0.9 convert_reduce_fusion
  1.7 1.1 fusion.7
  2.8 2.0 reshape.1411.values
  4.8 1.4 fusion.24
  6.2 0.6 broadcast_in_dim.37.zeros
  6.8 11.1 %pack.1 = (f32[2048,128]{1,0:T(8,128)}, s32[8192]{0:T(1024)}) custom-call(s32[4096]{0:T(1024)} %get-tuple-element.67.slots, s32[4096]{0:T(1024)} %get-tuple-element.66.cells, s32[8192]{0:T(1024)} %broadcast_in_dim.37.zeros, f32[32,4096]{1,0:T(8,128)} %reshape.1411.values), custom_call_target="tpu_custom_call" | custom-call | bytes 4194304 | tf_op jit(solution)/shard_map/pack/pallas_call | solution.py:76
  18.0 0.8 convert_element_type.74
  18.8 2.4 %maximum_maximum_fusion = f32[32,72,128]{2,1,0:T(8,128)} fusion(f32[32,2,128]{2,1,0:T(2,128)S(1)} %bitcast.156, f32[32,64,128]{2,1,0:T(8,128)} %bitcast.153, f32[72]{0:T(128)S(1)} %pad.48.clone), kind=kLoop, calls=%fused_computation.26 | loop fusion | flops 589824 | bytes 2261280 | tf_op jit(solution)/shard_map/concatenate | solution.py:611
  21.2 12.1 %all-to-all-start = ((f32[32,72,128]{2,1,0:T(8,128)}), f32[32,72,128]{2,1,0:T(8,128)}, u32[]{:S(2)}, u32[]{:S(2)}) async-start(f32[32,72,128]{2,1,0:T(8,128)} %maximum_maximum_fusion), calls=%async_computation | async-start | bytes 2359296 | tf_op jit(solution)/shard_map/all_to_all | solution.py:619
  33.5 0.4 reshape.1415
  34.4 2.0 copy.29
  36.5 0.6 pad.23.decay
  37.1 0.1 fusion.17
  37.3 0.1 fusion.20
  37.4 0.1 fusion.11
  37.6 3.1 %reduce-precision_convert_fusion.2 = (bf16[32,128,128]{2,1,0:T(8,128)(2,1)S(1)}, bf16[32,128,128]{2,1,0:T(8,128)(2,1)S(1)}, f32[32,128,128]{2,1,0:T(8,128)}) fusion(pred[128,128]{1,0:T(8,128)(4,1)S(1)} %get-tuple-element.52, f32[32]{0:T(128)S(1)} %exponential-minus-one_negate_fusion, f32[32]{0:T(128)S(1)} %broadcast_in_dim_reshape.3, ...), kind=kLoop, calls=%fused_computation.11 | loop fusion | flops 7340032 | bytes 4489856 | tf_op jit(solution)/shard_map/convert_element_type | solution.py:272
  40.7 0.2 pad_maximum_fusion.1.mix
  41.0 0.2 add_multiply_fusion.1
  41.2 19.7 %all-to-all-done.got = f32[32,72,128]{2,1,0:T(8,128)} async-done(((f32[32,72,128]{2,1,0:T(8,128)}), f32[32,72,128]{2,1,0:T(8,128)}, u32[]{:S(2)}, u32[]{:S(2)}) %all-to-all-start) | async-done | bytes 1179680 | tf_op jit(solution)/shard_map/all_to_all | solution.py:619
  60.9 1.5 and_convert_fusion
  62.5 0.7 pad.20.quarters
  63.2 0.9 broadcast_in_dim.43.decay
  64.1 33.5 %force.1 = (f32[768,1536]{1,0:T(8,128)}, f32[1536,128]{1,0:T(8,128)}) custom-call(s32[8192]{0:T(1024)} %bitcast.155, f32[32,72,128]{2,1,0:T(8,128)} %all-to-all-done.got, f32[32,8,64]{2,1,0:T(8,128)} %pad.20.quarters, f32[768,1536]{1,0:T(8,128)} %bitcast.148, f32[768,128]{1,0:T(8,128)} %broadcast_in_dim.43.decay), custom_call_target="tpu_custom_call" | custom-call | bytes 16777216 | tf_op jit(solution)/shard_map/force/pallas_call | solution.py:201
  97.7 8.5 %all-to-all-start.1 = ((f32[32,48,128]{2,1,0:T(8,128)}), f32[32,48,128]{2,1,0:T(8,128)}, u32[]{:S(2)}, u32[]{:S(2)}) async-start(f32[32,48,128]{2,1,0:T(8,128)} %bitcast.154), calls=%async_computation.1 | async-start | bytes 1572864 | tf_op jit(solution)/shard_map/all_to_all | solution.py:639
  106.2 0.7 constant_dynamic-slice_fusion.1.mix
  106.9 0.6 reduce-precision_convert_fusion.1
  107.5 0.3 pad_maximum_fusion.2.back
  107.8 0.7 constant_dynamic-slice_fusion.back
  108.5 1.2 copy-done.3
  109.7 1.1 copy-done.4
  110.9 1.0 reduce-precision_convert_fusion
  111.9 1.4 pad_maximum_fusion.first
  113.3 2.6 %copy-done = bf16[32,384,256]{2,1,0:T(8,128)(2,1)} copy-done((bf16[32,384,256]{2,1,0:T(8,128)(2,1)}, bf16[32,384,256]{2,1,0:T(8,128)(2,1)S(1)}, u32[]{:S(2)}) %copy-start) | copy-done | bytes 6291480
  116.0 0.7 constant_dynamic-slice_fusion.2.first
  116.7 10.7 %lon.2.low = f32[384,1536]{1,0:T(8,128)} custom-call(f32[768,1536]{1,0:T(8,128)} %get-tuple-element.21.x, bf16[32,384,256]{2,1,0:T(8,128)(2,1)} %copy-done, bf16[32,384,128]{2,1,0:T(8,128)(2,1)} %copy-done.1, bf16[32,384,128]{2,1,0:T(8,128)(2,1)} %copy-done.2), custom_call_target="tpu_custom_call" | custom-call | flops 1358954496 | bytes 31457280 | tf_op jit(solution)/shard_map/lon/pallas_call | solution.py:311
  127.3 4.8 %hub.1 = f32[1536,128]{1,0:T(8,128)} custom-call(f32[24,128]{1,0:T(8,128)} %pad.23.decay, f32[1536,128]{1,0:T(8,128)} %bitcast.16.moments, bf16[1,384,256]{2,1,0:T(8,128)(2,1)} %constant_dynamic-slice_fusion.2.first, bf16[1,384,128]{2,1,0:T(8,128)(2,1)} %constant_dynamic-slice_fusion.1.mix, bf16[1,384,128]{2,1,0:T(8,128)(2,1)} %constant_dynamic-slice_fusion.back), custom_call_target="tpu_custom_call" | custom-call | bytes 4194304 | tf_op jit(solution)/shard_map/hub/pallas_call | solution.py:410
  132.1 9.3 %all-to-all-start.2 = ((f32[32,48,128]{2,1,0:T(8,128)}), f32[32,48,128]{2,1,0:T(8,128)S(1)}, u32[]{:S(2)}, u32[]{:S(2)}) async-start(f32[32,48,128]{2,1,0:T(8,128)} %bitcast.151), calls=%async_computation.2 | async-start | bytes 1572864 | tf_op jit(solution)/shard_map/all_to_all | solution.py:646
  141.6 0.7 reshape.1420.vert
  142.3 0.3 slice_reduce_fusion.7
  142.7 10.7 %lon.3.high = f32[384,1536]{1,0:T(8,128)} custom-call(f32[768,1536]{1,0:T(8,128)} %get-tuple-element.21.x, bf16[32,384,256]{2,1,0:T(8,128)(2,1)} %copy-done, bf16[32,384,128]{2,1,0:T(8,128)(2,1)} %copy-done.1, bf16[32,384,128]{2,1,0:T(8,128)(2,1)} %copy-done.2), custom_call_target="tpu_custom_call" | custom-call | flops 1358954496 | bytes 31457280 | tf_op jit(solution)/shard_map/lon/pallas_call | solution.py:311
  153.4 6.6 %all-to-all-done.2 = f32[32,48,128]{2,1,0:T(8,128)S(1)} async-done(((f32[32,48,128]{2,1,0:T(8,128)}), f32[32,48,128]{2,1,0:T(8,128)S(1)}, u32[]{:S(2)}, u32[]{:S(2)}) %all-to-all-start.2) | async-done | bytes 786464 | tf_op jit(solution)/shard_map/all_to_all | solution.py:646
  160.0 0.8 broadcast_in_dim.73.coef
  160.9 11.9 %lat_states.1 = (f32[768,1536]{1,0:T(8,128)}, f32[2368,128]{1,0:T(8,128)}) custom-call(f32[384,1536]{1,0:T(8,128)} %lon.2.low, f32[384,1536]{1,0:T(8,128)} %lon.3.high, f32[768,128]{1,0:T(8,128)} %broadcast_in_dim.43.decay, f32[1536,128]{1,0:T(8,128)} %bitcast.150, f32[32]{0:T(128)} %reshape.1420.vert, f32[4,8,128]{2,1,0:T(8,128)} %broadcast_in_dim.73.coef), custom_call_target="tpu_custom_call" | custom-call | bytes 12582912 | tf_op jit(solution)/shard_map/lat_states/pallas_call | solution.py:483
  172.8 26.9 %all_to_all.25.sums = f32[8,296,128]{2,1,0:T(8,128)} all-to-all(f32[8,296,128]{2,1,0:T(8,128)} %bitcast.152), channel_id=1, replica_groups=mesh['band'=8,'sub'=32] {'band'}, dimensions={0} | all-to-all | bytes 2424832 | tf_op jit(solution)/shard_map/all_to_all | solution.py:651
  199.7 2.4 %level_hub.1 = f32[8,2,144,128]{3,2,1,0:T(8,128)} custom-call(f32[8,296,128]{2,1,0:T(8,128)} %all_to_all.25.sums), custom_call_target="tpu_custom_call" | custom-call | bytes 3145728 | tf_op jit(solution)/shard_map/level_hub/pallas_call | solution.py:529
  202.1 21.8 %all_to_all.26 = f32[8,2,144,128]{3,2,1,0:T(8,128)} all-to-all(f32[8,2,144,128]{3,2,1,0:T(8,128)} %level_hub.1), channel_id=1, replica_groups=mesh['band'=8,'sub'=32] {'band'}, dimensions={0} | all-to-all | bytes 2359296 | tf_op jit(solution)/shard_map/all_to_all | solution.py:654
  223.9 9.2 %level_states.1 = f32[768,1536]{1,0:T(8,128)} custom-call(f32[768,1536]{1,0:T(8,128)} %get-tuple-element.23.x, f32[32]{0:T(128)} %reshape.1420.vert, f32[4,2,2,6,24,128]{5,4,3,2,1,0:T(8,128)} %bitcast.149), custom_call_target="tpu_custom_call" | custom-call | bytes 11534336 | tf_op jit(solution)/shard_map/level_states/pallas_call | solution.py:560
  (49 shorter events, 1.4 us)
Async XLA Ops:
  18.8 14.6 %copy-start.6 = (f32[8,4,768]{2,1,0:T(4,128)S(1)}, f32[8,4,768]{2,1,0:T(4,128)}, u32[]{:S(2)}) copy-start(f32[8,4,768]{2,1,0:T(4,128)} %param.11) | copy-start | bytes 294916
  21.2 12.7 %copy-start.7 = (f32[8,4]{0,1:T(4,128)S(1)}, f32[8,4]{0,1:T(4,128)}, u32[]{:S(2)}) copy-start(f32[8,4]{0,1:T(4,128)} %param.12) | copy-start | bytes 388
  21.2 39.6 %all-to-all-start = ((f32[32,72,128]{2,1,0:T(8,128)}), f32[32,72,128]{2,1,0:T(8,128)}, u32[]{:S(2)}, u32[]{:S(2)}) async-start(f32[32,72,128]{2,1,0:T(8,128)} %maximum_maximum_fusion), calls=%async_computation | async-start | bytes 2359296 | tf_op jit(solution)/shard_map/all_to_all | solution.py:619
  40.9 65.3 %copy-start.1 = (bf16[32,384,128]{2,1,0:T(8,128)(2,1)}, bf16[32,384,128]{2,1,0:T(8,128)(2,1)S(1)}, u32[]{:S(2)}) copy-start(bf16[32,384,128]{2,1,0:T(8,128)(2,1)S(1)} %pad_maximum_fusion.1.mix) | copy-start | bytes 9437188
  97.7 29.6 %all-to-all-start.1 = ((f32[32,48,128]{2,1,0:T(8,128)}), f32[32,48,128]{2,1,0:T(8,128)}, u32[]{:S(2)}, u32[]{:S(2)}) async-start(f32[32,48,128]{2,1,0:T(8,128)} %bitcast.154), calls=%async_computation.1 | async-start | bytes 1572864 | tf_op jit(solution)/shard_map/all_to_all | solution.py:639
  107.5 2.3 copy-start.3
  107.5 3.4 %copy-start.4 = (f32[32,128,128]{2,1,0:T(8,128)S(1)}, f32[32,128,128]{2,1,0:T(8,128)}, u32[]{:S(2)}) copy-start(f32[32,128,128]{2,1,0:T(8,128)} %get-tuple-element.57) | copy-start | bytes 6291460
  107.8 4.1 %copy-start.2 = (bf16[32,384,128]{2,1,0:T(8,128)(2,1)}, bf16[32,384,128]{2,1,0:T(8,128)(2,1)S(1)}, u32[]{:S(2)}) copy-start(bf16[32,384,128]{2,1,0:T(8,128)(2,1)S(1)} %pad_maximum_fusion.2.back) | copy-start | bytes 9437188
  113.3 2.6 %copy-start = (bf16[32,384,256]{2,1,0:T(8,128)(2,1)}, bf16[32,384,256]{2,1,0:T(8,128)(2,1)S(1)}, u32[]{:S(2)}) copy-start(bf16[32,384,256]{2,1,0:T(8,128)(2,1)S(1)} %pad_maximum_fusion.first) | copy-start | bytes 18874372
  127.3 14.2 %copy-start.8 = (f32[8,4]{0,1:T(4,128)S(1)}, f32[8,4]{0,1:T(4,128)}, u32[]{:S(2)}) copy-start(f32[8,4]{0,1:T(4,128)} %param.13) | copy-start | bytes 388
  132.1 27.9 %all-to-all-start.2 = ((f32[32,48,128]{2,1,0:T(8,128)}), f32[32,48,128]{2,1,0:T(8,128)S(1)}, u32[]{:S(2)}, u32[]{:S(2)}) async-start(f32[32,48,128]{2,1,0:T(8,128)} %bitcast.151), calls=%async_computation.2 | async-start | bytes 1572864 | tf_op jit(solution)/shard_map/all_to_all | solution.py:646
  160.0 0.9 copy-start.5

commit v3 on v2

--- a/solution.py
+++ b/solution.py
@@ -20,7 +20,7 @@
     return pl.CostEstimate(flops=flops, bytes_accessed=moved, transcendentals=0)
 
 
-def route_slots(owners, sub_count, capacity):
+def route_ranks(owners, sub_count):
     count = owners.shape[0]
     block = 128
     owner_block = owners.reshape(count // block, block)
@@ -31,14 +31,14 @@
     totals = jnp.sum(match.astype(f32), axis=1)
     base = jnp.cumsum(totals, axis=0) - totals
     rank = jnp.sum((ahead + base[:, None, :]) * match.astype(f32), axis=2)
-    return owners * capacity + rank.reshape(count).astype(jnp.int32)
-
-
-def pack_kernel(slots, cells, zeros, values, packed, sent_cells, rows, big, sem):
-    clear = pltpu.make_async_copy(zeros, sent_cells, sem)
-    clear.start()
+    return rank.reshape(count).astype(jnp.int32)
+
+
+def pack_kernel(slots, table, values, packed, rows, big):
     count = values.shape[1]
     total = big.shape[0]
+    targets = total // 256
+    size = packed.shape[0] // targets
 
     @pl.loop(0, total // 64)
     def _(i):
@@ -47,7 +47,22 @@
     for j in range(count // LANE):
         part = values[:, j * LANE : (j + 1) * LANE]
         rows[j * LANE : (j + 1) * LANE, :] = jnp.concatenate([part] * 4, axis=0).T
-    clear.wait()
+
+    owner, rank, place = table[0:1, :], table[1:2, :], table[2:3, :]
+    mine = owner == lax.broadcasted_iota(jnp.int32, (targets, count), 0)
+    spot = (rank == lax.broadcasted_iota(jnp.int32, (256, count), 0)).astype(f32).astype(bf16)
+
+    def put(half):
+        left = jnp.where(mine, half, 0).astype(f32).astype(bf16)
+        return lax.dot_general(
+            left, spot, (((1,), (1,)), ((), ())), preferred_element_type=f32
+        )
+
+    cells = put(lax.shift_right_logical(place, 8)) * 256.0 + put(place & 255)
+    for half in range(2):
+        packed[pl.ds(64 + half, targets, stride=size), :] = cells[:, half * LANE : (half + 1) * LANE]
+    for extra in range(66, size):
+        packed[pl.ds(extra, targets, stride=size), :] = jnp.zeros((targets, LANE), f32)
 
     step = 16
 
@@ -55,41 +70,33 @@
     def _(i):
         for u in range(step):
             j = i * step + u
-            slot = slots[j]
-            big[pl.ds(slot, 1), :] = rows[pl.ds(j, 1), :]
-            sent_cells[slot] = cells[j]
+            big[pl.ds(slots[j], 1), :] = rows[pl.ds(j, 1), :]
 
     quarter = lax.broadcasted_iota(jnp.int32, (64, LANE), 1) // 32
 
-    @pl.loop(0, total // 256)
+    @pl.loop(0, targets)
     def _(d):
         start = pl.multiple_of(d * 256, 256)
         out = big[pl.ds(start, 64), :]
         for k in range(1, 4):
             out = jnp.where(quarter == k, big[pl.ds(start + 64 * k, 64), :], out)
-        packed[pl.ds(pl.multiple_of(d * 64, 64), 64), :] = out
-
-
-def pack(slots, cells, values, total):
+        packed[pl.ds(pl.multiple_of(d * size, 8), 64), :] = out
+
+
+def pack(slots, table, values, targets):
     count = values.shape[1]
-    smem = pl.BlockSpec(memory_space=pltpu.SMEM)
+    total = targets * 256
+    whole = pl.BlockSpec(memory_space=pltpu.VMEM)
     return pl.pallas_call(
         pack_kernel,
-        out_shape=(
-            jax.ShapeDtypeStruct((total // 4, LANE), f32),
-            jax.ShapeDtypeStruct((total,), jnp.int32),
-        ),
-        in_specs=[smem, smem, pl.BlockSpec(memory_space=pl.ANY), pl.BlockSpec(memory_space=pltpu.VMEM)],
-        out_specs=(pl.BlockSpec(memory_space=pltpu.VMEM), smem),
-        scratch_shapes=[
-            pltpu.VMEM((count, LANE), f32),
-            pltpu.VMEM((total, LANE), f32),
-            pltpu.SemaphoreType.DMA,
-        ],
+        out_shape=jax.ShapeDtypeStruct((targets * 72, LANE), f32),
+        in_specs=[pl.BlockSpec(memory_space=pltpu.SMEM), whole, whole],
+        out_specs=whole,
+        scratch_shapes=[pltpu.VMEM((count, LANE), f32), pltpu.VMEM((total, LANE), f32)],
         compiler_params=vmem(60),
         cost_estimate=cost(0, 4 << 20),
         name="pack",
-    )(slots, cells, jnp.zeros((total,), jnp.int32), values)
+    )(slots, table, values)
 
 
 def lat_sweeps(rows, decay, starts):
@@ -202,7 +209,7 @@
         functools.partial(forced_kernel, row_count, groups),
         grid=(tiles + 1,),
         out_shape=(
-            jax.ShapeDtypeStruct(background.shape, f32),
+            jax.ShapeDtypeStruct((tiles, rows, LANE), f32),
             jax.ShapeDtypeStruct((groups * 4 * tiles, LANE), f32),
         ),
         in_specs=[
@@ -212,7 +219,10 @@
             block,
             pl.BlockSpec((rows, LANE), lambda i: (0, 0), pipeline_mode=pl.Buffered(1)),
         ],
-        out_specs=(block, pl.BlockSpec((groups * 4 * tiles, LANE), lambda i: (0, 0))),
+        out_specs=(
+            pl.BlockSpec((None, rows, LANE), lambda i: (jnp.maximum(i - 1, 0), 0, 0)),
+            pl.BlockSpec((groups * 4 * tiles, LANE), lambda i: (0, 0)),
+        ),
         scratch_shapes=[pltpu.VMEM((total, LANE), f32)] + [pltpu.VMEM((depth, LANE), f32)] * CHAINS,
         compiler_params=vmem(60),
         cost_estimate=cost(0, 16 << 20),
@@ -279,11 +289,9 @@
     return jnp.dot(jnp.concatenate([high, low, high], axis=1), w, preferred_element_type=f32)
 
 
-def lon_apply(x, first, mix, back):
-    count, columns = x.shape
-    blocks = columns // LANE
-    stacked = jnp.concatenate([x[:, b * LANE : (b + 1) * LANE] for b in range(blocks)], axis=0)
-    both = dot3(stacked, first)
+def lon_apply(parts, first, mix, back):
+    count, blocks = parts[0].shape[0], len(parts)
+    both = dot3(jnp.concatenate(parts, axis=0), first)
     local, sums = both[:, :LANE], both[:, LANE:]
     line = sums[:count]
     for b in range(1, blocks):
@@ -293,33 +301,35 @@
         [states] + [pltpu.roll(states, LANE - 4 * b, 1) for b in range(1, blocks)], axis=0
     )
     out = local + dot3(spread, back)
-    return jnp.concatenate([out[b * count : (b + 1) * count] for b in range(blocks)], axis=1)
+    return [out[b * count : (b + 1) * count] for b in range(blocks)]
 
 
 def lon_kernel(x, first, mix, back, out):
-    count = x.shape[0] // first.shape[0]
+    tiles = x.shape[0]
+    count = x.shape[1] // first.shape[0]
     for g in range(first.shape[0]):
         at = slice(g * count, (g + 1) * count)
-        out[at, :] = lon_apply(x[at, :], first[g], mix[g], back[g])
+        done = lon_apply([x[b, at, :] for b in range(tiles)], first[g], mix[g], back[g])
+        for b in range(tiles):
+            out[b, at, :] = done[b]
 
 
 def lon_filter(x, weights, row_count, half):
-    rows, columns = x.shape
+    tiles, rows, _ = x.shape
     per_step = 4
     steps = rows // row_count // per_step // 2
-    block = pl.BlockSpec((per_step * row_count, columns), lambda i: (i + half * steps, 0))
     return pl.pallas_call(
         lon_kernel,
         grid=(steps,),
-        out_shape=jax.ShapeDtypeStruct((rows // 2, columns), f32),
-        in_specs=[block]
+        out_shape=jax.ShapeDtypeStruct((tiles, rows // 2, LANE), f32),
+        in_specs=[pl.BlockSpec((tiles, per_step * row_count, LANE), lambda i: (0, i + half * steps, 0))]
         + [
             pl.BlockSpec((per_step,) + w.shape[1:], lambda i: (i + half * steps, 0, 0))
             for w in weights
         ],
-        out_specs=pl.BlockSpec((per_step * row_count, columns), lambda i: (i, 0)),
+        out_specs=pl.BlockSpec((tiles, per_step * row_count, LANE), lambda i: (0, i, 0)),
         compiler_params=vmem(60),
-        cost_estimate=cost(3 * rows * columns * 3 * LANE, 30 << 20),
+        cost_estimate=cost(3 * rows * tiles * LANE * 3 * LANE, 30 << 20),
         name="lon",
     )(x, *weights)
 
@@ -369,7 +379,7 @@
 
     def put(d, k, value):
         for t in range(tiles):
-            work[k * blocks + d, t * LANE : (t + 1) * LANE] = value[t]
+            work[t, k * blocks + d, :] = value[t]
 
     zero = jnp.zeros((tiles, LANE), f32)
     s = [[None] * blocks for _ in range(4)]
@@ -396,13 +406,12 @@
     for k in range(4):
         for d in range(blocks):
             put(d, k, s[k][d])
-    done = lon_apply(work[...], first[0], mix[0], back[0])
-    for k in range(4):
-        for d in range(blocks):
-            row = done[k * blocks + d : k * blocks + d + 1]
-            for t in range(tiles):
-                base = d * depth + k * tiles + t
-                states[base : base + 1, :] = row[:, t * LANE : (t + 1) * LANE]
+    done = lon_apply([work[t] for t in range(tiles)], first[0], mix[0], back[0])
+    for t in range(tiles):
+        for k in range(4):
+            states[pl.ds(k * tiles + t, blocks, stride=depth), :] = done[t][
+                k * blocks : (k + 1) * blocks
+            ]
 
 
 def hub(decay, moments, weights):
@@ -412,7 +421,7 @@
         out_shape=jax.ShapeDtypeStruct(moments.shape, f32),
         in_specs=[pl.BlockSpec(memory_space=pltpu.VMEM)] * 5,
         out_specs=pl.BlockSpec(memory_space=pltpu.VMEM),
-        scratch_shapes=[pltpu.VMEM((128, depth // 4 * LANE), f32)],
+        scratch_shapes=[pltpu.VMEM((depth // 4, 128, LANE), f32)],
         compiler_params=vmem(60),
         cost_estimate=cost(0, 4 << 20),
         name="hub",
@@ -475,16 +484,15 @@
 
 
 def lat_states(low, high, decay, states, vert, coef, row_count, groups, variables):
-    rows, columns = 2 * low.shape[0], low.shape[1]
-    tiles = columns // LANE
-    part = pl.BlockSpec((rows // 2, LANE), lambda i: (0, i))
-    block = pl.BlockSpec((rows, LANE), lambda i: (0, i))
+    tiles, rows = low.shape[0], 2 * low.shape[1]
+    part = pl.BlockSpec((None, rows // 2, LANE), lambda i: (i, 0, 0))
+    block = pl.BlockSpec((None, rows, LANE), lambda i: (i, 0, 0))
     size = 2 * variables * (tiles * row_count + 8)
     return pl.pallas_call(
         functools.partial(lat_states_kernel, row_count, groups, variables),
         grid=(tiles,),
         out_shape=(
-            jax.ShapeDtypeStruct((rows, columns), f32),
+            jax.ShapeDtypeStruct((tiles, rows, LANE), f32),
             jax.ShapeDtypeStruct((size, LANE), f32),
         ),
         in_specs=[
@@ -502,78 +510,214 @@
     )(low, high, decay, states, vert, coef)
 
 
-def level_hub_kernel(sums, states):
-    bands = sums.shape[0]
-    depth = states.shape[2]
-    full = [jnp.broadcast_to(sums[b, 2 * depth : 2 * depth + 1, :], (8, LANE)) for b in range(bands)]
-    both = [
-        jnp.broadcast_to(sums[b, 2 * depth + 1 : 2 * depth + 2, :], (8, LANE)) for b in range(bands)
-    ]
-    for t in range(depth // 8):
-        at = slice(t * 8, t * 8 + 8)
-        later = slice(depth + t * 8, depth + t * 8 + 8)
+def level_exchange_kernel(sums, out, beside, merged, arrived, replies, entering, passed, *sems):
+    pair_send, pair_recv, hub_send, hub_recv, back_send, back_recv, last_send, last_recv = sems
+    band = lax.axis_index("band")
+    chip, core = band // 2, band % 2
+    depth = out.shape[1] // 2
+    tail = 2 * depth
+    mine_first = core * 4
+
+    def other(step):
+        return lax.rem(chip + step, 4) * 2 + core
+
+    def remote(src, dst, send, recv, target):
+        return pltpu.make_async_remote_copy(
+            src_ref=src,
+            dst_ref=dst,
+            send_sem=send,
+            recv_sem=recv,
+            device_id={"band": target},
+            device_id_type=pl.DeviceIdType.MESH,
+        )
+
+    sibling = chip * 2 + (1 - core)
+    barrier = pltpu.get_barrier_semaphore()
+    for target in [sibling] + [other(step) for step in (1, 2, 3)]:
+        pl.semaphore_signal(
+            barrier, inc=1, device_id={"band": target}, device_id_type=pl.DeviceIdType.MESH
+        )
+    pl.semaphore_wait(barrier, 4)
+
+    pair = remote(
+        sums.at[pl.ds((1 - core) * 4, 4)], beside, pair_send.at[0], pair_recv.at[0], sibling
+    )
+    pair.start()
+    pair.wait_recv()
+
+    def lower(a, b):
+        return jnp.where(core == 0, a, b)
+
+    def row(ref, chunk, at):
+        return jnp.broadcast_to(ref[chunk, at : at + 1, :], (8, LANE))
+
+    def bands_of(chunk, at):
+        a, b = sums[mine_first + chunk, at, :], beside[chunk, at, :]
+        return lower(a, b), lower(b, a)
+
+    def coefficients(chunk):
+        both = []
+        for at in (tail, tail + 1):
+            a, b = row(sums, mine_first + chunk, at), row(beside, chunk, at)
+            both.append((lower(a, b), lower(b, a)))
+        return both
+
+    def merge(chunk):
+        (full0, full1), (both0, both1) = coefficients(chunk)
+
+        @pl.loop(0, depth // 8)
+        def _(t):
+            at = pl.ds(pl.multiple_of(t * 8, 8), 8)
+            later = pl.ds(pl.multiple_of(depth + t * 8, 8), 8)
+            up0, up1 = bands_of(chunk, at)
+            down0, down1 = bands_of(chunk, later)
+            merged[chunk, at, :] = full1 * up0 + up1
+            merged[chunk, later, :] = down0 + full0 * (down1 + both1 * up0)
+
+        index = lax.broadcasted_iota(jnp.int32, (8, LANE), 0)
+        full = full0 * full1
+        both = both0 + full0 * both1 * full0
+        merged[chunk, tail : tail + 8, :] = jnp.where(index == 0, full, both)
+
+    sends = []
+    for step in (1, 2, 3):
+        chunk = lax.rem(chip + step, 4)
+        merge(chunk)
+        copy = remote(
+            merged.at[chunk], arrived.at[chip], hub_send.at[step - 1], hub_recv.at[step - 1], other(step)
+        )
+        copy.start()
+        sends.append(copy)
+    merge(chip)
+    arrived[chip] = merged[chip]
+    for copy in sends:
+        copy.wait_recv()
+
+    full = [row(arrived, c, tail) for c in range(4)]
+    both = [row(arrived, c, tail + 1) for c in range(4)]
+
+    @pl.loop(0, depth // 8)
+    def _(t):
+        at = pl.ds(pl.multiple_of(t * 8, 8), 8)
+        later = pl.ds(pl.multiple_of(depth + t * 8, 8), 8)
         state = jnp.zeros((8, LANE), f32)
-        entering = []
-        for b in range(bands):
-            entering.append(state)
-            states[b, 0, at, :] = state
-            state = full[b] * state + sums[b, at, :]
+        ups = []
+        for c in range(4):
+            ups.append(state)
+            replies[c, at, :] = state
+            state = full[c] * state + arrived[c, at, :]
         state = jnp.zeros((8, LANE), f32)
-        for b in range(bands - 1, -1, -1):
-            states[b, 1, at, :] = state
-            state = full[b] * state + (sums[b, later, :] + both[b] * entering[b])
-
-
-def level_hub(sums):
+        for c in (3, 2, 1, 0):
+            replies[c, later, :] = state
+            state = full[c] * state + (arrived[c, later, :] + both[c] * ups[c])
+
+    backs = []
+    for step in (1, 2, 3):
+        copy = remote(
+            replies.at[lax.rem(chip + step, 4)],
+            entering.at[chip],
+            back_send.at[step - 1],
+            back_recv.at[step - 1],
+            other(step),
+        )
+        copy.start()
+        backs.append(copy)
+    entering[chip] = replies[chip]
+    for copy in backs:
+        copy.wait_recv()
+
+    for chunk in range(4):
+        (full0, full1), (both0, both1) = coefficients(chunk)
+
+        @pl.loop(0, depth // 8)
+        def _(t):
+            at = pl.ds(pl.multiple_of(t * 8, 8), 8)
+            later = pl.ds(pl.multiple_of(depth + t * 8, 8), 8)
+            up0, _ = bands_of(chunk, at)
+            _, down1 = bands_of(chunk, later)
+            first = entering[chunk, at, :]
+            last = entering[chunk, later, :]
+            middle = full0 * first + up0
+            turned = full1 * last + (down1 + both1 * middle)
+            out[mine_first + chunk, at, :] = lower(first, middle)
+            out[mine_first + chunk, later, :] = lower(turned, last)
+            passed[chunk, at, :] = lower(middle, first)
+            passed[chunk, later, :] = lower(last, turned)
+
+    final = remote(passed, out.at[pl.ds(mine_first, 4)], last_send.at[0], last_recv.at[0], sibling)
+    final.start()
+    pair.wait_send()
+    for copy in sends + backs:
+        copy.wait_send()
+    final.wait()
+
+
+def level_exchange(sums):
     bands, size, _ = sums.shape
+    depth = (size - 8) // 2
+    whole = pl.BlockSpec(memory_space=pltpu.VMEM)
+    dma = pltpu.SemaphoreType.DMA
     return pl.pallas_call(
-        level_hub_kernel,
-        out_shape=jax.ShapeDtypeStruct((bands, 2, (size - 8) // 2, LANE), f32),
-        in_specs=[pl.BlockSpec(memory_space=pltpu.VMEM)],
-        out_specs=pl.BlockSpec(memory_space=pltpu.VMEM),
-        compiler_params=vmem(60),
+        level_exchange_kernel,
+        out_shape=jax.ShapeDtypeStruct((bands, 2 * depth, LANE), f32),
+        in_specs=[whole],
+        out_specs=whole,
+        scratch_shapes=[
+            pltpu.VMEM((4, size, LANE), f32),
+            pltpu.VMEM((4, size, LANE), f32),
+            pltpu.VMEM((4, size, LANE), f32),
+            pltpu.VMEM((4, 2 * depth, LANE), f32),
+            pltpu.VMEM((4, 2 * depth, LANE), f32),
+            pltpu.VMEM((4, 2 * depth, LANE), f32),
+            dma((1,)),
+            dma((1,)),
+            dma((3,)),
+            dma((3,)),
+            dma((3,)),
+            dma((3,)),
+            dma((1,)),
+            dma((1,)),
+        ],
+        compiler_params=pltpu.CompilerParams(
+            vmem_limit_bytes=60 << 20, collective_id=0, has_side_effects=True
+        ),
         cost_estimate=cost(0, 3 << 20),
-        name="level_hub",
+        name="level_exchange",
     )(sums)
 
 
-def level_states_kernel(row_count, groups, variables, x, vert, states, out):
-    levels = groups // variables
-    for var in range(variables):
+def level_states_kernel(x, vert, states, out):
+    var = pl.program_id(0)
+    variables = pl.num_programs(0)
+    tiles, levels, row_count, _ = x.shape
+    decay = [vert[lev * variables + var] for lev in range(levels)]
+    for ct in range(tiles):
         for t in range(row_count // 8):
-            spots = [
-                slice((lev * variables + var) * row_count + t * 8, (lev * variables + var) * row_count + t * 8 + 8)
-                for lev in range(levels)
-            ]
-            rows = [x[spot, :] for spot in spots]
-            starts = [states[var, 0, k, 0, t * 8 : t * 8 + 8, :] for k in range(2)]
-            rows, _ = level_sweeps(rows, lambda lev: vert[lev * variables + var], starts)
+            at = slice(t * 8, t * 8 + 8)
+            rows = [x[ct, lev, at, :] for lev in range(levels)]
+            starts = [states[ct // (tiles // 2), k, ct % (tiles // 2), at, :] for k in range(2)]
+            rows, _ = level_sweeps(rows, lambda lev: decay[lev], starts)
             for lev in range(levels):
-                out[spots[lev], :] = rows[lev]
-
-
-def level_states(x, vert, states, row_count, groups, variables):
-    rows, columns = x.shape
+                out[lev, at, ct * LANE : (ct + 1) * LANE] = rows[lev]
+
+
+def level_states(x, vert, states, shape):
+    levels, variables, row_count, columns = shape
     tiles = columns // LANE
-    half = tiles // 2
-    block = pl.BlockSpec((rows, LANE), lambda i: (0, i))
     return pl.pallas_call(
-        functools.partial(level_states_kernel, row_count, groups, variables),
-        grid=(tiles,),
-        out_shape=jax.ShapeDtypeStruct(x.shape, f32),
+        level_states_kernel,
+        grid=(variables,),
+        out_shape=jax.ShapeDtypeStruct(shape, f32),
         in_specs=[
-            block,
+            pl.BlockSpec((tiles, levels, None, row_count, LANE), lambda i: (0, 0, i, 0, 0)),
             pl.BlockSpec(memory_space=pltpu.SMEM),
-            pl.BlockSpec(
-                (variables, 1, 2, 1, row_count, LANE),
-                lambda i: (0, i // half, 0, i % half, 0, 0),
-            ),
+            pl.BlockSpec((None, 2, 2, tiles // 2, row_count, LANE), lambda i: (i, 0, 0, 0, 0, 0)),
         ],
-        out_specs=block,
+        out_specs=pl.BlockSpec((levels, None, row_count, columns), lambda i: (0, i, 0, 0)),
         compiler_params=vmem(60),
         cost_estimate=cost(0, 11 << 20),
         name="level_states",
-    )(x, vert, states)
+    )(x.reshape(tiles, levels, variables, row_count, LANE), vert, states)
 
 
 def level_coefficients(decays):
@@ -603,20 +747,13 @@
     owners = obs_owner[:, 0]
     capacity = 2 * owners.shape[0] // sub_count
 
-    slots = route_slots(owners, sub_count, capacity)
+    ranks = route_ranks(owners, sub_count)
     row, column = obs_cell // lon_count, obs_cell % lon_count
     place = ((row // 4) * lon_count + column) * 4 + row % 4
-    packed, sent = pack(slots, place, obs_values, sub_count * capacity)
+    table = jnp.stack([owners, ranks, place] + [jnp.zeros_like(place)] * 5)
     lines = capacity // LANE
-    message = jnp.concatenate(
-        [
-            packed.reshape(sub_count, capacity // 4, LANE),
-            sent.astype(f32).reshape(sub_count, lines, LANE),
-            jnp.zeros((sub_count, 8 - lines, LANE), f32),
-        ],
-        axis=1,
-    )
-    got = lax.all_to_all(message, "sub", 0, 0, tiled=True)
+    message = pack(owners * capacity + ranks, table, obs_values, sub_count)
+    got = lax.all_to_all(message.reshape(sub_count, -1, LANE), "sub", 0, 0, tiled=True)
 
     vert_decay = jnp.exp(-1.0 / vert_length)
     coef = level_coefficients(vert_decay)
@@ -648,19 +785,13 @@
     smooth, sums = lat_states(
         low, high, decay, states.reshape(-1, LANE), vert_decay, coef, row_count, groups, var_count
     )
-    sums = lax.all_to_all(
-        sums.reshape(band_count, -1, LANE), "band", 0, 0, tiled=True
-    )
-    entering = lax.all_to_all(level_hub(sums), "band", 0, 0, tiled=True)
-    result = level_states(
+    entering = level_exchange(sums.reshape(band_count, -1, LANE))
+    return level_states(
         smooth,
         vert_decay,
         entering.reshape(var_count, 2, 2, tiles // 2, row_count, LANE),
-        row_count,
-        groups,
-        var_count,
+        background.shape,
     )
-    return result.reshape(background.shape)
 
 
 def solution(mesh):

time: 235 us -> 207 us (0.88)
  blocking collectives: 48.6 us -> 0 us
  Pallas kernels: 94.4 us -> 119 us
  other arithmetic: 15.4 us -> 12.3 us
    all_to_all x2 -> x0, blocking collectives: 48.6 us -> none  [the longest x1 26.9 us: per_device(): lax.all_to_all(sums.reshape(band_count, -1, LANE), 'band', 0, 0, tiled=True)]
    pallas_call x3, Pallas kernels: 22.8 us -> 46.8 us  [the longest x1 32.3 us: level_exchange(): pl.pallas_call(level_exchange_kernel, out_shape=jax.ShapeDtypeStruct((ban...]
    concatenate x1 -> x0, other arithmetic: 2.43 us -> none  [per_device(): jnp.concatenate([packed.reshape(sub_count, capacity // 4, LANE), sent.ast...]
    unnamed x20 -> x22, local copies, waits for them, and re-layouts: 5.34 us -> 5.34 us
  transfers between devices with their start and end apart: 3 -> 3, of which waited for: 2 -> 2; matrix products, arithmetic and copies ran while one was open for 6% -> 7% of each run, Pallas kernels for 9% -> 10%
where the time goes in v3:
time: 207 us; the launch traced here: 206 us
  Pallas kernels  119 us (57%)
  starting transfers between devices  29.8 us (14%)
  waiting for transfers between devices  26.6 us (13%)
  local copies, waits for them, and re-layouts  16.9 us (8%)
  other arithmetic  12.3 us (6%)
    pallas_call x1, Pallas kernels, force(): pl.pallas_call(functools.partial(forced_kernel, row_count, groups), grid=...  33.5 us
    pallas_call x1, Pallas kernels, level_exchange(): pl.pallas_call(level_exchange_kernel, out_shape=jax.ShapeDtypeStruct((ban...  32.3 us
    pallas_call x2, Pallas kernels, lon_filter(): pl.pallas_call(lon_kernel, grid=(steps,), out_shape=jax.ShapeDtypeStruct(...  21.3 us
    all_to_all x1, waiting for transfers between devices, per_device(): lax.all_to_all(message.reshape(sub_count, -1, LANE), 'sub', 0, 0, tiled=T...  19.7 us
    all_to_all x1, starting transfers between devices, per_device(): lax.all_to_all(message.reshape(sub_count, -1, LANE), 'sub', 0, 0, tiled=T...  12.1 us
    pallas_call x1, Pallas kernels, lat_states(): pl.pallas_call(functools.partial(lat_states_kernel, row_count, groups, va...  11.9 us
    all_to_all x1, starting transfers between devices, per_device(): lax.all_to_all(states.reshape(sub_count, 4 * tiles, LANE), 'sub', 0, 0, t...  8.99 us
    pallas_call x1, Pallas kernels, pack(): pl.pallas_call(pack_kernel, out_shape=jax.ShapeDtypeStruct((targets * 72,...  8.92 us
  transfers between devices with their start and end apart: 3, of which 2 were waited for; matrix products, arithmetic and copies ran while one was open for 7% of the time, Pallas kernels for 10%

profile of v3, /device:TPU:1, one launch (start us, length us, event | category | flops | bytes accessed | tf_op | source)
XLA Modules:
  0.0 205.6 jit_solution(2912716761729506606)
XLA Ops:
  0.0 0.8 broadcast_multiply_fusion.1
  0.8 0.9 convert_reduce_fusion
  1.8 1.1 fusion.7
  2.9 0.6 bitcast_add_fusion.slots
  3.5 0.8 fusion.24
  4.3 2.0 reshape.1419.values
  6.3 0.8 stack.17.table
  7.1 8.9 %pack.1 = f32[2304,128]{1,0:T(8,128)} custom-call(s32[4096]{0:T(1024)} %bitcast_add_fusion.slots, s32[8,4096]{1,0:T(8,128)} %stack.17.table, f32[32,4096]{1,0:T(8,128)} %reshape.1419.values), custom_call_target="tpu_custom_call" | custom-call | bytes 4194304 | tf_op jit(solution)/shard_map/pack/pallas_call | solution.py:90
  16.0 12.1 %all-to-all-start = ((f32[32,72,128]{2,1,0:T(8,128)}), f32[32,72,128]{2,1,0:T(8,128)}, u32[]{:S(2)}, u32[]{:S(2)}) async-start(f32[32,72,128]{2,1,0:T(8,128)} %bitcast.150), calls=%async_computation | async-start | bytes 2359296 | tf_op jit(solution)/shard_map/all_to_all | solution.py:756
  28.3 0.4 reshape.1422
  29.2 2.0 copy.29
  31.2 0.6 pad.23.decay
  31.9 0.1 fusion.17
  32.0 0.1 fusion.20
  32.2 0.1 fusion.11
  32.3 3.1 %reduce-precision_convert_fusion.2 = (bf16[32,128,128]{2,1,0:T(8,128)(2,1)S(1)}, bf16[32,128,128]{2,1,0:T(8,128)(2,1)S(1)}, f32[32,128,128]{2,1,0:T(8,128)}) fusion(pred[128,128]{1,0:T(8,128)(4,1)S(1)} %get-tuple-element.48, f32[32]{0:T(128)S(1)} %exponential-minus-one_negate_fusion, f32[32]{0:T(128)S(1)} %broadcast_in_dim_reshape.3, ...), kind=kLoop, calls=%fused_computation.11 | loop fusion | flops 7340032 | bytes 4489856 | tf_op jit(solution)/shard_map/convert_element_type | solution.py:282
  35.4 0.2 pad_maximum_fusion.1.mix
  35.8 0.2 add_multiply_fusion.1
  35.9 19.7 %all-to-all-done.got = f32[32,72,128]{2,1,0:T(8,128)} async-done(((f32[32,72,128]{2,1,0:T(8,128)}), f32[32,72,128]{2,1,0:T(8,128)}, u32[]{:S(2)}, u32[]{:S(2)}) %all-to-all-start) | async-done | bytes 1179680 | tf_op jit(solution)/shard_map/all_to_all | solution.py:756
  55.6 1.5 and_convert_fusion
  57.2 0.1 convert_element_type.84
  57.3 0.7 pad.20.quarters
  57.9 0.9 broadcast_in_dim.34.decay
  58.9 33.5 %force.1 = (f32[12,768,128]{2,1,0:T(8,128)}, f32[1536,128]{1,0:T(8,128)}) custom-call(s32[8192]{0:T(1024)} %bitcast.161, f32[32,72,128]{2,1,0:T(8,128)} %all-to-all-done.got, f32[32,8,64]{2,1,0:T(8,128)} %pad.20.quarters, f32[768,1536]{1,0:T(8,128)} %bitcast.151, f32[768,128]{1,0:T(8,128)} %broadcast_in_dim.34.decay), custom_call_target="tpu_custom_call" | custom-call | bytes 16777216 | tf_op jit(solution)/shard_map/force/pallas_call | solution.py:208
  92.4 8.7 %all-to-all-start.1 = ((f32[32,48,128]{2,1,0:T(8,128)}), f32[32,48,128]{2,1,0:T(8,128)}, u32[]{:S(2)}, u32[]{:S(2)}) async-start(f32[32,48,128]{2,1,0:T(8,128)} %bitcast.157), calls=%async_computation.1 | async-start | bytes 1572864 | tf_op jit(solution)/shard_map/all_to_all | solution.py:776
  101.1 0.7 constant_dynamic-slice_fusion.1.mix
  101.8 0.6 reduce-precision_convert_fusion.1
  102.4 0.3 pad_maximum_fusion.2.back
  102.7 0.7 constant_dynamic-slice_fusion.back
  103.4 1.2 copy-done.3
  104.6 1.1 copy-done.4
  105.8 1.0 reduce-precision_convert_fusion
  106.8 1.4 pad_maximum_fusion.first
  108.2 2.6 %copy-done = bf16[32,384,256]{2,1,0:T(8,128)(2,1)} copy-done((bf16[32,384,256]{2,1,0:T(8,128)(2,1)}, bf16[32,384,256]{2,1,0:T(8,128)(2,1)S(1)}, u32[]{:S(2)}) %copy-start) | copy-done | bytes 6291480
  110.9 0.7 constant_dynamic-slice_fusion.2.first
  111.6 10.7 %lon.2.low = f32[12,384,128]{2,1,0:T(8,128)} custom-call(f32[12,768,128]{2,1,0:T(8,128)} %get-tuple-element.17.x, bf16[32,384,256]{2,1,0:T(8,128)(2,1)} %copy-done, bf16[32,384,128]{2,1,0:T(8,128)(2,1)} %copy-done.1, bf16[32,384,128]{2,1,0:T(8,128)(2,1)} %copy-done.2), custom_call_target="tpu_custom_call" | custom-call | flops 1358954496 | bytes 31457280 | tf_op jit(solution)/shard_map/lon/pallas_call | solution.py:321
  122.2 5.0 %hub.1 = f32[1536,128]{1,0:T(8,128)} custom-call(f32[24,128]{1,0:T(8,128)} %pad.23.decay, f32[1536,128]{1,0:T(8,128)} %bitcast.18.moments, bf16[1,384,256]{2,1,0:T(8,128)(2,1)} %constant_dynamic-slice_fusion.2.first, bf16[1,384,128]{2,1,0:T(8,128)(2,1)} %constant_dynamic-slice_fusion.1.mix, bf16[1,384,128]{2,1,0:T(8,128)(2,1)} %constant_dynamic-slice_fusion.back), custom_call_target="tpu_custom_call" | custom-call | bytes 4194304 | tf_op jit(solution)/shard_map/hub/pallas_call | solution.py:419
  127.2 9.0 %all-to-all-start.2 = ((f32[32,48,128]{2,1,0:T(8,128)}), f32[32,48,128]{2,1,0:T(8,128)S(1)}, u32[]{:S(2)}, u32[]{:S(2)}) async-start(f32[32,48,128]{2,1,0:T(8,128)} %bitcast.155), calls=%async_computation.2 | async-start | bytes 1572864 | tf_op jit(solution)/shard_map/all_to_all | solution.py:783
  136.3 0.6 reshape.1427.vert
  136.9 0.3 slice_reduce_fusion.7
  137.2 0.1 copy.35
  137.3 10.7 %lon.3.high = f32[12,384,128]{2,1,0:T(8,128)} custom-call(f32[12,768,128]{2,1,0:T(8,128)} %get-tuple-element.17.x, bf16[32,384,256]{2,1,0:T(8,128)(2,1)} %copy-done, bf16[32,384,128]{2,1,0:T(8,128)(2,1)} %copy-done.1, bf16[32,384,128]{2,1,0:T(8,128)(2,1)} %copy-done.2), custom_call_target="tpu_custom_call" | custom-call | flops 1358954496 | bytes 31457280 | tf_op jit(solution)/shard_map/lon/pallas_call | solution.py:321
  148.0 6.9 %all-to-all-done.2 = f32[32,48,128]{2,1,0:T(8,128)S(1)} async-done(((f32[32,48,128]{2,1,0:T(8,128)}), f32[32,48,128]{2,1,0:T(8,128)S(1)}, u32[]{:S(2)}, u32[]{:S(2)}) %all-to-all-start.2) | async-done | bytes 786464 | tf_op jit(solution)/shard_map/all_to_all | solution.py:783
  154.9 0.8 broadcast_in_dim.42.coef
  155.7 0.1 copy-done.5
  155.8 11.9 %lat_states.1 = (f32[12,768,128]{2,1,0:T(8,128)}, f32[2368,128]{1,0:T(8,128)}) custom-call(f32[12,384,128]{2,1,0:T(8,128)} %lon.2.low, f32[12,384,128]{2,1,0:T(8,128)} %lon.3.high, f32[768,128]{1,0:T(8,128)} %broadcast_in_dim.34.decay, f32[1536,128]{1,0:T(8,128)} %bitcast.154, f32[32]{0:T(128)} %reshape.1427.vert, f32[4,8,128]{2,1,0:T(8,128)} %broadcast_in_dim.42.coef), custom_call_target="tpu_custom_call" | custom-call | bytes 12582912 | tf_op jit(solution)/shard_map/lat_states/pallas_call | solution.py:491
  167.7 32.3 %level_exchange.1 = f32[8,288,128]{2,1,0:T(8,128)} custom-call(f32[8,296,128]{2,1,0:T(8,128)} %bitcast.156), custom_call_target="tpu_custom_call" | custom-call | bytes 3145728 | tf_op jit(solution)/shard_map/level_exchange/pallas_call | solution.py:660
  200.0 5.6 %level_states.1 = f32[8,4,24,1536]{3,2,1,0:T(8,128)} custom-call(f32[12,8,4,24,128]{4,3,2,1,0:T(8,128)} %bitcast.152, f32[32]{0:T(128)} %reshape.1427.vert, f32[4,2,2,6,24,128]{5,4,3,2,1,0:T(8,128)} %bitcast.153), custom_call_target="tpu_custom_call" | custom-call | bytes 11534336 | tf_op jit(solution)/shard_map/level_states/pallas_call | solution.py:707
  (49 shorter events, 1.0 us)
Async XLA Ops:
  0.0 6.3 %copy-start.6 = (s32[4096,1]{0,1:T(1,128)S(1)}, s32[4096,1]{0,1:T(1,128)}, u32[]{:S(2)}) copy-start(s32[4096,1]{0,1:T(1,128)} %param.9) | copy-start | bytes 49156
  7.1 21.1 %copy-start.7 = (f32[8,4,768]{2,1,0:T(4,128)S(1)}, f32[8,4,768]{2,1,0:T(4,128)}, u32[]{:S(2)}) copy-start(f32[8,4,768]{2,1,0:T(4,128)} %param.11) | copy-start | bytes 294916
  16.0 12.7 %copy-start.8 = (f32[8,4]{0,1:T(4,128)S(1)}, f32[8,4]{0,1:T(4,128)}, u32[]{:S(2)}) copy-start(f32[8,4]{0,1:T(4,128)} %param.12) | copy-start | bytes 388
  16.0 39.6 %all-to-all-start = ((f32[32,72,128]{2,1,0:T(8,128)}), f32[32,72,128]{2,1,0:T(8,128)}, u32[]{:S(2)}, u32[]{:S(2)}) async-start(f32[32,72,128]{2,1,0:T(8,128)} %bitcast.150), calls=%async_computation | async-start | bytes 2359296 | tf_op jit(solution)/shard_map/all_to_all | solution.py:756
  35.7 65.4 %copy-start.1 = (bf16[32,384,128]{2,1,0:T(8,128)(2,1)}, bf16[32,384,128]{2,1,0:T(8,128)(2,1)S(1)}, u32[]{:S(2)}) copy-start(bf16[32,384,128]{2,1,0:T(8,128)(2,1)S(1)} %pad_maximum_fusion.1.mix) | copy-start | bytes 9437188
  92.4 29.8 %all-to-all-start.1 = ((f32[32,48,128]{2,1,0:T(8,128)}), f32[32,48,128]{2,1,0:T(8,128)}, u32[]{:S(2)}, u32[]{:S(2)}) async-start(f32[32,48,128]{2,1,0:T(8,128)} %bitcast.157), calls=%async_computation.1 | async-start | bytes 1572864 | tf_op jit(solution)/shard_map/all_to_all | solution.py:776
  102.4 2.3 %copy-start.3 = (f32[32,128,4]{2,1,0:T(8,128)S(1)}, f32[32,128,4]{2,1,0:T(8,128)}, u32[]{:S(2)}) copy-start(f32[32,128,4]{2,1,0:T(8,128)} %copy.29) | copy-start | bytes 196612
  102.4 3.4 %copy-start.4 = (f32[32,128,128]{2,1,0:T(8,128)S(1)}, f32[32,128,128]{2,1,0:T(8,128)}, u32[]{:S(2)}) copy-start(f32[32,128,128]{2,1,0:T(8,128)} %get-tuple-element.53) | copy-start | bytes 6291460
  102.7 4.1 %copy-start.2 = (bf16[32,384,128]{2,1,0:T(8,128)(2,1)}, bf16[32,384,128]{2,1,0:T(8,128)(2,1)S(1)}, u32[]{:S(2)}) copy-start(bf16[32,384,128]{2,1,0:T(8,128)(2,1)S(1)} %pad_maximum_fusion.2.back) | copy-start | bytes 9437188
  108.2 2.7 %copy-start = (bf16[32,384,256]{2,1,0:T(8,128)(2,1)}, bf16[32,384,256]{2,1,0:T(8,128)(2,1)S(1)}, u32[]{:S(2)}) copy-start(bf16[32,384,256]{2,1,0:T(8,128)(2,1)S(1)} %pad_maximum_fusion.first) | copy-start | bytes 18874372
  122.2 14.0 %copy-start.9 = (f32[8,4]{0,1:T(4,128)S(1)}, f32[8,4]{0,1:T(4,128)}, u32[]{:S(2)}) copy-start(f32[8,4]{0,1:T(4,128)} %param.13) | copy-start | bytes 388
  127.2 27.7 %all-to-all-start.2 = ((f32[32,48,128]{2,1,0:T(8,128)}), f32[32,48,128]{2,1,0:T(8,128)S(1)}, u32[]{:S(2)}, u32[]{:S(2)}) async-start(f32[32,48,128]{2,1,0:T(8,128)} %bitcast.155), calls=%async_computation.2 | async-start | bytes 1572864 | tf_op jit(solution)/shard_map/all_to_all | solution.py:783
  154.9 0.9 copy-start.5

commit v4 on v3

--- a/solution.py
+++ b/solution.py
@@ -35,7 +35,7 @@
 
 
 def pack_kernel(slots, table, values, packed, rows, big):
-    count = values.shape[1]
+    levels, _, count = values.shape
     total = big.shape[0]
     targets = total // 256
     size = packed.shape[0] // targets
@@ -45,7 +45,9 @@
         big[pl.ds(pl.multiple_of(i * 64, 64), 64), :] = jnp.zeros((64, LANE), f32)
 
     for j in range(count // LANE):
-        part = values[:, j * LANE : (j + 1) * LANE]
+        part = jnp.concatenate(
+            [values[lev, :, j * LANE : (j + 1) * LANE] for lev in range(levels)], axis=0
+        )
         rows[j * LANE : (j + 1) * LANE, :] = jnp.concatenate([part] * 4, axis=0).T
 
     owner, rank, place = table[0:1, :], table[1:2, :], table[2:3, :]
@@ -84,7 +86,7 @@
 
 
 def pack(slots, table, values, targets):
-    count = values.shape[1]
+    count = values.shape[2]
     total = targets * 256
     whole = pl.BlockSpec(memory_space=pltpu.VMEM)
     return pl.pallas_call(
@@ -99,80 +101,103 @@
     )(slots, table, values)
 
 
-def lat_sweeps(rows, decay, starts):
-    count = len(rows)
-    ends = []
+def lat_sweeps(sets, decays, starts):
+    count = len(sets[0])
+    ends = [[] for _ in sets]
     for sweep in range(4):
         order = range(count) if sweep % 2 == 0 else range(count - 1, -1, -1)
-        state = starts[sweep]
-        out = [None] * count
+        states = [start[sweep] for start in starts]
+        outs = [[None] * count for _ in sets]
         for r in order:
-            state = rows[r] + decay(r) * (state - rows[r])
-            out[r] = state
-        ends.append(state)
-        rows = out
-    return rows, ends
+            for i, rows in enumerate(sets):
+                a, rest = decays[i](r)
+                states[i] = a * states[i] + rest * rows[r]
+                outs[i][r] = states[i]
+        for i in range(len(sets)):
+            ends[i].append(states[i])
+        sets = outs
+    return sets, ends
+
+
+def decay_of_octet(decay, groups, o):
+    rows = decay.shape[0] // 2
+
+    def pair(r):
+        at = r * groups + o * 8
+        return decay[at : at + 8, :], decay[rows + at : rows + at + 8, :]
+
+    return pair
 
 
 CHAINS = 8
-
-
-def forced_kernel(row_count, groups, places, got, quarters, background, decay, forced, moments, spread, *chains):
-    step_id = pl.program_id(0)
+SIDE = 1
+
+
+def forced_kernel(row_count, groups, places, got, quarters, background, decay, forced, moments, spread, field, sem, out_sem, *chains):
     total = spread.shape[0]
     depth = chains[0].shape[0]
     sources = got.shape[0]
-
-    @pl.when(step_id == 0)
-    def _():
-        @pl.loop(0, depth // 64)
-        def _(i):
-            at = pl.ds(pl.multiple_of(i * 64, 64), 64)
-            for chain in chains:
-                chain[at, :] = jnp.zeros((64, LANE), f32)
-
-        lane = lax.broadcasted_iota(jnp.int32, (8, LANE), 1) // 32
-        pick = (lane == lax.broadcasted_iota(jnp.int32, (8, LANE), 0)).astype(bf16)
-        quarter = lax.broadcasted_iota(jnp.int32, (64, LANE), 1) // 32
-        wanted = quarter.astype(f32)
-
-        def turns(x):
-            return [x] + [pltpu.roll(x, 32 * k, 1) for k in range(1, 4)]
-
-        def repeat(turned, k):
-            out = turned[(3 - k) % 4]
-            for q in range(3):
-                out = jnp.where(quarter == q, turned[(q - k) % 4], out)
-            return out
-
-        @pl.loop(0, sources)
-        def _(d):
-            part = turns(got[d, :64, :])
-            mark = turns(
-                lax.dot_general(
-                    quarters[d].astype(bf16), pick, (((0,), (0,)), ((), ())), preferred_element_type=f32
-                )
+    tiles = forced.shape[0]
+    fetches = [
+        pltpu.make_async_copy(
+            background.at[:, ct * LANE : (ct + 1) * LANE], field.at[ct], sem.at[ct]
+        )
+        for ct in range(tiles)
+    ]
+    for fetch in fetches:
+        fetch.start()
+
+    @pl.loop(0, depth // 64)
+    def _(i):
+        at = pl.ds(pl.multiple_of(i * 64, 64), 64)
+        for chain in chains:
+            chain[at, :] = jnp.zeros((64, LANE), f32)
+
+    lane = lax.broadcasted_iota(jnp.int32, (8, LANE), 1) // 32
+    pick = (lane == lax.broadcasted_iota(jnp.int32, (8, LANE), 0)).astype(bf16)
+    quarter = lax.broadcasted_iota(jnp.int32, (64, LANE), 1) // 32
+    wanted = quarter.astype(f32)
+
+    def turns(x):
+        return [x] + [pltpu.roll(x, 32 * k, 1) for k in range(1, 4)]
+
+    def repeat(turned, k):
+        out = turned[(3 - k) % 4]
+        for q in range(3):
+            out = jnp.where(quarter == q, turned[(q - k) % 4], out)
+        return out
+
+    @pl.loop(0, sources)
+    def _(d):
+        part = turns(got[d, :64, :])
+        mark = turns(
+            lax.dot_general(
+                quarters[d].astype(bf16), pick, (((0,), (0,)), ((), ())), preferred_element_type=f32
             )
-            for k in range(4):
-                one = jnp.where(repeat(mark, k) == wanted, repeat(part, k), 0.0)
-                spread[pl.ds(pl.multiple_of(d * 256 + k * 64, 64), 64), :] = one
-
-        step = 4
-
-        @pl.loop(0, total // (CHAINS * step))
-        def _(i):
-            for u in range(step):
-                spots = [(i * step + u) * CHAINS + c for c in range(CHAINS)]
-                where = [pl.ds(places[j], 1) for j in spots]
-                adds = [spread[pl.ds(j, 1), :] for j in spots]
-                olds = [chains[c][where[c], :] for c in range(CHAINS)]
-                for c in range(CHAINS):
-                    chains[c][where[c], :] = olds[c] + adds[c]
-
-    @pl.when(step_id > 0)
-    def _():
-        ct = step_id - 1
-        columns = depth // (row_count // 4)
+        )
+        for k in range(4):
+            one = jnp.where(repeat(mark, k) == wanted, repeat(part, k), 0.0)
+            spread[pl.ds(pl.multiple_of(d * 256 + k * 64, 64), 64), :] = one
+
+    step = 4
+
+    @pl.loop(0, total // (CHAINS * step))
+    def _(i):
+        for u in range(step):
+            spots = [(i * step + u) * CHAINS + c for c in range(CHAINS)]
+            where = [pl.ds(places[j], 1) for j in spots]
+            adds = [spread[pl.ds(j, 1), :] for j in spots]
+            olds = [chains[c][where[c], :] for c in range(CHAINS)]
+            for c in range(CHAINS):
+                chains[c][where[c], :] = olds[c] + adds[c]
+
+    for fetch in fetches:
+        fetch.wait()
+    columns = depth // (row_count // 4)
+
+    @pl.loop(0, tiles)
+    def _(ct):
+        out = field.at[ct]
         for rr in range(row_count // 4):
             at = pl.ds(pl.multiple_of(rr * columns + ct * LANE, LANE), LANE)
             parts = [chain[at, :] for chain in chains]
@@ -183,20 +208,29 @@
                 for o in range(groups // 8):
                     at = pl.ds(o * 8 * row_count + rr * 4 + q, 8, stride=row_count)
                     first = q * groups + o * 8
-                    forced[at, :] = background[at, :] + turned[first : first + 8, :]
+                    out[at, :] = out[at, :] + turned[first : first + 8, :]
+        pltpu.make_async_copy(field.at[ct], forced.at[ct], out_sem.at[ct]).start()
         zero = jnp.zeros((8, LANE), f32)
         per_group = moments.shape[0] // groups
-        for o in range(groups // 8):
-            rows = [
-                forced[pl.ds(o * 8 * row_count + r, 8, stride=row_count), :]
-                for r in range(row_count)
+        for first in range(0, groups // 8, SIDE):
+            octets = range(first, first + SIDE)
+            sets = [
+                [
+                    out[pl.ds(o * 8 * row_count + r, 8, stride=row_count), :]
+                    for r in range(row_count)
+                ]
+                for o in octets
             ]
             _, ends = lat_sweeps(
-                rows, lambda r: decay[r * groups + o * 8 : r * groups + o * 8 + 8, :], [zero] * 4
+                sets, [decay_of_octet(decay, groups, o) for o in octets], [[zero] * 4] * SIDE
             )
-            for k in range(4):
-                start = o * 8 * per_group + k * (per_group // 4) + ct
-                moments[pl.ds(start, 8, stride=per_group), :] = ends[k]
+            for i, o in enumerate(octets):
+                for k in range(4):
+                    start = o * 8 * per_group + k * (per_group // 4) + ct
+                    moments[pl.ds(start, 8, stride=per_group), :] = ends[i][k]
+
+    for ct in range(tiles):
+        pltpu.make_async_copy(field.at[ct], forced.at[ct], out_sem.at[ct]).wait()
 
 
 def force(places, got, quarters, background, decay, row_count, groups):
@@ -204,27 +238,29 @@
     tiles = columns // LANE
     total = places.shape[0]
     depth = rows * columns // LANE
-    block = pl.BlockSpec((rows, LANE), lambda i: (0, jnp.maximum(i - 1, 0)))
+    whole = pl.BlockSpec(memory_space=pltpu.VMEM)
     return pl.pallas_call(
         functools.partial(forced_kernel, row_count, groups),
-        grid=(tiles + 1,),
         out_shape=(
             jax.ShapeDtypeStruct((tiles, rows, LANE), f32),
             jax.ShapeDtypeStruct((groups * 4 * tiles, LANE), f32),
         ),
         in_specs=[
             pl.BlockSpec(memory_space=pltpu.SMEM),
-            pl.BlockSpec(got.shape, lambda i: (0, 0, 0), pipeline_mode=pl.Buffered(1)),
-            pl.BlockSpec(quarters.shape, lambda i: (0, 0, 0), pipeline_mode=pl.Buffered(1)),
-            block,
-            pl.BlockSpec((rows, LANE), lambda i: (0, 0), pipeline_mode=pl.Buffered(1)),
+            whole,
+            whole,
+            pl.BlockSpec(memory_space=pl.ANY),
+            whole,
         ],
-        out_specs=(
-            pl.BlockSpec((None, rows, LANE), lambda i: (jnp.maximum(i - 1, 0), 0, 0)),
-            pl.BlockSpec((groups * 4 * tiles, LANE), lambda i: (0, 0)),
-        ),
-        scratch_shapes=[pltpu.VMEM((total, LANE), f32)] + [pltpu.VMEM((depth, LANE), f32)] * CHAINS,
-        compiler_params=vmem(60),
+        out_specs=(pl.BlockSpec(memory_space=pl.ANY), whole),
+        scratch_shapes=[
+            pltpu.VMEM((total, LANE), f32),
+            pltpu.VMEM((tiles, rows, LANE), f32),
+            pltpu.SemaphoreType.DMA((tiles,)),
+            pltpu.SemaphoreType.DMA((tiles,)),
+        ]
+        + [pltpu.VMEM((depth, LANE), f32)] * CHAINS,
+        compiler_params=vmem(58),
         cost_estimate=cost(0, 16 << 20),
         name="force",
     )(places, got, quarters, background, decay)
@@ -304,30 +340,68 @@
     return [out[b * count : (b + 1) * count] for b in range(blocks)]
 
 
-def lon_kernel(x, first, mix, back, out):
-    tiles = x.shape[0]
-    count = x.shape[1] // first.shape[0]
-    for g in range(first.shape[0]):
-        at = slice(g * count, (g + 1) * count)
-        done = lon_apply([x[b, at, :] for b in range(tiles)], first[g], mix[g], back[g])
-        for b in range(tiles):
-            out[b, at, :] = done[b]
+LON_STEP = 4
+
+
+def lon_kernel(count, first_group, x, first, mix, back, out, xs, ws, ms, bs, done, sems, out_sem):
+    tiles, rows, _ = out.shape
+    steps = rows // count // LON_STEP
+    size = LON_STEP * count
+
+    def fetches(i):
+        group = first_group + i * LON_STEP
+        source = pl.ds(pl.multiple_of(group * count, 8), size)
+        target = pl.ds(pl.multiple_of(i * size, 8), size)
+        inside = pl.ds(i * LON_STEP, LON_STEP)
+        outside = pl.ds(group, LON_STEP)
+        return [
+            pltpu.make_async_copy(x.at[:, source], xs.at[:, target], sems.at[0, i]),
+            pltpu.make_async_copy(first.at[outside], ws.at[inside], sems.at[1, i]),
+            pltpu.make_async_copy(mix.at[outside], ms.at[inside], sems.at[2, i]),
+            pltpu.make_async_copy(back.at[outside], bs.at[inside], sems.at[3, i]),
+        ]
+
+    def write(i):
+        at = pl.ds(pl.multiple_of(i * size, 8), size)
+        return pltpu.make_async_copy(done.at[:, at], out.at[:, at], out_sem.at[i])
+
+    for i in range(steps):
+        for fetch in fetches(i):
+            fetch.start()
+
+    @pl.loop(0, steps)
+    def _(i):
+        for fetch in fetches(i):
+            fetch.wait()
+        for u in range(LON_STEP):
+            g = i * LON_STEP + u
+            at = pl.ds(pl.multiple_of(g * count, 8), count)
+            parts = lon_apply([xs[b, at, :] for b in range(tiles)], ws[g], ms[g], bs[g])
+            for b in range(tiles):
+                done[b, at, :] = parts[b]
+        write(i).start()
+
+    for i in range(steps):
+        write(i).wait()
 
 
 def lon_filter(x, weights, row_count, half):
     tiles, rows, _ = x.shape
-    per_step = 4
-    steps = rows // row_count // per_step // 2
+    groups = rows // row_count // 2
+    steps = groups // LON_STEP
+    any_space = pl.BlockSpec(memory_space=pl.ANY)
     return pl.pallas_call(
-        lon_kernel,
-        grid=(steps,),
+        functools.partial(lon_kernel, row_count, half * groups),
         out_shape=jax.ShapeDtypeStruct((tiles, rows // 2, LANE), f32),
-        in_specs=[pl.BlockSpec((tiles, per_step * row_count, LANE), lambda i: (0, i + half * steps, 0))]
+        in_specs=[any_space] * 4,
+        out_specs=any_space,
+        scratch_shapes=[pltpu.VMEM((tiles, rows // 2, LANE), f32)]
+        + [pltpu.VMEM((groups,) + w.shape[1:], w.dtype) for w in weights]
         + [
-            pl.BlockSpec((per_step,) + w.shape[1:], lambda i: (i + half * steps, 0, 0))
-            for w in weights
+            pltpu.VMEM((tiles, rows // 2, LANE), f32),
+            pltpu.SemaphoreType.DMA((4, steps)),
+            pltpu.SemaphoreType.DMA((steps,)),
         ],
-        out_specs=pl.BlockSpec((tiles, per_step * row_count, LANE), lambda i: (0, i, 0)),
         compiler_params=vmem(60),
         cost_estimate=cost(3 * rows * tiles * LANE * 3 * LANE, 30 << 20),
         name="lon",
@@ -436,74 +510,98 @@
         state = starts[sweep]
         out = [None] * count
         for r in order:
-            state = rows[r] + decay(r) * (state - rows[r])
+            state = decay(r) * state + (1.0 - decay(r)) * rows[r]
             out[r] = state
         ends.append(state)
         rows = out
     return rows, ends
 
 
-def lat_states_kernel(row_count, groups, variables, low, high, decay, states, vert, coef, out, sums):
-    ct = pl.program_id(0)
+def lat_states_kernel(row_count, groups, variables, low, high, decay, states, vert, coef, out, sums, field, sems, out_sem):
+    tiles = out.shape[0]
     per_group = states.shape[0] // groups
-    half = low.shape[0]
-    for o in range(groups // 8):
-        base = o * 8 * row_count
-        x, first = (low, base) if base < half else (high, base - half)
-        rows = [x[pl.ds(first + r, 8, stride=row_count), :] for r in range(row_count)]
-        starts = [
-            states[pl.ds(o * 8 * per_group + k * (per_group // 4) + ct, 8, stride=per_group), :]
-            for k in range(4)
+    half = low.shape[1]
+    levels = groups // variables
+    depth = tiles // 2 * row_count
+    size = sums.shape[0] // (2 * variables)
+
+    def fetches(ct):
+        return [
+            pltpu.make_async_copy(low.at[ct], field.at[ct, :half], sems.at[0, ct]),
+            pltpu.make_async_copy(high.at[ct], field.at[ct, half:], sems.at[1, ct]),
         ]
-        rows, _ = lat_sweeps(
-            rows, lambda r: decay[r * groups + o * 8 : r * groups + o * 8 + 8, :], starts
-        )
-        for r in range(row_count):
-            out[pl.ds(base + r, 8, stride=row_count), :] = rows[r]
-    zero = jnp.zeros((8, LANE), f32)
-    levels = groups // variables
-    halves = pl.num_programs(0) // 2
-    depth = halves * row_count
-    size = sums.shape[0] // (2 * variables)
-    for var in range(variables):
-        for t in range(row_count // 8):
-            rows = []
-            for lev in range(levels):
-                base = (lev * variables + var) * row_count + t * 8
-                rows.append(out[base : base + 8, :])
-            _, ends = level_sweeps(rows, lambda lev: vert[lev * variables + var], [zero, zero])
-            for k in range(2):
-                start = (var * 2 + ct // halves) * size + k * depth + (ct % halves) * row_count + t * 8
-                sums[pl.ds(pl.multiple_of(start, 8), 8), :] = ends[k]
-
-    @pl.when(ct == 0)
-    def _():
-        for target in range(2 * variables):
-            start = target * size + 2 * depth
-            sums[start : start + 8, :] = coef[target // 2]
+
+    for ct in range(tiles):
+        for fetch in fetches(ct):
+            fetch.start()
+
+    @pl.loop(0, tiles)
+    def _(ct):
+        for fetch in fetches(ct):
+            fetch.wait()
+        done = field.at[ct]
+        for first in range(0, groups // 8, SIDE):
+            octets = range(first, first + SIDE)
+            sets = [
+                [
+                    done[pl.ds(o * 8 * row_count + r, 8, stride=row_count), :]
+                    for r in range(row_count)
+                ]
+                for o in octets
+            ]
+            starts = [
+                [
+                    states[
+                        pl.ds(o * 8 * per_group + k * (per_group // 4) + ct, 8, stride=per_group), :
+                    ]
+                    for k in range(4)
+                ]
+                for o in octets
+            ]
+            sets, _ = lat_sweeps(sets, [decay_of_octet(decay, groups, o) for o in octets], starts)
+            for i, o in enumerate(octets):
+                for r in range(row_count):
+                    done[pl.ds(o * 8 * row_count + r, 8, stride=row_count), :] = sets[i][r]
+        pltpu.make_async_copy(done, out.at[ct], out_sem.at[ct]).start()
+        zero = jnp.zeros((8, LANE), f32)
+        side = lax.div(ct, tiles // 2)
+        spot = lax.rem(ct, tiles // 2)
+        for var in range(variables):
+            for t in range(row_count // 8):
+                rows = []
+                for lev in range(levels):
+                    base = (lev * variables + var) * row_count + t * 8
+                    rows.append(done[base : base + 8, :])
+                _, ends = level_sweeps(rows, lambda lev: vert[lev * variables + var], [zero, zero])
+                for k in range(2):
+                    start = (var * 2 + side) * size + k * depth + spot * row_count + t * 8
+                    sums[pl.ds(pl.multiple_of(start, 8), 8), :] = ends[k]
+
+    for target in range(2 * variables):
+        start = target * size + 2 * depth
+        sums[start : start + 8, :] = coef[target // 2]
+    for ct in range(tiles):
+        pltpu.make_async_copy(field.at[ct], out.at[ct], out_sem.at[ct]).wait()
 
 
 def lat_states(low, high, decay, states, vert, coef, row_count, groups, variables):
     tiles, rows = low.shape[0], 2 * low.shape[1]
-    part = pl.BlockSpec((None, rows // 2, LANE), lambda i: (i, 0, 0))
-    block = pl.BlockSpec((None, rows, LANE), lambda i: (i, 0, 0))
     size = 2 * variables * (tiles * row_count + 8)
+    whole = pl.BlockSpec(memory_space=pltpu.VMEM)
+    any_space = pl.BlockSpec(memory_space=pl.ANY)
     return pl.pallas_call(
         functools.partial(lat_states_kernel, row_count, groups, variables),
-        grid=(tiles,),
         out_shape=(
             jax.ShapeDtypeStruct((tiles, rows, LANE), f32),
             jax.ShapeDtypeStruct((size, LANE), f32),
         ),
-        in_specs=[
-            part,
-            part,
-            pl.BlockSpec((rows, LANE), lambda i: (0, 0)),
-            pl.BlockSpec(states.shape, lambda i: (0, 0)),
-            pl.BlockSpec(memory_space=pltpu.SMEM),
-            pl.BlockSpec(coef.shape, lambda i: (0, 0, 0)),
+        in_specs=[any_space, any_space, whole, whole, pl.BlockSpec(memory_space=pltpu.SMEM), whole],
+        out_specs=(any_space, whole),
+        scratch_shapes=[
+            pltpu.VMEM((tiles, rows, LANE), f32),
+            pltpu.SemaphoreType.DMA((2, tiles)),
+            pltpu.SemaphoreType.DMA((tiles,)),
         ],
-        out_specs=(block, pl.BlockSpec((size, LANE), lambda i: (0, 0))),
         compiler_params=vmem(60),
         cost_estimate=cost(0, 12 << 20),
         name="lat_states",
@@ -686,34 +784,48 @@
     )(sums)
 
 
-def level_states_kernel(x, vert, states, out):
-    var = pl.program_id(0)
-    variables = pl.num_programs(0)
-    tiles, levels, row_count, _ = x.shape
-    decay = [vert[lev * variables + var] for lev in range(levels)]
-    for ct in range(tiles):
-        for t in range(row_count // 8):
-            at = slice(t * 8, t * 8 + 8)
-            rows = [x[ct, lev, at, :] for lev in range(levels)]
-            starts = [states[ct // (tiles // 2), k, ct % (tiles // 2), at, :] for k in range(2)]
-            rows, _ = level_sweeps(rows, lambda lev: decay[lev], starts)
-            for lev in range(levels):
-                out[lev, at, ct * LANE : (ct + 1) * LANE] = rows[lev]
+def level_states_kernel(source, vert, states, out, x, result, in_sem, sem):
+    tiles, levels, variables, row_count, _ = x.shape
+    fetches = [
+        pltpu.make_async_copy(source.at[:, :, var], x.at[:, :, var], in_sem.at[var])
+        for var in range(variables)
+    ]
+    for fetch in fetches:
+        fetch.start()
+    writes = []
+    for var in range(variables):
+        fetches[var].wait()
+        decay = [vert[lev * variables + var] for lev in range(levels)]
+        for ct in range(tiles):
+            for t in range(row_count // 8):
+                at = slice(t * 8, t * 8 + 8)
+                rows = [x[ct, lev, var, at, :] for lev in range(levels)]
+                starts = [states[var, ct // (tiles // 2), k, ct % (tiles // 2), at, :] for k in range(2)]
+                rows, _ = level_sweeps(rows, lambda lev: decay[lev], starts)
+                for lev in range(levels):
+                    result[lev, var, at, ct * LANE : (ct + 1) * LANE] = rows[lev]
+        write = pltpu.make_async_copy(result.at[:, var], out.at[:, var], sem.at[var])
+        write.start()
+        writes.append(write)
+    for write in writes:
+        write.wait()
 
 
 def level_states(x, vert, states, shape):
     levels, variables, row_count, columns = shape
     tiles = columns // LANE
+    whole = pl.BlockSpec(memory_space=pltpu.VMEM)
     return pl.pallas_call(
         level_states_kernel,
-        grid=(variables,),
         out_shape=jax.ShapeDtypeStruct(shape, f32),
-        in_specs=[
-            pl.BlockSpec((tiles, levels, None, row_count, LANE), lambda i: (0, 0, i, 0, 0)),
-            pl.BlockSpec(memory_space=pltpu.SMEM),
-            pl.BlockSpec((None, 2, 2, tiles // 2, row_count, LANE), lambda i: (i, 0, 0, 0, 0, 0)),
+        in_specs=[pl.BlockSpec(memory_space=pl.ANY), pl.BlockSpec(memory_space=pltpu.SMEM), whole],
+        out_specs=pl.BlockSpec(memory_space=pl.ANY),
+        scratch_shapes=[
+            pltpu.VMEM((tiles, levels, variables, row_count, LANE), f32),
+            pltpu.VMEM(shape, f32),
+            pltpu.SemaphoreType.DMA((variables,)),
+            pltpu.SemaphoreType.DMA((variables,)),
         ],
-        out_specs=pl.BlockSpec((levels, None, row_count, columns), lambda i: (0, i, 0, 0)),
         compiler_params=vmem(60),
         cost_estimate=cost(0, 11 << 20),
         name="level_states",
@@ -743,7 +855,6 @@
     groups = level_count * var_count
     tiles = lon_count // LANE
     tile_field = background.reshape(groups * row_count, lon_count)
-    obs_values = obs_columns.reshape(groups, -1)
     owners = obs_owner[:, 0]
     capacity = 2 * owners.shape[0] // sub_count
 
@@ -752,7 +863,7 @@
     place = ((row // 4) * lon_count + column) * 4 + row % 4
     table = jnp.stack([owners, ranks, place] + [jnp.zeros_like(place)] * 5)
     lines = capacity // LANE
-    message = pack(owners * capacity + ranks, table, obs_values, sub_count)
+    message = pack(owners * capacity + ranks, table, obs_columns, sub_count)
     got = lax.all_to_all(message.reshape(sub_count, -1, LANE), "sub", 0, 0, tiled=True)
 
     vert_decay = jnp.exp(-1.0 / vert_length)
@@ -761,7 +872,9 @@
 
     lat_all = jnp.exp(-1.0 / lat_length).reshape(groups, sub_count, row_count)
     own_lat = lax.dynamic_index_in_dim(lat_all, sub_index, 1, False)
-    decay = jnp.broadcast_to(own_lat.T.reshape(row_count * groups, 1), (row_count * groups, LANE))
+    own_lat = own_lat.T.reshape(row_count * groups, 1)
+    own_lat = jnp.concatenate([own_lat, 1.0 - own_lat])
+    decay = jnp.broadcast_to(own_lat, (2 * row_count * groups, LANE))
     hub_lat = lax.dynamic_index_in_dim(lat_all, sub_index, 0, False)
     hub_lat = jnp.pad(hub_lat.T, ((0, 0), (0, LANE - sub_count)))
 
@@ -769,6 +882,7 @@
     weights = lon_weights(lengths, lon_count)
     own_weights = [lax.dynamic_slice_in_dim(w, sub_index, 1, 0) for w in weights]
 
+    got, weights = lax.optimization_barrier((got, weights))
     places = got[:, capacity // 4 : capacity // 4 + lines, :].reshape(-1).astype(jnp.int32)
     quarters = (places & 3).astype(f32).reshape(sub_count, 4, capacity // 4)
     quarters = jnp.pad(quarters, ((0, 0), (0, 4), (0, 0)))

time: 207 us -> 196 us (0.947)
  Pallas kernels: 119 us -> 110 us
  waiting for transfers between devices: 26.6 us -> 19.9 us
  other arithmetic: 12.3 us -> 18.9 us
  local copies, waits for them, and re-layouts: 16.9 us -> 14.6 us
    all_to_all x1, waiting for transfers between devices: 19.7 us -> 9.1 us  [per_device(): lax.all_to_all(message.reshape(sub_count, -1, LANE), 'sub', 0, 0, tiled=T...]
    concatenate x3, other arithmetic: 1.97 us -> 8.18 us  [thirds(): return jnp.concatenate([high, high, low], axis=1)]
    pallas_call x4, Pallas kernels: 60.4 us -> 55.5 us  [the longest x1 28.9 us: force(): pl.pallas_call(functools.partial(forced_kernel, row_count, groups), out_s...]
    unnamed x22 -> x16, local copies, waits for them, and re-layouts: 5.34 us -> 1.49 us
    all_to_all x1, waiting for transfers between devices: 0.01 us -> 2.89 us  [per_device(): lax.all_to_all(moments.reshape(sub_count, 4 * tiles, LANE), 'sub', 0, 0,...]
    pallas_call x1, Pallas kernels: 11.9 us -> 9.24 us  [lat_states(): pl.pallas_call(functools.partial(lat_states_kernel, row_count, groups, va...]
  transfers between devices with their start and end apart: 3 -> 3, of which waited for: 2 -> 3; matrix products, arithmetic and copies ran while one was open for 7% -> 12% of each run, Pallas kernels for 10% -> 11%
where the time goes in v4:
time: 196 us; the launch traced here: 195 us
  Pallas kernels  110 us (56%)
  starting transfers between devices  30.2 us (15%)
  waiting for transfers between devices  19.9 us (10%)
  other arithmetic  18.9 us (10%)
  local copies, waits for them, and re-layouts  14.6 us (7%)
    pallas_call x1, Pallas kernels, level_exchange(): pl.pallas_call(level_exchange_kernel, out_shape=jax.ShapeDtypeStruct((ban...  31.5 us
    pallas_call x1, Pallas kernels, force(): pl.pallas_call(functools.partial(forced_kernel, row_count, groups), out_s...  28.9 us
    pallas_call x2, Pallas kernels, lon_filter(): pl.pallas_call(functools.partial(lon_kernel, row_count, half * groups), o...  21.5 us
    all_to_all x1, starting transfers between devices, per_device(): lax.all_to_all(message.reshape(sub_count, -1, LANE), 'sub', 0, 0, tiled=T...  12.1 us
    all_to_all x1, starting transfers between devices, per_device(): lax.all_to_all(moments.reshape(sub_count, 4 * tiles, LANE), 'sub', 0, 0,...  9.45 us
    pallas_call x1, Pallas kernels, lat_states(): pl.pallas_call(functools.partial(lat_states_kernel, row_count, groups, va...  9.24 us
    all_to_all x1, waiting for transfers between devices, per_device(): lax.all_to_all(message.reshape(sub_count, -1, LANE), 'sub', 0, 0, tiled=T...  9.1 us
    pallas_call x1, Pallas kernels, pack(): pl.pallas_call(pack_kernel, out_shape=jax.ShapeDtypeStruct((targets * 72,...  8.89 us
  transfers between devices with their start and end apart: 3, of which 3 were waited for; matrix products, arithmetic and copies ran while one was open for 12% of the time, Pallas kernels for 11%

profile of v4, /device:TPU:1, one launch (start us, length us, event | category | flops | bytes accessed | tf_op | source)
XLA Modules:
  0.0 195.4 jit_solution(13372392186719683631)
XLA Ops:
  0.0 0.7 broadcast_multiply_fusion.1
  0.7 0.9 convert_reduce_fusion
  1.7 1.1 fusion.7
  2.8 0.6 bitcast_add_fusion.slots
  3.4 0.8 fusion.23
  4.2 1.5 stack.17.table
  5.7 8.9 %pack.1 = f32[2304,128]{1,0:T(8,128)} custom-call(s32[4096]{0:T(1024)} %bitcast_add_fusion.slots, s32[8,4096]{1,0:T(8,128)} %stack.17.table, f32[8,4,4096]{2,1,0:T(4,128)} %values.1), custom_call_target="tpu_custom_call" | custom-call | bytes 4194304 | tf_op jit(solution)/shard_map/pack/pallas_call | solution.py:92
  14.6 12.1 %all-to-all-start = ((f32[32,72,128]{2,1,0:T(8,128)}), f32[32,72,128]{2,1,0:T(8,128)}, u32[]{:S(2)}, u32[]{:S(2)}) async-start(f32[32,72,128]{2,1,0:T(8,128)} %bitcast.150), calls=%async_computation | async-start | bytes 2359296 | tf_op jit(solution)/shard_map/all_to_all | solution.py:867
  26.8 0.1 fusion.19
  26.9 0.1 fusion.11
  27.3 0.1 divide_exponential_fusion.6
  27.4 2.0 %copy.28 = f32[32,128,4]{2,1,0:T(8,128)} copy(f32[32,128,4]{1,0,2:T(8,128)S(1)} %pad_maximum_fusion.3) | data formatting | bytes 131072 | tf_op jit(solution)/shard_map/concatenate | solution.py:283
  29.5 0.4 reshape.1431
  30.1 0.1 fusion.17
  30.3 3.7 %reduce-precision_convert_fusion.2 = (bf16[32,128,128]{2,1,0:T(8,128)(2,1)S(1)}, bf16[32,128,128]{2,1,0:T(8,128)(2,1)S(1)}, f32[32,128,128]{2,1,0:T(8,128)S(1)}) fusion(pred[128,128]{1,0:T(8,128)(4,1)S(1)} %get-tuple-element.56, f32[32]{0:T(128)S(1)} %exponential-minus-one_negate_fusion, f32[32]{0:T(128)S(1)} %broadcast_in_dim_reshape.3, ...), kind=kLoop, calls=%fused_computation.11 | loop fusion | flops 7340032 | bytes 4489856 | tf_op jit(solution)/shard_map/convert_element_type | solution.py:318
  33.9 0.3 pad_maximum_fusion.1.mix
  34.3 0.2 add_multiply_fusion.1
  34.4 0.6 reduce-precision_convert_fusion.1
  35.0 1.8 pad_maximum_fusion.2.back
  36.8 1.2 copy-done.1
  38.0 1.0 reduce-precision_convert_fusion
  39.0 6.1 %pad_maximum_fusion.first = bf16[32,384,256]{2,1,0:T(8,128)(2,1)} fusion(bf16[32,128,256]{2,1,0:T(8,128)(2,1)S(1)} %get-tuple-element.42, bf16[32,128,256]{2,1,0:T(8,128)(2,1)S(1)} %get-tuple-element.41), kind=kLoop, calls=%fused_computation | loop fusion | flops 18874368 | bytes 10485760 | tf_op jit(solution)/shard_map/concatenate | solution.py:319
  45.1 9.1 %all-to-all-done.got = f32[32,72,128]{2,1,0:T(8,128)} async-done(((f32[32,72,128]{2,1,0:T(8,128)}), f32[32,72,128]{2,1,0:T(8,128)}, u32[]{:S(2)}, u32[]{:S(2)}) %all-to-all-start) | async-done | bytes 1179680 | tf_op jit(solution)/shard_map/all_to_all | solution.py:867
  54.2 1.5 and_convert_fusion
  55.8 0.1 convert_element_type.91
  55.9 0.7 pad.22.quarters
  56.5 1.2 broadcast_in_dim.41.decay
  57.7 28.9 %force.1 = (f32[12,768,128]{2,1,0:T(8,128)}, f32[1536,128]{1,0:T(8,128)}) custom-call(s32[8192]{0:T(1024)} %bitcast.161, f32[32,72,128]{2,1,0:T(8,128)} %all-to-all-done.got, f32[32,8,64]{2,1,0:T(8,128)} %pad.22.quarters, f32[768,1536]{1,0:T(8,128)} %bitcast.152, f32[1536,128]{1,0:T(8,128)} %broadcast_in_dim.41.decay), custom_call_target="tpu_custom_call" | custom-call | bytes 16777216 | tf_op jit(solution)/shard_map/force/pallas_call | solution.py:242
  86.6 9.4 %all-to-all-start.1 = ((f32[32,48,128]{2,1,0:T(8,128)}), f32[32,48,128]{2,1,0:T(8,128)}, u32[]{:S(2)}, u32[]{:S(2)}) async-start(f32[32,48,128]{2,1,0:T(8,128)} %bitcast.157), calls=%async_computation.1 | async-start | bytes 1572864 | tf_op jit(solution)/shard_map/all_to_all | solution.py:890
  96.1 0.7 constant_dynamic-slice_fusion.3
  96.9 0.6 pad.23.decay
  97.5 0.6 constant_dynamic-slice_fusion.1.mix
  98.1 1.5 constant_dynamic-slice_fusion.back
  99.7 1.6 constant_dynamic-slice_fusion.2.first
  101.3 10.7 %lon.2.low = f32[12,384,128]{2,1,0:T(8,128)} custom-call(f32[12,768,128]{2,1,0:T(8,128)} %get-tuple-element.25.x, bf16[32,384,256]{2,1,0:T(8,128)(2,1)} %pad_maximum_fusion.first, bf16[32,384,128]{2,1,0:T(8,128)(2,1)} %copy-done, bf16[32,384,128]{2,1,0:T(8,128)(2,1)} %pad_maximum_fusion.2.back), custom_call_target="tpu_custom_call" | custom-call | flops 1358954496 | bytes 31457280 | tf_op jit(solution)/shard_map/lon/pallas_call | solution.py:393
  112.0 2.9 %all-to-all-done.1 = f32[32,48,128]{2,1,0:T(8,128)} async-done(((f32[32,48,128]{2,1,0:T(8,128)}), f32[32,48,128]{2,1,0:T(8,128)}, u32[]{:S(2)}, u32[]{:S(2)}) %all-to-all-start.1) | async-done | bytes 786464 | tf_op jit(solution)/shard_map/all_to_all | solution.py:890
  114.9 5.0 %hub.1 = f32[1536,128]{1,0:T(8,128)} custom-call(f32[24,128]{1,0:T(8,128)} %pad.23.decay, f32[1536,128]{1,0:T(8,128)} %bitcast.18.moments, bf16[1,384,256]{2,1,0:T(8,128)(2,1)} %constant_dynamic-slice_fusion.2.first, bf16[1,384,128]{2,1,0:T(8,128)(2,1)} %constant_dynamic-slice_fusion.1.mix, bf16[1,384,128]{2,1,0:T(8,128)(2,1)} %constant_dynamic-slice_fusion.back), custom_call_target="tpu_custom_call" | custom-call | bytes 4194304 | tf_op jit(solution)/shard_map/hub/pallas_call | solution.py:493
  120.0 8.7 %all-to-all-start.2 = ((f32[32,48,128]{2,1,0:T(8,128)}), f32[32,48,128]{2,1,0:T(8,128)S(1)}, u32[]{:S(2)}, u32[]{:S(2)}) async-start(f32[32,48,128]{2,1,0:T(8,128)} %bitcast.155), calls=%async_computation.2 | async-start | bytes 1572864 | tf_op jit(solution)/shard_map/all_to_all | solution.py:897
  128.8 0.6 reshape.1437.vert
  129.4 0.3 slice_reduce_fusion.7
  129.7 0.1 copy.35
  129.8 10.8 %lon.3.high = f32[12,384,128]{2,1,0:T(8,128)} custom-call(f32[12,768,128]{2,1,0:T(8,128)} %get-tuple-element.25.x, bf16[32,384,256]{2,1,0:T(8,128)(2,1)} %pad_maximum_fusion.first, bf16[32,384,128]{2,1,0:T(8,128)(2,1)} %copy-done, bf16[32,384,128]{2,1,0:T(8,128)(2,1)} %pad_maximum_fusion.2.back), custom_call_target="tpu_custom_call" | custom-call | flops 1358954496 | bytes 31457280 | tf_op jit(solution)/shard_map/lon/pallas_call | solution.py:393
  140.6 7.9 %all-to-all-done.2 = f32[32,48,128]{2,1,0:T(8,128)S(1)} async-done(((f32[32,48,128]{2,1,0:T(8,128)}), f32[32,48,128]{2,1,0:T(8,128)S(1)}, u32[]{:S(2)}, u32[]{:S(2)}) %all-to-all-start.2) | async-done | bytes 786464 | tf_op jit(solution)/shard_map/all_to_all | solution.py:897
  148.5 0.8 broadcast_in_dim.42.coef
  149.3 0.1 copy-done.2
  149.4 9.2 %lat_states.1 = (f32[12,768,128]{2,1,0:T(8,128)}, f32[2368,128]{1,0:T(8,128)}) custom-call(f32[12,384,128]{2,1,0:T(8,128)} %lon.2.low, f32[12,384,128]{2,1,0:T(8,128)} %lon.3.high, f32[1536,128]{1,0:T(8,128)} %broadcast_in_dim.41.decay, f32[1536,128]{1,0:T(8,128)} %bitcast.154, f32[32]{0:T(128)} %reshape.1437.vert, f32[4,8,128]{2,1,0:T(8,128)} %broadcast_in_dim.42.coef), custom_call_target="tpu_custom_call" | custom-call | bytes 12582912 | tf_op jit(solution)/shard_map/lat_states/pallas_call | solution.py:592
  158.6 31.5 %level_exchange.1 = f32[8,288,128]{2,1,0:T(8,128)} custom-call(f32[8,296,128]{2,1,0:T(8,128)} %bitcast.156), custom_call_target="tpu_custom_call" | custom-call | bytes 3145728 | tf_op jit(solution)/shard_map/level_exchange/pallas_call | solution.py:758
  190.2 5.1 %level_states.1 = f32[8,4,24,1536]{3,2,1,0:T(8,128)} custom-call(f32[12,8,4,24,128]{4,3,2,1,0:T(8,128)} %bitcast.151, f32[32]{0:T(128)} %reshape.1437.vert, f32[4,2,2,6,24,128]{5,4,3,2,1,0:T(8,128)} %bitcast.153), custom_call_target="tpu_custom_call" | custom-call | bytes 11534336 | tf_op jit(solution)/shard_map/level_states/pallas_call | solution.py:818
  (44 shorter events, 1.0 us)
Async XLA Ops:
  5.7 21.4 %copy-start.5 = (f32[8,4]{0,1:T(4,128)S(1)}, f32[8,4]{0,1:T(4,128)}, u32[]{:S(2)}) copy-start(f32[8,4]{0,1:T(4,128)} %param.12) | copy-start | bytes 388
  14.6 14.8 %copy-start.4 = (f32[8,4,768]{2,1,0:T(4,128)S(1)}, f32[8,4,768]{2,1,0:T(4,128)}, u32[]{:S(2)}) copy-start(f32[8,4,768]{2,1,0:T(4,128)} %param.11) | copy-start | bytes 294916
  14.6 39.6 %all-to-all-start = ((f32[32,72,128]{2,1,0:T(8,128)}), f32[32,72,128]{2,1,0:T(8,128)}, u32[]{:S(2)}, u32[]{:S(2)}) async-start(f32[32,72,128]{2,1,0:T(8,128)} %bitcast.150), calls=%async_computation | async-start | bytes 2359296 | tf_op jit(solution)/shard_map/all_to_all | solution.py:867
  29.9 4.0 %copy-start.3 = (f32[32,32,24]{2,1,0:T(8,128)}, f32[32,32,24]{2,1,0:T(8,128)S(1)}, u32[]{:S(2)}) copy-start(f32[32,32,24]{2,1,0:T(8,128)S(1)} %reshape.1431) | copy-start | bytes 294916
  34.2 63.3 %copy-start = (bf16[32,384,128]{2,1,0:T(8,128)(2,1)}, bf16[32,384,128]{2,1,0:T(8,128)(2,1)S(1)}, u32[]{:S(2)}) copy-start(bf16[32,384,128]{2,1,0:T(8,128)(2,1)S(1)} %pad_maximum_fusion.1.mix) | copy-start | bytes 9437188
  35.0 3.0 %copy-start.1 = (f32[32,128,4]{2,1,0:T(8,128)S(1)}, f32[32,128,4]{2,1,0:T(8,128)}, u32[]{:S(2)}) copy-start(f32[32,128,4]{2,1,0:T(8,128)} %copy.28) | copy-start | bytes 196612
  86.6 28.3 %all-to-all-start.1 = ((f32[32,48,128]{2,1,0:T(8,128)}), f32[32,48,128]{2,1,0:T(8,128)}, u32[]{:S(2)}, u32[]{:S(2)}) async-start(f32[32,48,128]{2,1,0:T(8,128)} %bitcast.157), calls=%async_computation.1 | async-start | bytes 1572864 | tf_op jit(solution)/shard_map/all_to_all | solution.py:890
  112.0 16.6 %copy-start.6 = (f32[8,4]{0,1:T(4,128)S(1)}, f32[8,4]{0,1:T(4,128)}, u32[]{:S(2)}) copy-start(f32[8,4]{0,1:T(4,128)} %param.13) | copy-start | bytes 388
  120.0 28.5 %all-to-all-start.2 = ((f32[32,48,128]{2,1,0:T(8,128)}), f32[32,48,128]{2,1,0:T(8,128)S(1)}, u32[]{:S(2)}, u32[]{:S(2)}) async-start(f32[32,48,128]{2,1,0:T(8,128)} %bitcast.155), calls=%async_computation.2 | async-start | bytes 1572864 | tf_op jit(solution)/shard_map/all_to_all | solution.py:897
  148.5 0.9 copy-start.2

commit v5 on v4

--- a/solution.py
+++ b/solution.py
@@ -343,75 +343,7 @@
 LON_STEP = 4
 
 
-def lon_kernel(count, first_group, x, first, mix, back, out, xs, ws, ms, bs, done, sems, out_sem):
-    tiles, rows, _ = out.shape
-    steps = rows // count // LON_STEP
-    size = LON_STEP * count
-
-    def fetches(i):
-        group = first_group + i * LON_STEP
-        source = pl.ds(pl.multiple_of(group * count, 8), size)
-        target = pl.ds(pl.multiple_of(i * size, 8), size)
-        inside = pl.ds(i * LON_STEP, LON_STEP)
-        outside = pl.ds(group, LON_STEP)
-        return [
-            pltpu.make_async_copy(x.at[:, source], xs.at[:, target], sems.at[0, i]),
-            pltpu.make_async_copy(first.at[outside], ws.at[inside], sems.at[1, i]),
-            pltpu.make_async_copy(mix.at[outside], ms.at[inside], sems.at[2, i]),
-            pltpu.make_async_copy(back.at[outside], bs.at[inside], sems.at[3, i]),
-        ]
-
-    def write(i):
-        at = pl.ds(pl.multiple_of(i * size, 8), size)
-        return pltpu.make_async_copy(done.at[:, at], out.at[:, at], out_sem.at[i])
-
-    for i in range(steps):
-        for fetch in fetches(i):
-            fetch.start()
-
-    @pl.loop(0, steps)
-    def _(i):
-        for fetch in fetches(i):
-            fetch.wait()
-        for u in range(LON_STEP):
-            g = i * LON_STEP + u
-            at = pl.ds(pl.multiple_of(g * count, 8), count)
-            parts = lon_apply([xs[b, at, :] for b in range(tiles)], ws[g], ms[g], bs[g])
-            for b in range(tiles):
-                done[b, at, :] = parts[b]
-        write(i).start()
-
-    for i in range(steps):
-        write(i).wait()
-
-
-def lon_filter(x, weights, row_count, half):
-    tiles, rows, _ = x.shape
-    groups = rows // row_count // 2
-    steps = groups // LON_STEP
-    any_space = pl.BlockSpec(memory_space=pl.ANY)
-    return pl.pallas_call(
-        functools.partial(lon_kernel, row_count, half * groups),
-        out_shape=jax.ShapeDtypeStruct((tiles, rows // 2, LANE), f32),
-        in_specs=[any_space] * 4,
-        out_specs=any_space,
-        scratch_shapes=[pltpu.VMEM((tiles, rows // 2, LANE), f32)]
-        + [pltpu.VMEM((groups,) + w.shape[1:], w.dtype) for w in weights]
-        + [
-            pltpu.VMEM((tiles, rows // 2, LANE), f32),
-            pltpu.SemaphoreType.DMA((4, steps)),
-            pltpu.SemaphoreType.DMA((steps,)),
-        ],
-        compiler_params=vmem(60),
-        cost_estimate=cost(3 * rows * tiles * LANE * 3 * LANE, 30 << 20),
-        name="lon",
-    )(x, *weights)
-
-
-def hub_kernel(decay, moments, first, mix, back, states, work):
-    blocks = 32
-    depth = moments.shape[0] // blocks
-    tiles = depth // 4
+def hub_coefficients(decay):
     count = decay.shape[0]
     coef = [decay[r : r + 1, :] for r in range(count)]
 
@@ -443,35 +375,119 @@
     bfbp = backward(fbp)
     fq = forward(up)
     bfq = backward(fq)
-    t21, t31, t41, t32, t42 = bp[0], fbp[-1], bfbp[0], fq[-1], bfq[0]
+    return full, bp[0], fbp[-1], bfbp[0], fq[-1], bfq[0]
+
+
+def state_exchange_kernel(
+    count, field, moments, decay, first, mix, back, own_first, own_mix, own_back, out, states,
+    arrived, replies, work, xs, ws, ms, bs, sems, out_sem, send, recv, back_send, back_recv,
+):
+    tiles, rows, _ = out.shape
+    blocks = arrived.shape[0]
+    me = lax.axis_index("sub")
+    steps = rows // count // LON_STEP
+    size = LON_STEP * count
+
+    def fetches(i):
+        group = i * LON_STEP
+        at = pl.ds(pl.multiple_of(group * count, 8), size)
+        inside = pl.ds(group, LON_STEP)
+        return [
+            pltpu.make_async_copy(field.at[:, at], xs.at[:, at], sems.at[0, i]),
+            pltpu.make_async_copy(first.at[inside], ws.at[inside], sems.at[1, i]),
+            pltpu.make_async_copy(mix.at[inside], ms.at[inside], sems.at[2, i]),
+            pltpu.make_async_copy(back.at[inside], bs.at[inside], sems.at[3, i]),
+        ]
+
+    def write(i):
+        at = pl.ds(pl.multiple_of(i * size, 8), size)
+        return pltpu.make_async_copy(xs.at[:, at], out.at[:, at], out_sem.at[i])
+
+    for i in range(steps):
+        for fetch in fetches(i):
+            fetch.start()
+
+    def lon_steps(start, stop):
+        @pl.loop(start, stop)
+        def _(i):
+            for fetch in fetches(i):
+                fetch.wait()
+            for u in range(LON_STEP):
+                g = i * LON_STEP + u
+                at = pl.ds(pl.multiple_of(g * count, 8), count)
+                parts = lon_apply([xs[b, at, :] for b in range(tiles)], ws[g], ms[g], bs[g])
+                for b in range(tiles):
+                    xs[b, at, :] = parts[b]
+            write(i).start()
+
+    barrier = pltpu.get_barrier_semaphore()
+
+    @pl.loop(1, blocks)
+    def _(step):
+        target = lax.rem(me + step, blocks)
+        pl.semaphore_signal(
+            barrier, inc=1, device_id={"sub": target}, device_id_type=pl.DeviceIdType.MESH
+        )
+
+    pl.semaphore_wait(barrier, blocks - 1)
+
+    def outward(step):
+        target = lax.rem(me + step, blocks)
+        return pltpu.make_async_remote_copy(
+            src_ref=moments.at[target],
+            dst_ref=arrived.at[me],
+            send_sem=send.at[step - 1],
+            recv_sem=recv.at[step - 1],
+            device_id={"sub": target},
+            device_id_type=pl.DeviceIdType.MESH,
+        )
+
+    def homeward(step):
+        target = lax.rem(me + step, blocks)
+        return pltpu.make_async_remote_copy(
+            src_ref=replies.at[target],
+            dst_ref=states.at[me],
+            send_sem=back_send.at[step - 1],
+            recv_sem=back_recv.at[step - 1],
+            device_id={"sub": target},
+            device_id_type=pl.DeviceIdType.MESH,
+        )
+
+    @pl.loop(1, blocks)
+    def _(step):
+        outward(step).start()
+
+    arrived[me] = moments[me]
+    lon_steps(0, steps // 2)
+
+    @pl.loop(1, blocks)
+    def _(step):
+        outward(step).wait_recv()
+
+    full, t21, t31, t41, t32, t42 = hub_coefficients(decay)
 
     def at(table, d):
         return jnp.broadcast_to(table[:, d : d + 1], (tiles, LANE))
 
     def moment(d, k):
-        return moments[d * depth + k * tiles : d * depth + (k + 1) * tiles, :]
-
-    def put(d, k, value):
-        for t in range(tiles):
-            work[t, k * blocks + d, :] = value[t]
-
-    zero = jnp.zeros((tiles, LANE), f32)
+        return arrived[d, k * tiles : (k + 1) * tiles, :]
+
+    carry = jnp.zeros((tiles, LANE), f32)
     s = [[None] * blocks for _ in range(4)]
-    carry = zero
     for d in range(blocks):
         s[0][d] = carry
         carry = at(full, d) * carry + moment(d, 0)
-    carry = zero
+    carry = jnp.zeros((tiles, LANE), f32)
     for d in range(blocks - 1, -1, -1):
         s[1][d] = carry
         carry = at(full, d) * carry + (moment(d, 1) + at(t21, d) * s[0][d])
-    carry = zero
+    carry = jnp.zeros((tiles, LANE), f32)
     for d in range(blocks):
         s[2][d] = carry
         carry = at(full, d) * carry + (
             moment(d, 2) + at(t31, d) * s[0][d] + at(t32, d) * s[1][d]
         )
-    carry = zero
+    carry = jnp.zeros((tiles, LANE), f32)
     for d in range(blocks - 1, -1, -1):
         s[3][d] = carry
         carry = at(full, d) * carry + (
@@ -479,27 +495,64 @@
         )
     for k in range(4):
         for d in range(blocks):
-            put(d, k, s[k][d])
-    done = lon_apply([work[t] for t in range(tiles)], first[0], mix[0], back[0])
+            for t in range(tiles):
+                work[t, k * blocks + d : k * blocks + d + 1, :] = s[k][d][t : t + 1, :]
+    done = lon_apply([work[t] for t in range(tiles)], own_first[0], own_mix[0], own_back[0])
     for t in range(tiles):
         for k in range(4):
-            states[pl.ds(k * tiles + t, blocks, stride=depth), :] = done[t][
-                k * blocks : (k + 1) * blocks
-            ]
-
-
-def hub(decay, moments, weights):
-    depth = moments.shape[0] // 32
+            replies[:, k * tiles + t, :] = done[t][k * blocks : (k + 1) * blocks]
+
+    @pl.loop(1, blocks)
+    def _(step):
+        homeward(step).start()
+
+    states[me] = replies[me]
+    lon_steps(steps // 2, steps)
+
+    @pl.loop(1, blocks)
+    def _(step):
+        homeward(step).wait_recv()
+
+    @pl.loop(1, blocks)
+    def _(step):
+        outward(step).wait_send()
+        homeward(step).wait_send()
+
+    for i in range(steps):
+        write(i).wait()
+
+
+def state_exchange(field, moments, decay, weights, own_weights, row_count):
+    tiles, rows, _ = field.shape
+    blocks, depth, _ = moments.shape
+    groups = rows // row_count
+    steps = groups // LON_STEP
+    any_space = pl.BlockSpec(memory_space=pl.ANY)
+    whole = pl.BlockSpec(memory_space=pltpu.VMEM)
+    dma = pltpu.SemaphoreType.DMA
     return pl.pallas_call(
-        hub_kernel,
-        out_shape=jax.ShapeDtypeStruct(moments.shape, f32),
-        in_specs=[pl.BlockSpec(memory_space=pltpu.VMEM)] * 5,
-        out_specs=pl.BlockSpec(memory_space=pltpu.VMEM),
-        scratch_shapes=[pltpu.VMEM((depth // 4, 128, LANE), f32)],
-        compiler_params=vmem(60),
-        cost_estimate=cost(0, 4 << 20),
-        name="hub",
-    )(decay, moments, *weights)
+        functools.partial(state_exchange_kernel, row_count),
+        out_shape=(
+            jax.ShapeDtypeStruct(field.shape, f32),
+            jax.ShapeDtypeStruct(moments.shape, f32),
+        ),
+        in_specs=[any_space, whole, whole] + [any_space] * 3 + [whole] * 3,
+        out_specs=(any_space, whole),
+        scratch_shapes=[
+            pltpu.VMEM(moments.shape, f32),
+            pltpu.VMEM(moments.shape, f32),
+            pltpu.VMEM((tiles, 4 * blocks, LANE), f32),
+            pltpu.VMEM(field.shape, f32),
+        ]
+        + [pltpu.VMEM(w.shape, w.dtype) for w in weights]
+        + [dma((4, steps)), dma((steps,))]
+        + [dma((blocks - 1,))] * 4,
+        compiler_params=pltpu.CompilerParams(
+            vmem_limit_bytes=60 << 20, collective_id=1, has_side_effects=True
+        ),
+        cost_estimate=cost(6 * rows * tiles * LANE * 3 * LANE, 60 << 20),
+        name="state_exchange",
+    )(field, moments, decay, *weights, *own_weights)
 
 
 def level_sweeps(rows, decay, starts):
@@ -517,28 +570,22 @@
     return rows, ends
 
 
-def lat_states_kernel(row_count, groups, variables, low, high, decay, states, vert, coef, out, sums, field, sems, out_sem):
+def lat_states_kernel(row_count, groups, variables, source, decay, states, vert, coef, out, sums, field, sems, out_sem):
     tiles = out.shape[0]
     per_group = states.shape[0] // groups
-    half = low.shape[1]
     levels = groups // variables
     depth = tiles // 2 * row_count
     size = sums.shape[0] // (2 * variables)
 
-    def fetches(ct):
-        return [
-            pltpu.make_async_copy(low.at[ct], field.at[ct, :half], sems.at[0, ct]),
-            pltpu.make_async_copy(high.at[ct], field.at[ct, half:], sems.at[1, ct]),
-        ]
+    def fetch(ct):
+        return pltpu.make_async_copy(source.at[ct], field.at[ct], sems.at[ct])
 
     for ct in range(tiles):
-        for fetch in fetches(ct):
-            fetch.start()
+        fetch(ct).start()
 
     @pl.loop(0, tiles)
     def _(ct):
-        for fetch in fetches(ct):
-            fetch.wait()
+        fetch(ct).wait()
         done = field.at[ct]
         for first in range(0, groups // 8, SIDE):
             octets = range(first, first + SIDE)
@@ -584,8 +631,8 @@
         pltpu.make_async_copy(field.at[ct], out.at[ct], out_sem.at[ct]).wait()
 
 
-def lat_states(low, high, decay, states, vert, coef, row_count, groups, variables):
-    tiles, rows = low.shape[0], 2 * low.shape[1]
+def lat_states(x, decay, states, vert, coef, row_count, groups, variables):
+    tiles, rows, _ = x.shape
     size = 2 * variables * (tiles * row_count + 8)
     whole = pl.BlockSpec(memory_space=pltpu.VMEM)
     any_space = pl.BlockSpec(memory_space=pl.ANY)
@@ -595,17 +642,17 @@
             jax.ShapeDtypeStruct((tiles, rows, LANE), f32),
             jax.ShapeDtypeStruct((size, LANE), f32),
         ),
-        in_specs=[any_space, any_space, whole, whole, pl.BlockSpec(memory_space=pltpu.SMEM), whole],
+        in_specs=[any_space, whole, whole, pl.BlockSpec(memory_space=pltpu.SMEM), whole],
         out_specs=(any_space, whole),
         scratch_shapes=[
             pltpu.VMEM((tiles, rows, LANE), f32),
-            pltpu.SemaphoreType.DMA((2, tiles)),
+            pltpu.SemaphoreType.DMA((tiles,)),
             pltpu.SemaphoreType.DMA((tiles,)),
         ],
         compiler_params=vmem(60),
         cost_estimate=cost(0, 12 << 20),
         name="lat_states",
-    )(low, high, decay, states, vert, coef)
+    )(x, decay, states, vert, coef)
 
 
 def level_exchange_kernel(sums, out, beside, merged, arrived, replies, entering, passed, *sems):
@@ -882,22 +929,16 @@
     weights = lon_weights(lengths, lon_count)
     own_weights = [lax.dynamic_slice_in_dim(w, sub_index, 1, 0) for w in weights]
 
-    got, weights = lax.optimization_barrier((got, weights))
+    got, weights, own_weights = lax.optimization_barrier((got, weights, own_weights))
     places = got[:, capacity // 4 : capacity // 4 + lines, :].reshape(-1).astype(jnp.int32)
     quarters = (places & 3).astype(f32).reshape(sub_count, 4, capacity // 4)
     quarters = jnp.pad(quarters, ((0, 0), (0, 4), (0, 0)))
     forced, moments = force(places >> 2, got, quarters, tile_field, decay, row_count, groups)
-    moments = lax.all_to_all(
-        moments.reshape(sub_count, 4 * tiles, LANE), "sub", 0, 0, tiled=True
+    smooth, states = state_exchange(
+        forced, moments.reshape(sub_count, 4 * tiles, LANE), hub_lat, weights, own_weights, row_count
     )
-    low = lon_filter(forced, weights, row_count, 0)
-    moments, low = lax.optimization_barrier((moments, low))
-    states = hub(hub_lat, moments.reshape(-1, LANE), own_weights)
-    states, forced = lax.optimization_barrier((states, forced))
-    states = lax.all_to_all(states.reshape(sub_count, 4 * tiles, LANE), "sub", 0, 0, tiled=True)
-    high = lon_filter(forced, weights, row_count, 1)
     smooth, sums = lat_states(
-        low, high, decay, states.reshape(-1, LANE), vert_decay, coef, row_count, groups, var_count
+        smooth, decay, states.reshape(-1, LANE), vert_decay, coef, row_count, groups, var_count
     )
     entering = level_exchange(sums.reshape(band_count, -1, LANE))
     return level_states(

time: 196 us -> 183 us (0.934)
  Pallas kernels: 110 us -> 133 us
  starting transfers between devices: 30.2 us -> 12.1 us
  waiting for transfers between devices: 19.9 us -> 8.55 us
  other arithmetic: 18.9 us -> 12.8 us
    pallas_call x3 -> x1, Pallas kernels: 26.5 us -> 49.3 us  [state_exchange(): pl.pallas_call(functools.partial(state_exchange_kernel, row_count), out_s...]
    all_to_all x2 -> x0, starting transfers between devices: 18.1 us -> none  [the longest x1 9.45 us: per_device(): lax.all_to_all(moments.reshape(sub_count, 4 * tiles, LANE), 'sub', 0, 0,...]
    all_to_all x2 -> x0, waiting for transfers between devices: 10.8 us -> none  [the longest x1 7.89 us: per_device(): lax.all_to_all(states.reshape(sub_count, 4 * tiles, LANE), 'sub', 0, 0, t...]
    concatenate x3, other arithmetic: 8.18 us -> 1.99 us  [thirds(): return jnp.concatenate([high, high, low], axis=1)]
    unnamed x16, local copies, waits for them, and re-layouts: 1.49 us -> 4.14 us
  transfers between devices with their start and end apart: 3 -> 1, of which waited for: 3 -> 1; matrix products, arithmetic and copies ran while one was open for 12% -> 8% of each run, Pallas kernels for 11% -> 0%
where the time goes in v5:
time: 183 us; the launch traced here: 182 us
  Pallas kernels  133 us (73%)
  local copies, waits for them, and re-layouts  14.6 us (8%)
  other arithmetic  12.8 us (7%)
  starting transfers between devices  12.1 us (7%)
  waiting for transfers between devices  8.55 us (5%)
    pallas_call x1, Pallas kernels, state_exchange(): pl.pallas_call(functools.partial(state_exchange_kernel, row_count), out_s...  49.3 us
    pallas_call x1, Pallas kernels, level_exchange(): pl.pallas_call(level_exchange_kernel, out_shape=jax.ShapeDtypeStruct((ban...  30.9 us
    pallas_call x1, Pallas kernels, force(): pl.pallas_call(functools.partial(forced_kernel, row_count, groups), out_s...  29.3 us
    all_to_all x1, starting transfers between devices, per_device(): lax.all_to_all(message.reshape(sub_count, -1, LANE), 'sub', 0, 0, tiled=T...  12.1 us
    pallas_call x1, Pallas kernels, lat_states(): pl.pallas_call(functools.partial(lat_states_kernel, row_count, groups, va...  9.09 us
    pallas_call x1, Pallas kernels, pack(): pl.pallas_call(pack_kernel, out_shape=jax.ShapeDtypeStruct((targets * 72,...  8.95 us
    all_to_all x1, waiting for transfers between devices, per_device(): lax.all_to_all(message.reshape(sub_count, -1, LANE), 'sub', 0, 0, tiled=T...  8.55 us
    convert_element_type x3, other arithmetic, thirds(): high = high.astype(bf16)  5.25 us
  transfers between devices with their start and end apart: 1, of which 1 were waited for; matrix products, arithmetic and copies ran while one was open for 8% of the time, Pallas kernels for 0%

profile of v5, /device:TPU:1, one launch (start us, length us, event | category | flops | bytes accessed | tf_op | source)
XLA Modules:
  0.0 182.2 jit_solution(8731317548114695602)
XLA Ops:
  0.0 0.7 broadcast_multiply_fusion.1
  0.7 0.9 convert_reduce_fusion
  1.7 1.1 fusion.7
  2.8 0.8 fusion.23
  3.6 0.6 bitcast_add_fusion.slots
  4.2 1.5 stack.17.table
  5.7 9.0 %pack.1 = f32[2304,128]{1,0:T(8,128)} custom-call(s32[4096]{0:T(1024)} %bitcast_add_fusion.slots, s32[8,4096]{1,0:T(8,128)} %stack.17.table, f32[8,4,4096]{2,1,0:T(4,128)} %values.1), custom_call_target="tpu_custom_call" | custom-call | bytes 4194304 | tf_op jit(solution)/shard_map/pack/pallas_call | solution.py:92
  14.7 12.1 %all-to-all-start = ((f32[32,72,128]{2,1,0:T(8,128)}), f32[32,72,128]{2,1,0:T(8,128)}, u32[]{:S(2)}, u32[]{:S(2)}) async-start(f32[32,72,128]{2,1,0:T(8,128)} %bitcast.148), calls=%async_computation | async-start | bytes 2359296 | tf_op jit(solution)/shard_map/all_to_all | solution.py:914
  27.0 0.4 reshape.1425
  27.4 0.1 copy.27
  27.5 0.1 broadcast_in_dim_reshape.3
  27.6 0.1 add.320
  27.7 0.2 add_multiply_fusion.1
  27.8 0.6 reduce-precision_convert_fusion.1
  28.4 0.3 pad_maximum_fusion.2.back
  28.7 0.7 constant_dynamic-slice_fusion.2.own_back
  29.4 0.1 copy.31
  29.5 0.1 reshape.1426
  29.6 0.3 slice_reduce_fusion.7
  29.9 0.1 fusion.11
  30.0 0.1 divide_exponential_fusion.6
  30.1 0.1 fusion.17
  30.3 0.1 copy.33
  30.4 2.0 %copy.28 = f32[32,128,4]{2,1,0:T(8,128)} copy(f32[32,128,4]{1,0,2:T(8,128)S(1)} %pad_maximum_fusion.3) | data formatting | bytes 131072 | tf_op jit(solution)/shard_map/concatenate | solution.py:283
  32.4 0.1 copy.32
  32.5 0.6 pad.23.decay
  33.1 0.1 copy.35
  33.2 0.6 reshape.1429.vert
  33.8 0.1 fusion.19
  34.0 3.7 %reduce-precision_convert_fusion.2 = (bf16[32,128,128]{2,1,0:T(8,128)(2,1)S(1)}, bf16[32,128,128]{2,1,0:T(8,128)(2,1)S(1)}, f32[32,128,128]{2,1,0:T(8,128)S(1)}) fusion(pred[128,128]{1,0:T(8,128)(4,1)S(1)} %get-tuple-element.58, f32[32]{0:T(128)S(1)} %exponential-minus-one_negate_fusion, f32[32]{0:T(128)S(1)} %broadcast_in_dim_reshape.3, ...), kind=kLoop, calls=%fused_computation.11 | loop fusion | flops 7340032 | bytes 4489856 | tf_op jit(solution)/shard_map/convert_element_type | solution.py:318
  37.7 0.3 pad_maximum_fusion.1.mix
  38.0 0.6 constant_dynamic-slice_fusion.3.own_mix
  38.6 1.3 copy-done.3
  39.9 1.0 reduce-precision_convert_fusion
  41.0 1.4 pad_maximum_fusion.first
  42.4 2.7 %copy-done = bf16[32,384,256]{2,1,0:T(8,128)(2,1)} copy-done((bf16[32,384,256]{2,1,0:T(8,128)(2,1)}, bf16[32,384,256]{2,1,0:T(8,128)(2,1)S(1)}, u32[]{:S(2)}) %copy-start) | copy-done | bytes 6291480
  45.0 0.7 constant_dynamic-slice_fusion.4.own_first
  45.7 8.6 %all-to-all-done.got = f32[32,72,128]{2,1,0:T(8,128)} async-done(((f32[32,72,128]{2,1,0:T(8,128)}), f32[32,72,128]{2,1,0:T(8,128)}, u32[]{:S(2)}, u32[]{:S(2)}) %all-to-all-start) | async-done | bytes 1179680 | tf_op jit(solution)/shard_map/all_to_all | solution.py:914
  54.3 1.5 and_convert_fusion
  55.8 0.1 convert_element_type.91
  55.9 0.7 pad.22.quarters
  56.6 1.2 broadcast_in_dim.41.decay
  57.8 29.3 %force.1 = (f32[12,768,128]{2,1,0:T(8,128)}, f32[1536,128]{1,0:T(8,128)}) custom-call(s32[8192]{0:T(1024)} %bitcast.158, f32[32,72,128]{2,1,0:T(8,128)} %all-to-all-done.got, f32[32,8,64]{2,1,0:T(8,128)} %pad.22.quarters, f32[768,1536]{1,0:T(8,128)} %bitcast.150, f32[1536,128]{1,0:T(8,128)} %broadcast_in_dim.41.decay), custom_call_target="tpu_custom_call" | custom-call | bytes 16777216 | tf_op jit(solution)/shard_map/force/pallas_call | solution.py:242
  87.0 49.3 %state_exchange.1 = (f32[12,768,128]{2,1,0:T(8,128)}, f32[32,48,128]{2,1,0:T(8,128)}) custom-call(f32[12,768,128]{2,1,0:T(8,128)} %get-tuple-element.19.field, f32[32,48,128]{2,1,0:T(8,128)} %bitcast.153, f32[24,128]{1,0:T(8,128)} %pad.23.decay, bf16[32,384,256]{2,1,0:T(8,128)(2,1)} %copy-done, bf16[32,384,128]{2,1,0:T(8,128)(2,1)} %copy-done.2, ...), custom_call_target="tpu_custom_call" | custom-call | flops 2717908992 | bytes 62914560 | tf_op jit(solution)/shard_map/state_exchange/pallas_call | solution.py:533
  136.4 0.7 broadcast_in_dim.42.coef
  137.0 9.1 %lat_states.1 = (f32[12,768,128]{2,1,0:T(8,128)}, f32[2368,128]{1,0:T(8,128)}) custom-call(f32[12,768,128]{2,1,0:T(8,128)} %get-tuple-element.27.source, f32[1536,128]{1,0:T(8,128)} %broadcast_in_dim.41.decay, f32[1536,128]{1,0:T(8,128)} %bitcast.154, f32[32]{0:T(128)} %reshape.1429.vert, f32[4,8,128]{2,1,0:T(8,128)} %broadcast_in_dim.42.coef), custom_call_target="tpu_custom_call" | custom-call | bytes 12582912 | tf_op jit(solution)/shard_map/lat_states/pallas_call | solution.py:639
  146.1 30.9 %level_exchange.1 = f32[8,288,128]{2,1,0:T(8,128)} custom-call(f32[8,296,128]{2,1,0:T(8,128)} %bitcast.152), custom_call_target="tpu_custom_call" | custom-call | bytes 3145728 | tf_op jit(solution)/shard_map/level_exchange/pallas_call | solution.py:805
  177.0 5.1 %level_states.1 = f32[8,4,24,1536]{3,2,1,0:T(8,128)} custom-call(f32[12,8,4,24,128]{4,3,2,1,0:T(8,128)} %bitcast.149, f32[32]{0:T(128)} %reshape.1429.vert, f32[4,2,2,6,24,128]{5,4,3,2,1,0:T(8,128)} %bitcast.151), custom_call_target="tpu_custom_call" | custom-call | bytes 11534336 | tf_op jit(solution)/shard_map/level_states/pallas_call | solution.py:865
  (38 shorter events, 0.4 us)
Async XLA Ops:
  5.7 21.2 %copy-start.4 = (f32[8,4,768]{2,1,0:T(4,128)S(1)}, f32[8,4,768]{2,1,0:T(4,128)}, u32[]{:S(2)}) copy-start(f32[8,4,768]{2,1,0:T(4,128)} %param.11) | copy-start | bytes 294916
  14.7 12.7 %copy-start.5 = (f32[8,4]{0,1:T(4,128)S(1)}, f32[8,4]{0,1:T(4,128)}, u32[]{:S(2)}) copy-start(f32[8,4]{0,1:T(4,128)} %param.12) | copy-start | bytes 388
  14.7 39.6 %all-to-all-start = ((f32[32,72,128]{2,1,0:T(8,128)}), f32[32,72,128]{2,1,0:T(8,128)}, u32[]{:S(2)}, u32[]{:S(2)}) async-start(f32[32,72,128]{2,1,0:T(8,128)} %bitcast.148), calls=%async_computation | async-start | bytes 2359296 | tf_op jit(solution)/shard_map/all_to_all | solution.py:914
  28.4 1.2 copy-start.6
  28.7 8.9 %copy-start.1 = (bf16[32,384,128]{2,1,0:T(8,128)(2,1)}, bf16[32,384,128]{2,1,0:T(8,128)(2,1)S(1)}, u32[]{:S(2)}) copy-start(bf16[32,384,128]{2,1,0:T(8,128)(2,1)S(1)} %pad_maximum_fusion.2.back) | copy-start | bytes 9437188
  37.6 2.3 %copy-start.3 = (f32[32,128,4]{2,1,0:T(8,128)S(1)}, f32[32,128,4]{2,1,0:T(8,128)}, u32[]{:S(2)}) copy-start(f32[32,128,4]{2,1,0:T(8,128)} %copy.28) | copy-start | bytes 196612
  38.0 3.0 %copy-start.2 = (bf16[32,384,128]{2,1,0:T(8,128)(2,1)}, bf16[32,384,128]{2,1,0:T(8,128)(2,1)S(1)}, u32[]{:S(2)}) copy-start(bf16[32,384,128]{2,1,0:T(8,128)(2,1)S(1)} %pad_maximum_fusion.1.mix) | copy-start | bytes 9437188
  42.4 2.7 %copy-start = (bf16[32,384,256]{2,1,0:T(8,128)(2,1)}, bf16[32,384,256]{2,1,0:T(8,128)(2,1)S(1)}, u32[]{:S(2)}) copy-start(bf16[32,384,256]{2,1,0:T(8,128)(2,1)S(1)} %pad_maximum_fusion.first) | copy-start | bytes 18874372

commit v6 on v5

--- a/solution.py
+++ b/solution.py
@@ -147,14 +147,8 @@
     for fetch in fetches:
         fetch.start()
 
-    @pl.loop(0, depth // 64)
-    def _(i):
-        at = pl.ds(pl.multiple_of(i * 64, 64), 64)
-        for chain in chains:
-            chain[at, :] = jnp.zeros((64, LANE), f32)
-
-    lane = lax.broadcasted_iota(jnp.int32, (8, LANE), 1) // 32
-    pick = (lane == lax.broadcasted_iota(jnp.int32, (8, LANE), 0)).astype(bf16)
+    row = lax.broadcasted_iota(jnp.int32, (8, LANE), 0)
+    picks = [(row == k).astype(f32).astype(bf16) for k in range(4)]
     quarter = lax.broadcasted_iota(jnp.int32, (64, LANE), 1) // 32
     wanted = quarter.astype(f32)
 
@@ -167,19 +161,26 @@
             out = jnp.where(quarter == q, turned[(q - k) % 4], out)
         return out
 
-    @pl.loop(0, sources)
-    def _(d):
-        part = turns(got[d, :64, :])
-        mark = turns(
-            lax.dot_general(
-                quarters[d].astype(bf16), pick, (((0,), (0,)), ((), ())), preferred_element_type=f32
-            )
-        )
-        for k in range(4):
-            one = jnp.where(repeat(mark, k) == wanted, repeat(part, k), 0.0)
-            spread[pl.ds(pl.multiple_of(d * 256 + k * 64, 64), 64), :] = one
-
-    step = 4
+    share = depth // sources
+    together = 2
+
+    @pl.loop(0, sources // together)
+    def _(i):
+        for e in range(together):
+            d = i * together + e
+            at = pl.ds(pl.multiple_of(d * share, 8), share)
+            for chain in chains:
+                chain[at, :] = jnp.zeros((share, LANE), f32)
+            part = turns(got[d, :64, :])
+            marks = quarters[d].astype(bf16)
+            for k in range(4):
+                mark = lax.dot_general(
+                    marks, picks[k], (((0,), (0,)), ((), ())), preferred_element_type=f32
+                )
+                one = jnp.where(mark == wanted, repeat(part, k), 0.0)
+                spread[pl.ds(pl.multiple_of(d * 256 + k * 64, 64), 64), :] = one
+
+    step = 16
 
     @pl.loop(0, total // (CHAINS * step))
     def _(i):
@@ -378,9 +379,11 @@
     return full, bp[0], fbp[-1], bfbp[0], fq[-1], bfq[0]
 
 
-def state_exchange_kernel(
-    count, field, moments, decay, first, mix, back, own_first, own_mix, own_back, out, states,
-    arrived, replies, work, xs, ws, ms, bs, sems, out_sem, send, recv, back_send, back_recv,
+def exchange_kernel(
+    count, variables, field, moments, decay, table, first, mix, back, own_first, own_mix, own_back,
+    vert, coef, out, entered, arrived, replies, states, work, xs, ws, ms, bs, sums, beside, merged,
+    joined, answers, entering, passed, sems, out_sem, send, recv, back_send, back_recv, pair_send,
+    pair_recv, hub_send, hub_recv, reply_send, reply_recv, last_send, last_recv,
 ):
     tiles, rows, _ = out.shape
     blocks = arrived.shape[0]
@@ -398,10 +401,6 @@
             pltpu.make_async_copy(mix.at[inside], ms.at[inside], sems.at[2, i]),
             pltpu.make_async_copy(back.at[inside], bs.at[inside], sems.at[3, i]),
         ]
-
-    def write(i):
-        at = pl.ds(pl.multiple_of(i * size, 8), size)
-        return pltpu.make_async_copy(xs.at[:, at], out.at[:, at], out_sem.at[i])
 
     for i in range(steps):
         for fetch in fetches(i):
@@ -418,7 +417,6 @@
                 parts = lon_apply([xs[b, at, :] for b in range(tiles)], ws[g], ms[g], bs[g])
                 for b in range(tiles):
                     xs[b, at, :] = parts[b]
-            write(i).start()
 
     barrier = pltpu.get_barrier_semaphore()
 
@@ -429,7 +427,18 @@
             barrier, inc=1, device_id={"sub": target}, device_id_type=pl.DeviceIdType.MESH
         )
 
-    pl.semaphore_wait(barrier, blocks - 1)
+    band = lax.axis_index("band")
+    chip, core = band // 2, band % 2
+    sibling = chip * 2 + (1 - core)
+
+    def other(step):
+        return lax.rem(chip + step, 4) * 2 + core
+
+    for target in [sibling] + [other(step) for step in (1, 2, 3)]:
+        pl.semaphore_signal(
+            barrier, inc=1, device_id={"band": target}, device_id_type=pl.DeviceIdType.MESH
+        )
+    pl.semaphore_wait(barrier, blocks - 1 + 4)
 
     def outward(step):
         target = lax.rem(me + step, blocks)
@@ -518,41 +527,222 @@
         outward(step).wait_send()
         homeward(step).wait_send()
 
-    for i in range(steps):
-        write(i).wait()
-
-
-def state_exchange(field, moments, decay, weights, own_weights, row_count):
+    groups = rows // count
+    levels = groups // variables
+    half = tiles // 2
+    depth = half * count
+    tail = 2 * depth
+    zero = jnp.zeros((8, LANE), f32)
+    mine_first = core * 4
+
+    def level_remote(src, dst, send_sem, recv_sem, target):
+        return pltpu.make_async_remote_copy(
+            src_ref=src,
+            dst_ref=dst,
+            send_sem=send_sem,
+            recv_sem=recv_sem,
+            device_id={"band": target},
+            device_id_type=pl.DeviceIdType.MESH,
+        )
+
+    def pair(j):
+        return level_remote(
+            sums.at[(1 - core) * 4 + j], beside.at[j], pair_send.at[j], pair_recv.at[j], sibling
+        )
+
+    for target in range(2 * variables):
+        sums[target, tail : tail + 8, :] = coef[target // 2]
+
+    for side in range(2):
+
+        @pl.loop(0, half)
+        def _(spot):
+            ct = side * half + spot
+            done = xs.at[ct]
+            for o in range(groups // 8):
+                lines = [
+                    done[pl.ds(o * 8 * count + r, 8, stride=count), :] for r in range(count)
+                ]
+                starts = [states[o * 8 : o * 8 + 8, k * tiles + ct, :] for k in range(4)]
+                lines, _ = lat_sweeps([lines], [decay_of_octet(table, groups, o)], [starts])
+                for r in range(count):
+                    done[pl.ds(o * 8 * count + r, 8, stride=count), :] = lines[0][r]
+            pltpu.make_async_copy(done, out.at[ct], out_sem.at[ct]).start()
+            for var in range(variables):
+                for t in range(count // 8):
+                    lines = []
+                    for lev in range(levels):
+                        base = (lev * variables + var) * count + t * 8
+                        lines.append(done[base : base + 8, :])
+                    _, ends = level_sweeps(
+                        lines, lambda lev: vert[lev * variables + var], [zero, zero]
+                    )
+                    for k in range(2):
+                        at = pl.ds(pl.multiple_of(k * depth + spot * count + t * 8, 8), 8)
+                        sums[var * 2 + side, at, :] = ends[k]
+
+        for j in (side, side + 2):
+            pair(j).start()
+
+    def lower(a, b):
+        return jnp.where(core == 0, a, b)
+
+    def row(ref, chunk, at):
+        return jnp.broadcast_to(ref[chunk, at : at + 1, :], (8, LANE))
+
+    def bands_of(chunk, at):
+        a, b = sums[mine_first + chunk, at, :], beside[chunk, at, :]
+        return lower(a, b), lower(b, a)
+
+    def coefficients(chunk):
+        both = []
+        for at in (tail, tail + 1):
+            a, b = row(sums, mine_first + chunk, at), row(beside, chunk, at)
+            both.append((lower(a, b), lower(b, a)))
+        return both
+
+    def hub_copy(j):
+        step = lax.rem(j - chip + 4, 4)
+        return level_remote(
+            merged.at[j], joined.at[chip], hub_send.at[step - 1], hub_recv.at[step - 1], j * 2 + core
+        )
+
+    for j in (0, 2, 1, 3):
+        pair(j).wait_recv()
+        (full0, full1), (both0, both1) = coefficients(j)
+
+        @pl.loop(0, depth // 8)
+        def _(t):
+            at = pl.ds(pl.multiple_of(t * 8, 8), 8)
+            later = pl.ds(pl.multiple_of(depth + t * 8, 8), 8)
+            up0, up1 = bands_of(j, at)
+            down0, down1 = bands_of(j, later)
+            merged[j, at, :] = full1 * up0 + up1
+            merged[j, later, :] = down0 + full0 * (down1 + both1 * up0)
+
+        index = lax.broadcasted_iota(jnp.int32, (8, LANE), 0)
+        merged[j, tail : tail + 8, :] = jnp.where(
+            index == 0, full0 * full1, both0 + full0 * both1 * full0
+        )
+
+        @pl.when(chip != j)
+        def _():
+            hub_copy(j).start()
+
+    joined[chip] = merged[chip]
+    for step in (1, 2, 3):
+        hub_copy(lax.rem(chip + step, 4)).wait_recv()
+
+    fulls = [row(joined, c, tail) for c in range(4)]
+    boths = [row(joined, c, tail + 1) for c in range(4)]
+
+    @pl.loop(0, depth // 8)
+    def _(t):
+        at = pl.ds(pl.multiple_of(t * 8, 8), 8)
+        later = pl.ds(pl.multiple_of(depth + t * 8, 8), 8)
+        state = jnp.zeros((8, LANE), f32)
+        ups = []
+        for c in range(4):
+            ups.append(state)
+            answers[c, at, :] = state
+            state = fulls[c] * state + joined[c, at, :]
+        state = jnp.zeros((8, LANE), f32)
+        for c in (3, 2, 1, 0):
+            answers[c, later, :] = state
+            state = fulls[c] * state + (joined[c, later, :] + boths[c] * ups[c])
+
+    answer_copies = []
+    for step in (2, 1, 3):
+        copy = level_remote(
+            answers.at[lax.rem(chip + step, 4)],
+            entering.at[chip],
+            reply_send.at[step - 1],
+            reply_recv.at[step - 1],
+            other(step),
+        )
+        copy.start()
+        answer_copies.append(copy)
+    entering[chip] = answers[chip]
+    for copy in answer_copies:
+        copy.wait_recv()
+
+    last = []
+    for j in range(4):
+        (full0, full1), (both0, both1) = coefficients(j)
+
+        @pl.loop(0, depth // 8)
+        def _(t):
+            at = pl.ds(pl.multiple_of(t * 8, 8), 8)
+            later = pl.ds(pl.multiple_of(depth + t * 8, 8), 8)
+            up0, _ = bands_of(j, at)
+            _, down1 = bands_of(j, later)
+            below = entering[j, at, :]
+            above = entering[j, later, :]
+            middle = full0 * below + up0
+            turned = full1 * above + (down1 + both1 * middle)
+            entered[mine_first + j, at, :] = lower(below, middle)
+            entered[mine_first + j, later, :] = lower(turned, above)
+            passed[j, at, :] = lower(middle, below)
+            passed[j, later, :] = lower(above, turned)
+
+        copy = level_remote(
+            passed.at[j], entered.at[mine_first + j], last_send.at[j], last_recv.at[j], sibling
+        )
+        copy.start()
+        last.append(copy)
+
+    for j in range(4):
+        pair(j).wait_send()
+    for step in (1, 2, 3):
+        hub_copy(lax.rem(chip + step, 4)).wait_send()
+    for copy in answer_copies:
+        copy.wait_send()
+    for copy in last:
+        copy.wait()
+    for ct in range(tiles):
+        pltpu.make_async_copy(xs.at[ct], out.at[ct], out_sem.at[ct]).wait()
+
+
+def exchange(field, moments, decay, table, weights, own_weights, vert, coef, row_count, variables):
     tiles, rows, _ = field.shape
     blocks, depth, _ = moments.shape
     groups = rows // row_count
     steps = groups // LON_STEP
+    chunk = tiles * row_count
     any_space = pl.BlockSpec(memory_space=pl.ANY)
     whole = pl.BlockSpec(memory_space=pltpu.VMEM)
     dma = pltpu.SemaphoreType.DMA
     return pl.pallas_call(
-        functools.partial(state_exchange_kernel, row_count),
+        functools.partial(exchange_kernel, row_count, variables),
         out_shape=(
             jax.ShapeDtypeStruct(field.shape, f32),
-            jax.ShapeDtypeStruct(moments.shape, f32),
+            jax.ShapeDtypeStruct((2 * variables, chunk, LANE), f32),
         ),
-        in_specs=[any_space, whole, whole] + [any_space] * 3 + [whole] * 3,
+        in_specs=[any_space, whole, whole, whole]
+        + [any_space] * 3
+        + [whole] * 3
+        + [pl.BlockSpec(memory_space=pltpu.SMEM), whole],
         out_specs=(any_space, whole),
         scratch_shapes=[
+            pltpu.VMEM(moments.shape, f32),
             pltpu.VMEM(moments.shape, f32),
             pltpu.VMEM(moments.shape, f32),
             pltpu.VMEM((tiles, 4 * blocks, LANE), f32),
             pltpu.VMEM(field.shape, f32),
         ]
         + [pltpu.VMEM(w.shape, w.dtype) for w in weights]
-        + [dma((4, steps)), dma((steps,))]
-        + [dma((blocks - 1,))] * 4,
+        + [pltpu.VMEM((2 * variables, chunk + 8, LANE), f32)]
+        + [pltpu.VMEM((4, chunk + 8, LANE), f32)] * 3
+        + [pltpu.VMEM((4, chunk, LANE), f32)] * 3
+        + [dma((4, steps)), dma((tiles,))]
+        + [dma((blocks - 1,))] * 4
+        + [dma((4,)), dma((4,)), dma((3,)), dma((3,)), dma((3,)), dma((3,)), dma((4,)), dma((4,))],
         compiler_params=pltpu.CompilerParams(
-            vmem_limit_bytes=60 << 20, collective_id=1, has_side_effects=True
+            vmem_limit_bytes=60 << 20, collective_id=0, has_side_effects=True
         ),
         cost_estimate=cost(6 * rows * tiles * LANE * 3 * LANE, 60 << 20),
-        name="state_exchange",
-    )(field, moments, decay, *weights, *own_weights)
+        name="exchange",
+    )(field, moments, decay, table, *weights, *own_weights, vert, coef)
 
 
 def level_sweeps(rows, decay, starts):
@@ -568,267 +758,6 @@
         ends.append(state)
         rows = out
     return rows, ends
-
-
-def lat_states_kernel(row_count, groups, variables, source, decay, states, vert, coef, out, sums, field, sems, out_sem):
-    tiles = out.shape[0]
-    per_group = states.shape[0] // groups
-    levels = groups // variables
-    depth = tiles // 2 * row_count
-    size = sums.shape[0] // (2 * variables)
-
-    def fetch(ct):
-        return pltpu.make_async_copy(source.at[ct], field.at[ct], sems.at[ct])
-
-    for ct in range(tiles):
-        fetch(ct).start()
-
-    @pl.loop(0, tiles)
-    def _(ct):
-        fetch(ct).wait()
-        done = field.at[ct]
-        for first in range(0, groups // 8, SIDE):
-            octets = range(first, first + SIDE)
-            sets = [
-                [
-                    done[pl.ds(o * 8 * row_count + r, 8, stride=row_count), :]
-                    for r in range(row_count)
-                ]
-                for o in octets
-            ]
-            starts = [
-                [
-                    states[
-                        pl.ds(o * 8 * per_group + k * (per_group // 4) + ct, 8, stride=per_group), :
-                    ]
-                    for k in range(4)
-                ]
-                for o in octets
-            ]
-            sets, _ = lat_sweeps(sets, [decay_of_octet(decay, groups, o) for o in octets], starts)
-            for i, o in enumerate(octets):
-                for r in range(row_count):
-                    done[pl.ds(o * 8 * row_count + r, 8, stride=row_count), :] = sets[i][r]
-        pltpu.make_async_copy(done, out.at[ct], out_sem.at[ct]).start()
-        zero = jnp.zeros((8, LANE), f32)
-        side = lax.div(ct, tiles // 2)
-        spot = lax.rem(ct, tiles // 2)
-        for var in range(variables):
-            for t in range(row_count // 8):
-                rows = []
-                for lev in range(levels):
-                    base = (lev * variables + var) * row_count + t * 8
-                    rows.append(done[base : base + 8, :])
-                _, ends = level_sweeps(rows, lambda lev: vert[lev * variables + var], [zero, zero])
-                for k in range(2):
-                    start = (var * 2 + side) * size + k * depth + spot * row_count + t * 8
-                    sums[pl.ds(pl.multiple_of(start, 8), 8), :] = ends[k]
-
-    for target in range(2 * variables):
-        start = target * size + 2 * depth
-        sums[start : start + 8, :] = coef[target // 2]
-    for ct in range(tiles):
-        pltpu.make_async_copy(field.at[ct], out.at[ct], out_sem.at[ct]).wait()
-
-
-def lat_states(x, decay, states, vert, coef, row_count, groups, variables):
-    tiles, rows, _ = x.shape
-    size = 2 * variables * (tiles * row_count + 8)
-    whole = pl.BlockSpec(memory_space=pltpu.VMEM)
-    any_space = pl.BlockSpec(memory_space=pl.ANY)
-    return pl.pallas_call(
-        functools.partial(lat_states_kernel, row_count, groups, variables),
-        out_shape=(
-            jax.ShapeDtypeStruct((tiles, rows, LANE), f32),
-            jax.ShapeDtypeStruct((size, LANE), f32),
-        ),
-        in_specs=[any_space, whole, whole, pl.BlockSpec(memory_space=pltpu.SMEM), whole],
-        out_specs=(any_space, whole),
-        scratch_shapes=[
-            pltpu.VMEM((tiles, rows, LANE), f32),
-            pltpu.SemaphoreType.DMA((tiles,)),
-            pltpu.SemaphoreType.DMA((tiles,)),
-        ],
-        compiler_params=vmem(60),
-        cost_estimate=cost(0, 12 << 20),
-        name="lat_states",
-    )(x, decay, states, vert, coef)
-
-
-def level_exchange_kernel(sums, out, beside, merged, arrived, replies, entering, passed, *sems):
-    pair_send, pair_recv, hub_send, hub_recv, back_send, back_recv, last_send, last_recv = sems
-    band = lax.axis_index("band")
-    chip, core = band // 2, band % 2
-    depth = out.shape[1] // 2
-    tail = 2 * depth
-    mine_first = core * 4
-
-    def other(step):
-        return lax.rem(chip + step, 4) * 2 + core
-
-    def remote(src, dst, send, recv, target):
-        return pltpu.make_async_remote_copy(
-            src_ref=src,
-            dst_ref=dst,
-            send_sem=send,
-            recv_sem=recv,
-            device_id={"band": target},
-            device_id_type=pl.DeviceIdType.MESH,
-        )
-
-    sibling = chip * 2 + (1 - core)
-    barrier = pltpu.get_barrier_semaphore()
-    for target in [sibling] + [other(step) for step in (1, 2, 3)]:
-        pl.semaphore_signal(
-            barrier, inc=1, device_id={"band": target}, device_id_type=pl.DeviceIdType.MESH
-        )
-    pl.semaphore_wait(barrier, 4)
-
-    pair = remote(
-        sums.at[pl.ds((1 - core) * 4, 4)], beside, pair_send.at[0], pair_recv.at[0], sibling
-    )
-    pair.start()
-    pair.wait_recv()
-
-    def lower(a, b):
-        return jnp.where(core == 0, a, b)
-
-    def row(ref, chunk, at):
-        return jnp.broadcast_to(ref[chunk, at : at + 1, :], (8, LANE))
-
-    def bands_of(chunk, at):
-        a, b = sums[mine_first + chunk, at, :], beside[chunk, at, :]
-        return lower(a, b), lower(b, a)
-
-    def coefficients(chunk):
-        both = []
-        for at in (tail, tail + 1):
-            a, b = row(sums, mine_first + chunk, at), row(beside, chunk, at)
-            both.append((lower(a, b), lower(b, a)))
-        return both
-
-    def merge(chunk):
-        (full0, full1), (both0, both1) = coefficients(chunk)
-
-        @pl.loop(0, depth // 8)
-        def _(t):
-            at = pl.ds(pl.multiple_of(t * 8, 8), 8)
-            later = pl.ds(pl.multiple_of(depth + t * 8, 8), 8)
-            up0, up1 = bands_of(chunk, at)
-            down0, down1 = bands_of(chunk, later)
-            merged[chunk, at, :] = full1 * up0 + up1
-            merged[chunk, later, :] = down0 + full0 * (down1 + both1 * up0)
-
-        index = lax.broadcasted_iota(jnp.int32, (8, LANE), 0)
-        full = full0 * full1
-        both = both0 + full0 * both1 * full0
-        merged[chunk, tail : tail + 8, :] = jnp.where(index == 0, full, both)
-
-    sends = []
-    for step in (1, 2, 3):
-        chunk = lax.rem(chip + step, 4)
-        merge(chunk)
-        copy = remote(
-            merged.at[chunk], arrived.at[chip], hub_send.at[step - 1], hub_recv.at[step - 1], other(step)
-        )
-        copy.start()
-        sends.append(copy)
-    merge(chip)
-    arrived[chip] = merged[chip]
-    for copy in sends:
-        copy.wait_recv()
-
-    full = [row(arrived, c, tail) for c in range(4)]
-    both = [row(arrived, c, tail + 1) for c in range(4)]
-
-    @pl.loop(0, depth // 8)
-    def _(t):
-        at = pl.ds(pl.multiple_of(t * 8, 8), 8)
-        later = pl.ds(pl.multiple_of(depth + t * 8, 8), 8)
-        state = jnp.zeros((8, LANE), f32)
-        ups = []
-        for c in range(4):
-            ups.append(state)
-            replies[c, at, :] = state
-            state = full[c] * state + arrived[c, at, :]
-        state = jnp.zeros((8, LANE), f32)
-        for c in (3, 2, 1, 0):
-            replies[c, later, :] = state
-            state = full[c] * state + (arrived[c, later, :] + both[c] * ups[c])
-
-    backs = []
-    for step in (1, 2, 3):
-        copy = remote(
-            replies.at[lax.rem(chip + step, 4)],
-            entering.at[chip],
-            back_send.at[step - 1],
-            back_recv.at[step - 1],
-            other(step),
-        )
-        copy.start()
-        backs.append(copy)
-    entering[chip] = replies[chip]
-    for copy in backs:
-        copy.wait_recv()
-
-    for chunk in range(4):
-        (full0, full1), (both0, both1) = coefficients(chunk)
-
-        @pl.loop(0, depth // 8)
-        def _(t):
-            at = pl.ds(pl.multiple_of(t * 8, 8), 8)
-            later = pl.ds(pl.multiple_of(depth + t * 8, 8), 8)
-            up0, _ = bands_of(chunk, at)
-            _, down1 = bands_of(chunk, later)
-            first = entering[chunk, at, :]
-            last = entering[chunk, later, :]
-            middle = full0 * first + up0
-            turned = full1 * last + (down1 + both1 * middle)
-            out[mine_first + chunk, at, :] = lower(first, middle)
-            out[mine_first + chunk, later, :] = lower(turned, last)
-            passed[chunk, at, :] = lower(middle, first)
-            passed[chunk, later, :] = lower(last, turned)
-
-    final = remote(passed, out.at[pl.ds(mine_first, 4)], last_send.at[0], last_recv.at[0], sibling)
-    final.start()
-    pair.wait_send()
-    for copy in sends + backs:
-        copy.wait_send()
-    final.wait()
-
-
-def level_exchange(sums):
-    bands, size, _ = sums.shape
-    depth = (size - 8) // 2
-    whole = pl.BlockSpec(memory_space=pltpu.VMEM)
-    dma = pltpu.SemaphoreType.DMA
-    return pl.pallas_call(
-        level_exchange_kernel,
-        out_shape=jax.ShapeDtypeStruct((bands, 2 * depth, LANE), f32),
-        in_specs=[whole],
-        out_specs=whole,
-        scratch_shapes=[
-            pltpu.VMEM((4, size, LANE), f32),
-            pltpu.VMEM((4, size, LANE), f32),
-            pltpu.VMEM((4, size, LANE), f32),
-            pltpu.VMEM((4, 2 * depth, LANE), f32),
-            pltpu.VMEM((4, 2 * depth, LANE), f32),
-            pltpu.VMEM((4, 2 * depth, LANE), f32),
-            dma((1,)),
-            dma((1,)),
-            dma((3,)),
-            dma((3,)),
-            dma((3,)),
-            dma((3,)),
-            dma((1,)),
-            dma((1,)),
-        ],
-        compiler_params=pltpu.CompilerParams(
-            vmem_limit_bytes=60 << 20, collective_id=0, has_side_effects=True
-        ),
-        cost_estimate=cost(0, 3 << 20),
-        name="level_exchange",
-    )(sums)
 
 
 def level_states_kernel(source, vert, states, out, x, result, in_sem, sem):
@@ -934,13 +863,18 @@
     quarters = (places & 3).astype(f32).reshape(sub_count, 4, capacity // 4)
     quarters = jnp.pad(quarters, ((0, 0), (0, 4), (0, 0)))
     forced, moments = force(places >> 2, got, quarters, tile_field, decay, row_count, groups)
-    smooth, states = state_exchange(
-        forced, moments.reshape(sub_count, 4 * tiles, LANE), hub_lat, weights, own_weights, row_count
+    smooth, entering = exchange(
+        forced,
+        moments.reshape(sub_count, 4 * tiles, LANE),
+        hub_lat,
+        decay,
+        weights,
+        own_weights,
+        vert_decay,
+        coef,
+        row_count,
+        var_count,
     )
-    smooth, sums = lat_states(
-        smooth, decay, states.reshape(-1, LANE), vert_decay, coef, row_count, groups, var_count
-    )
-    entering = level_exchange(sums.reshape(band_count, -1, LANE))
     return level_states(
         smooth,
         vert_decay,

time: 183 us -> 166 us (0.907)
  Pallas kernels: 133 us -> 114 us
    pallas_call x1, Pallas kernels: 29.3 us -> 19.7 us  [force(): pl.pallas_call(functools.partial(forced_kernel, row_count, groups), out_s...]
    pallas_call x3 -> x1, Pallas kernels: 89.3 us -> 80.6 us  [exchange(): pl.pallas_call(functools.partial(exchange_kernel, row_count, variables),...]
  transfers between devices with their start and end apart: 1 -> 1, of which waited for: 1 -> 1; matrix products, arithmetic and copies ran while one was open for 8% -> 9% of each run, Pallas kernels for 0% -> 0%
where the time goes in v6:
time: 166 us; the launch traced here: 164 us
  Pallas kernels  114 us (69%)
  local copies, waits for them, and re-layouts  14.6 us (9%)
  other arithmetic  12.8 us (8%)
  starting transfers between devices  12.1 us (7%)
  waiting for transfers between devices  8.54 us (5%)
    pallas_call x1, Pallas kernels, exchange(): pl.pallas_call(functools.partial(exchange_kernel, row_count, variables),...  80.6 us
    pallas_call x1, Pallas kernels, force(): pl.pallas_call(functools.partial(forced_kernel, row_count, groups), out_s...  19.7 us
    all_to_all x1, starting transfers between devices, per_device(): lax.all_to_all(message.reshape(sub_count, -1, LANE), 'sub', 0, 0, tiled=T...  12.1 us
    pallas_call x1, Pallas kernels, pack(): pl.pallas_call(pack_kernel, out_shape=jax.ShapeDtypeStruct((targets * 72,...  8.95 us
    all_to_all x1, waiting for transfers between devices, per_device(): lax.all_to_all(message.reshape(sub_count, -1, LANE), 'sub', 0, 0, tiled=T...  8.54 us
    convert_element_type x3, other arithmetic, thirds(): high = high.astype(bf16)  5.25 us
    pallas_call x1, Pallas kernels, level_states(): pl.pallas_call(level_states_kernel, out_shape=jax.ShapeDtypeStruct(shape,...  5.05 us
    unnamed x16, local copies, waits for them, and re-layouts  4.13 us
  transfers between devices with their start and end apart: 1, of which 1 were waited for; matrix products, arithmetic and copies ran while one was open for 9% of the time, Pallas kernels for 0%

profile of v6, /device:TPU:1, one launch (start us, length us, event | category | flops | bytes accessed | tf_op | source)
XLA Modules:
  0.0 163.9 jit_solution(6132242883085594689)
XLA Ops:
  0.0 0.7 broadcast_multiply_fusion.1
  0.7 0.9 convert_reduce_fusion
  1.7 0.1 reduce_window_sum.11
  1.7 1.1 fusion.7
  2.8 0.8 fusion.23
  3.6 0.6 bitcast_add_fusion.slots
  4.2 1.5 stack.17.table
  5.7 9.0 %pack.1 = f32[2304,128]{1,0:T(8,128)} custom-call(s32[4096]{0:T(1024)} %bitcast_add_fusion.slots, s32[8,4096]{1,0:T(8,128)} %stack.17.table, f32[8,4,4096]{2,1,0:T(4,128)} %values.1), custom_call_target="tpu_custom_call" | custom-call | bytes 4194304 | tf_op jit(solution)/shard_map/pack/pallas_call | solution.py:92
  14.7 12.1 %all-to-all-start = ((f32[32,72,128]{2,1,0:T(8,128)}), f32[32,72,128]{2,1,0:T(8,128)}, u32[]{:S(2)}, u32[]{:S(2)}) async-start(f32[32,72,128]{2,1,0:T(8,128)} %bitcast.146), calls=%async_computation | async-start | bytes 2359296 | tf_op jit(solution)/shard_map/all_to_all | solution.py:843
  26.9 0.1 divide_exponential_fusion.2
  27.0 0.4 reshape.1419
  27.4 0.3 slice_reduce_fusion.7
  27.7 0.1 copy.27
  27.8 0.1 broadcast_in_dim_reshape.3
  27.9 0.1 copy.31
  28.0 0.1 reshape.1420
  28.1 0.1 add.320
  28.2 0.2 add_multiply_fusion.1
  28.3 0.6 reduce-precision_convert_fusion.1
  28.9 0.3 pad_maximum_fusion.2.back
  29.2 0.7 constant_dynamic-slice_fusion.2.own_back
  29.9 0.1 fusion.11
  30.0 0.1 divide_exponential_fusion.6
  30.1 0.1 fusion.17
  30.4 0.1 copy.33
  30.4 0.6 reshape.1422.vert
  31.0 0.1 copy.35
  31.1 0.1 copy.32
  31.2 0.6 pad.23.decay
  31.8 2.0 %copy.28 = f32[32,128,4]{2,1,0:T(8,128)} copy(f32[32,128,4]{1,0,2:T(8,128)S(1)} %pad_maximum_fusion.3) | data formatting | bytes 131072 | tf_op jit(solution)/shard_map/concatenate | solution.py:284
  33.8 0.1 fusion.19
  34.0 3.7 %reduce-precision_convert_fusion.2 = (bf16[32,128,128]{2,1,0:T(8,128)(2,1)S(1)}, bf16[32,128,128]{2,1,0:T(8,128)(2,1)S(1)}, f32[32,128,128]{2,1,0:T(8,128)S(1)}) fusion(pred[128,128]{1,0:T(8,128)(4,1)S(1)} %get-tuple-element.54, f32[32]{0:T(128)S(1)} %exponential-minus-one_negate_fusion, f32[32]{0:T(128)S(1)} %broadcast_in_dim_reshape.3, ...), kind=kLoop, calls=%fused_computation.11 | loop fusion | flops 7340032 | bytes 4489856 | tf_op jit(solution)/shard_map/convert_element_type | solution.py:319
  37.7 0.3 pad_maximum_fusion.1.mix
  38.0 0.6 constant_dynamic-slice_fusion.3.own_mix
  38.7 1.3 copy-done.3
  39.9 1.0 reduce-precision_convert_fusion
  41.0 1.4 pad_maximum_fusion.first
  42.4 2.7 %copy-done = bf16[32,384,256]{2,1,0:T(8,128)(2,1)} copy-done((bf16[32,384,256]{2,1,0:T(8,128)(2,1)}, bf16[32,384,256]{2,1,0:T(8,128)(2,1)S(1)}, u32[]{:S(2)}) %copy-start) | copy-done | bytes 6291480
  45.1 0.7 constant_dynamic-slice_fusion.4.own_first
  45.8 8.5 %all-to-all-done.got = f32[32,72,128]{2,1,0:T(8,128)} async-done(((f32[32,72,128]{2,1,0:T(8,128)}), f32[32,72,128]{2,1,0:T(8,128)}, u32[]{:S(2)}, u32[]{:S(2)}) %all-to-all-start) | async-done | bytes 1179680 | tf_op jit(solution)/shard_map/all_to_all | solution.py:843
  54.3 1.5 and_convert_fusion
  55.8 0.1 convert_element_type.91
  55.9 0.7 pad.22.quarters
  56.6 1.1 broadcast_in_dim.41.decay.table
  57.7 19.7 %force.1 = (f32[12,768,128]{2,1,0:T(8,128)}, f32[1536,128]{1,0:T(8,128)}) custom-call(s32[8192]{0:T(1024)} %bitcast.154, f32[32,72,128]{2,1,0:T(8,128)} %all-to-all-done.got, f32[32,8,64]{2,1,0:T(8,128)} %pad.22.quarters, f32[768,1536]{1,0:T(8,128)} %bitcast.148, f32[1536,128]{1,0:T(8,128)} %broadcast_in_dim.41.decay.table), custom_call_target="tpu_custom_call" | custom-call | bytes 16777216 | tf_op jit(solution)/shard_map/force/pallas_call | solution.py:243
  77.4 0.7 broadcast_in_dim.42.coef
  78.1 80.6 %exchange.1 = (f32[12,768,128]{2,1,0:T(8,128)}, f32[8,288,128]{2,1,0:T(8,128)}) custom-call(f32[12,768,128]{2,1,0:T(8,128)} %get-tuple-element.17.field, f32[32,48,128]{2,1,0:T(8,128)} %bitcast.150, f32[24,128]{1,0:T(8,128)} %pad.23.decay, f32[1536,128]{1,0:T(8,128)} %broadcast_in_dim.41.decay.table, bf16[32,384,256]{2,1,0:T(8,128)(2,1)} %copy-done, ...), custom_call_target="tpu_custom_call" | custom-call | flops 2717908992 | bytes 62914560 | tf_op jit(solution)/shard_map/exchange/pallas_call | solution.py:715
  158.7 5.1 %level_states.1 = f32[8,4,24,1536]{3,2,1,0:T(8,128)} custom-call(f32[12,8,4,24,128]{4,3,2,1,0:T(8,128)} %bitcast.147, f32[32]{0:T(128)} %reshape.1422.vert, f32[4,2,2,6,24,128]{5,4,3,2,1,0:T(8,128)} %bitcast.149), custom_call_target="tpu_custom_call" | custom-call | bytes 11534336 | tf_op jit(solution)/shard_map/level_states/pallas_call | solution.py:794
  (36 shorter events, 0.3 us)
Async XLA Ops:
  5.7 21.2 %copy-start.4 = (f32[8,4,768]{2,1,0:T(4,128)S(1)}, f32[8,4,768]{2,1,0:T(4,128)}, u32[]{:S(2)}) copy-start(f32[8,4,768]{2,1,0:T(4,128)} %param.11) | copy-start | bytes 294916
  14.7 12.7 %copy-start.6 = (f32[8,4]{0,1:T(4,128)S(1)}, f32[8,4]{0,1:T(4,128)}, u32[]{:S(2)}) copy-start(f32[8,4]{0,1:T(4,128)} %param.13) | copy-start | bytes 388
  14.7 13.1 %copy-start.5 = (f32[8,4]{0,1:T(4,128)S(1)}, f32[8,4]{0,1:T(4,128)}, u32[]{:S(2)}) copy-start(f32[8,4]{0,1:T(4,128)} %param.12) | copy-start | bytes 388
  14.7 39.6 %all-to-all-start = ((f32[32,72,128]{2,1,0:T(8,128)}), f32[32,72,128]{2,1,0:T(8,128)}, u32[]{:S(2)}, u32[]{:S(2)}) async-start(f32[32,72,128]{2,1,0:T(8,128)} %bitcast.146), calls=%async_computation | async-start | bytes 2359296 | tf_op jit(solution)/shard_map/all_to_all | solution.py:843
  29.2 8.5 %copy-start.1 = (bf16[32,384,128]{2,1,0:T(8,128)(2,1)}, bf16[32,384,128]{2,1,0:T(8,128)(2,1)S(1)}, u32[]{:S(2)}) copy-start(bf16[32,384,128]{2,1,0:T(8,128)(2,1)S(1)} %pad_maximum_fusion.2.back) | copy-start | bytes 9437188
  37.7 2.3 %copy-start.3 = (f32[32,128,4]{2,1,0:T(8,128)S(1)}, f32[32,128,4]{2,1,0:T(8,128)}, u32[]{:S(2)}) copy-start(f32[32,128,4]{2,1,0:T(8,128)} %copy.28) | copy-start | bytes 196612
  38.0 3.0 %copy-start.2 = (bf16[32,384,128]{2,1,0:T(8,128)(2,1)}, bf16[32,384,128]{2,1,0:T(8,128)(2,1)S(1)}, u32[]{:S(2)}) copy-start(bf16[32,384,128]{2,1,0:T(8,128)(2,1)S(1)} %pad_maximum_fusion.1.mix) | copy-start | bytes 9437188
  42.4 2.7 %copy-start = (bf16[32,384,256]{2,1,0:T(8,128)(2,1)}, bf16[32,384,256]{2,1,0:T(8,128)(2,1)S(1)}, u32[]{:S(2)}) copy-start(bf16[32,384,256]{2,1,0:T(8,128)(2,1)S(1)} %pad_maximum_fusion.first) | copy-start | bytes 18874372

commit v7 on v6

--- a/solution.py
+++ b/solution.py
@@ -34,39 +34,41 @@
     return rank.reshape(count).astype(jnp.int32)
 
 
-def pack_kernel(slots, table, values, packed, rows, big):
+def pack_kernel(slots, slot_row, place_row, values, packed, rows, big):
     levels, _, count = values.shape
     total = big.shape[0]
     targets = total // 256
     size = packed.shape[0] // targets
-
-    @pl.loop(0, total // 64)
-    def _(i):
-        big[pl.ds(pl.multiple_of(i * 64, 64), 64), :] = jnp.zeros((64, LANE), f32)
+    share = total // (count // LANE)
 
     for j in range(count // LANE):
+        big[j * share : (j + 1) * share, :] = jnp.zeros((share, LANE), f32)
         part = jnp.concatenate(
             [values[lev, :, j * LANE : (j + 1) * LANE] for lev in range(levels)], axis=0
         )
         rows[j * LANE : (j + 1) * LANE, :] = jnp.concatenate([part] * 4, axis=0).T
 
-    owner, rank, place = table[0:1, :], table[1:2, :], table[2:3, :]
+    slot, place = slot_row[...], place_row[...]
+    owner, rank = lax.shift_right_logical(slot, 8), slot & 255
     mine = owner == lax.broadcasted_iota(jnp.int32, (targets, count), 0)
     spot = (rank == lax.broadcasted_iota(jnp.int32, (256, count), 0)).astype(f32).astype(bf16)
 
     def put(half):
-        left = jnp.where(mine, half, 0).astype(f32).astype(bf16)
-        return lax.dot_general(
-            left, spot, (((1,), (1,)), ((), ())), preferred_element_type=f32
-        )
-
-    cells = put(lax.shift_right_logical(place, 8)) * 256.0 + put(place & 255)
+        return jnp.where(mine, half, 0).astype(f32).astype(bf16)
+
+    both = lax.dot_general(
+        jnp.concatenate([put(lax.shift_right_logical(place, 8)), put(place & 255)], axis=0),
+        spot,
+        (((1,), (1,)), ((), ())),
+        preferred_element_type=f32,
+    )
+    cells = both[:targets] * 256.0 + both[targets:]
     for half in range(2):
         packed[pl.ds(64 + half, targets, stride=size), :] = cells[:, half * LANE : (half + 1) * LANE]
     for extra in range(66, size):
         packed[pl.ds(extra, targets, stride=size), :] = jnp.zeros((targets, LANE), f32)
 
-    step = 16
+    step = PACK_STEP
 
     @pl.loop(0, count // step)
     def _(i):
@@ -76,29 +78,35 @@
 
     quarter = lax.broadcasted_iota(jnp.int32, (64, LANE), 1) // 32
 
-    @pl.loop(0, targets)
-    def _(d):
-        start = pl.multiple_of(d * 256, 256)
-        out = big[pl.ds(start, 64), :]
-        for k in range(1, 4):
-            out = jnp.where(quarter == k, big[pl.ds(start + 64 * k, 64), :], out)
-        packed[pl.ds(pl.multiple_of(d * size, 8), 64), :] = out
-
-
-def pack(slots, table, values, targets):
+    @pl.loop(0, targets // PACK_SIDE)
+    def _(i):
+        for e in range(PACK_SIDE):
+            d = i * PACK_SIDE + e
+            start = pl.multiple_of(d * 256, 256)
+            out = big[pl.ds(start, 64), :]
+            for k in range(1, 4):
+                out = jnp.where(quarter == k, big[pl.ds(start + 64 * k, 64), :], out)
+            packed[pl.ds(pl.multiple_of(d * size, 8), 64), :] = out
+
+
+PACK_STEP = 64
+PACK_SIDE = 8
+
+
+def pack(slots, place, values, targets):
     count = values.shape[2]
     total = targets * 256
     whole = pl.BlockSpec(memory_space=pltpu.VMEM)
     return pl.pallas_call(
         pack_kernel,
         out_shape=jax.ShapeDtypeStruct((targets * 72, LANE), f32),
-        in_specs=[pl.BlockSpec(memory_space=pltpu.SMEM), whole, whole],
+        in_specs=[pl.BlockSpec(memory_space=pltpu.SMEM), whole, whole, whole],
         out_specs=whole,
         scratch_shapes=[pltpu.VMEM((count, LANE), f32), pltpu.VMEM((total, LANE), f32)],
         compiler_params=vmem(60),
         cost_estimate=cost(0, 4 << 20),
         name="pack",
-    )(slots, table, values)
+    )(slots, slots.reshape(1, count), place.reshape(1, count), values)
 
 
 def lat_sweeps(sets, decays, starts):
@@ -467,13 +475,12 @@
         outward(step).start()
 
     arrived[me] = moments[me]
+    full, t21, t31, t41, t32, t42 = hub_coefficients(decay)
     lon_steps(0, steps // 2)
 
     @pl.loop(1, blocks)
     def _(step):
         outward(step).wait_recv()
-
-    full, t21, t31, t41, t32, t42 = hub_coefficients(decay)
 
     def at(table, d):
         return jnp.broadcast_to(table[:, d : d + 1], (tiles, LANE))
@@ -837,9 +844,8 @@
     ranks = route_ranks(owners, sub_count)
     row, column = obs_cell // lon_count, obs_cell % lon_count
     place = ((row // 4) * lon_count + column) * 4 + row % 4
-    table = jnp.stack([owners, ranks, place] + [jnp.zeros_like(place)] * 5)
     lines = capacity // LANE
-    message = pack(owners * capacity + ranks, table, obs_columns, sub_count)
+    message = pack(owners * capacity + ranks, place, obs_columns, sub_count)
     got = lax.all_to_all(message.reshape(sub_count, -1, LANE), "sub", 0, 0, tiled=True)
 
     vert_decay = jnp.exp(-1.0 / vert_length)
@@ -858,7 +864,8 @@
     weights = lon_weights(lengths, lon_count)
     own_weights = [lax.dynamic_slice_in_dim(w, sub_index, 1, 0) for w in weights]
 
-    got, weights, own_weights = lax.optimization_barrier((got, weights, own_weights))
+    ready = (got, weights, own_weights, decay, hub_lat, coef, vert_decay)
+    got, weights, own_weights, decay, hub_lat, coef, vert_decay = lax.optimization_barrier(ready)
     places = got[:, capacity // 4 : capacity // 4 + lines, :].reshape(-1).astype(jnp.int32)
     quarters = (places & 3).astype(f32).reshape(sub_count, 4, capacity // 4)
     quarters = jnp.pad(quarters, ((0, 0), (0, 4), (0, 0)))

time: 166 us -> 163 us (0.982)
  Pallas kernels: 114 us -> 112 us
  other arithmetic: 12.8 us -> 14.7 us
    pallas_call x1, Pallas kernels: 80.6 us -> 78.4 us  [exchange(): pl.pallas_call(functools.partial(exchange_kernel, row_count, variables),...]
    pallas_call x1, Pallas kernels: 8.95 us -> 6.94 us  [pack(): pl.pallas_call(pack_kernel, out_shape=jax.ShapeDtypeStruct((targets * 72,...]
    pallas_call x1, Pallas kernels: 19.7 us -> 21.6 us  [force(): pl.pallas_call(functools.partial(forced_kernel, row_count, groups), out_s...]
where the time goes in v7:
time: 163 us; the launch traced here: 162 us
  Pallas kernels  112 us (69%)
  other arithmetic  14.7 us (9%)
  local copies, waits for them, and re-layouts  13.1 us (8%)
  starting transfers between devices  12 us (7%)
  waiting for transfers between devices  8.54 us (5%)
    pallas_call x1, Pallas kernels, exchange(): pl.pallas_call(functools.partial(exchange_kernel, row_count, variables),...  78.4 us
    pallas_call x1, Pallas kernels, force(): pl.pallas_call(functools.partial(forced_kernel, row_count, groups), out_s...  21.6 us
    all_to_all x1, starting transfers between devices, per_device(): lax.all_to_all(message.reshape(sub_count, -1, LANE), 'sub', 0, 0, tiled=T...  12 us
    all_to_all x1, waiting for transfers between devices, per_device(): lax.all_to_all(message.reshape(sub_count, -1, LANE), 'sub', 0, 0, tiled=T...  8.54 us
    pallas_call x1, Pallas kernels, pack(): pl.pallas_call(pack_kernel, out_shape=jax.ShapeDtypeStruct((targets * 72,...  6.94 us
    convert_element_type x3, other arithmetic, thirds(): high = high.astype(bf16)  5.25 us
    pallas_call x1, Pallas kernels, level_states(): pl.pallas_call(level_states_kernel, out_shape=jax.ShapeDtypeStruct(shape,...  5.05 us
    unnamed x16, local copies, waits for them, and re-layouts  4.13 us
  transfers between devices with their start and end apart: 1, of which 1 were waited for; matrix products, arithmetic and copies ran while one was open for 9% of the time, Pallas kernels for 0%

profile of v7, /device:TPU:1, one launch (start us, length us, event | category | flops | bytes accessed | tf_op | source)
XLA Modules:
  0.0 162.0 jit_solution(4151992898175624847)
XLA Ops:
  0.0 0.7 broadcast_multiply_fusion.1
  0.7 0.9 convert_reduce_fusion
  1.7 0.1 reduce_window_sum.11
  1.7 1.1 fusion.7
  2.8 1.3 bitcast_add_fusion.slot_row
  4.2 1.4 fusion.23
  5.5 0.6 bitcast_add_fusion.1.slots
  6.1 6.9 %pack.1 = f32[2304,128]{1,0:T(8,128)} custom-call(s32[4096]{0:T(1024)} %bitcast_add_fusion.1.slots, s32[1,4096]{1,0:T(1,128)} %bitcast_add_fusion.slot_row, s32[1,4096]{1,0:T(1,128)} %bitcast.155, f32[8,4,4096]{2,1,0:T(4,128)} %values.1), custom_call_target="tpu_custom_call" | custom-call | bytes 4194304 | tf_op jit(solution)/shard_map/pack/pallas_call | solution.py:100
  13.1 12.0 %all-to-all-start = ((f32[32,72,128]{2,1,0:T(8,128)}), f32[32,72,128]{2,1,0:T(8,128)}, u32[]{:S(2)}, u32[]{:S(2)}) async-start(f32[32,72,128]{2,1,0:T(8,128)} %bitcast.148), calls=%async_computation | async-start | bytes 2359296 | tf_op jit(solution)/shard_map/all_to_all | solution.py:849
  25.2 0.1 divide_exponential_fusion.2
  25.2 0.4 reshape.1438
  25.7 0.3 slice_reduce_fusion.7
  26.0 0.1 copy.27
  26.1 0.1 broadcast_in_dim_reshape.3
  26.2 0.1 copy.31
  26.3 0.1 reshape.1439
  26.4 0.1 add.323
  26.4 0.2 add_multiply_fusion.1
  26.6 0.6 reduce-precision_convert_fusion.1
  27.2 0.3 pad_maximum_fusion.2.back
  27.5 0.7 constant_dynamic-slice_fusion.2.own_back
  28.2 0.1 fusion.11
  28.3 0.1 divide_exponential_fusion.6
  28.4 0.1 fusion.17
  28.6 0.1 copy.34
  28.7 0.6 reshape.1440.vert
  29.3 0.1 copy.35
  29.4 0.1 copy.32
  29.5 0.6 pad.22.decay
  30.1 2.0 %copy.28 = f32[32,128,4]{2,1,0:T(8,128)} copy(f32[32,128,4]{1,0,2:T(8,128)S(1)} %pad_maximum_fusion.3) | data formatting | bytes 131072 | tf_op jit(solution)/shard_map/concatenate | solution.py:292
  32.1 0.1 fusion.19
  32.3 3.7 %reduce-precision_convert_fusion.2 = (bf16[32,128,128]{2,1,0:T(8,128)(2,1)S(1)}, bf16[32,128,128]{2,1,0:T(8,128)(2,1)S(1)}, f32[32,128,128]{2,1,0:T(8,128)S(1)}) fusion(pred[128,128]{1,0:T(8,128)(4,1)S(1)} %get-tuple-element.62, f32[32]{0:T(128)S(1)} %exponential-minus-one_negate_fusion, f32[32]{0:T(128)S(1)} %broadcast_in_dim_reshape.3, ...), kind=kLoop, calls=%fused_computation.11 | loop fusion | flops 7340032 | bytes 4489856 | tf_op jit(solution)/shard_map/convert_element_type | solution.py:327
  36.0 0.3 pad_maximum_fusion.1.mix
  36.3 0.6 constant_dynamic-slice_fusion.3.own_mix
  37.0 1.3 copy-done.3
  38.2 1.0 reduce-precision_convert_fusion
  39.3 1.4 pad_maximum_fusion.first
  40.7 2.7 %copy-done = bf16[32,384,256]{2,1,0:T(8,128)(2,1)} copy-done((bf16[32,384,256]{2,1,0:T(8,128)(2,1)}, bf16[32,384,256]{2,1,0:T(8,128)(2,1)S(1)}, u32[]{:S(2)}) %copy-start) | copy-done | bytes 6291480
  43.4 0.7 constant_dynamic-slice_fusion.4.own_first
  44.0 8.5 %all-to-all-done.got = f32[32,72,128]{2,1,0:T(8,128)} async-done(((f32[32,72,128]{2,1,0:T(8,128)}), f32[32,72,128]{2,1,0:T(8,128)}, u32[]{:S(2)}, u32[]{:S(2)}) %all-to-all-start) | async-done | bytes 1179680 | tf_op jit(solution)/shard_map/all_to_all | solution.py:849
  52.6 0.7 broadcast_in_dim.42.coef
  53.2 1.1 broadcast_in_dim.41.decay.table
  54.4 1.5 and_convert_fusion
  55.9 0.1 convert_element_type.91
  56.0 0.7 pad.24.quarters
  56.7 21.6 %force.1 = (f32[12,768,128]{2,1,0:T(8,128)}, f32[1536,128]{1,0:T(8,128)}) custom-call(s32[8192]{0:T(1024)} %bitcast.154, f32[32,72,128]{2,1,0:T(8,128)} %all-to-all-done.got, f32[32,8,64]{2,1,0:T(8,128)} %pad.24.quarters, f32[768,1536]{1,0:T(8,128)} %bitcast.149, f32[1536,128]{1,0:T(8,128)} %broadcast_in_dim.41.decay.table), custom_call_target="tpu_custom_call" | custom-call | bytes 16777216 | tf_op jit(solution)/shard_map/force/pallas_call | solution.py:251
  78.4 78.4 %exchange.1 = (f32[12,768,128]{2,1,0:T(8,128)}, f32[8,288,128]{2,1,0:T(8,128)}) custom-call(f32[12,768,128]{2,1,0:T(8,128)} %get-tuple-element.22.field, f32[32,48,128]{2,1,0:T(8,128)} %bitcast.151, f32[24,128]{1,0:T(8,128)} %pad.22.decay, f32[1536,128]{1,0:T(8,128)} %broadcast_in_dim.41.decay.table, bf16[32,384,256]{2,1,0:T(8,128)(2,1)} %copy-done, ...), custom_call_target="tpu_custom_call" | custom-call | flops 2717908992 | bytes 62914560 | tf_op jit(solution)/shard_map/exchange/pallas_call | solution.py:722
  156.7 5.1 %level_states.1 = f32[8,4,24,1536]{3,2,1,0:T(8,128)} custom-call(f32[12,8,4,24,128]{4,3,2,1,0:T(8,128)} %bitcast.147, f32[32]{0:T(128)} %reshape.1440.vert, f32[4,2,2,6,24,128]{5,4,3,2,1,0:T(8,128)} %bitcast.150), custom_call_target="tpu_custom_call" | custom-call | bytes 11534336 | tf_op jit(solution)/shard_map/level_states/pallas_call | solution.py:801
  (34 shorter events, 0.3 us)
Async XLA Ops:
  5.5 19.7 %copy-start.4 = (f32[8,4,768]{2,1,0:T(4,128)S(1)}, f32[8,4,768]{2,1,0:T(4,128)}, u32[]{:S(2)}) copy-start(f32[8,4,768]{2,1,0:T(4,128)} %param.11) | copy-start | bytes 294916
  6.1 19.6 %copy-start.6 = (f32[8,4]{0,1:T(4,128)S(1)}, f32[8,4]{0,1:T(4,128)}, u32[]{:S(2)}) copy-start(f32[8,4]{0,1:T(4,128)} %param.13) | copy-start | bytes 388
  6.1 19.9 %copy-start.5 = (f32[8,4]{0,1:T(4,128)S(1)}, f32[8,4]{0,1:T(4,128)}, u32[]{:S(2)}) copy-start(f32[8,4]{0,1:T(4,128)} %param.12) | copy-start | bytes 388
  13.1 39.5 %all-to-all-start = ((f32[32,72,128]{2,1,0:T(8,128)}), f32[32,72,128]{2,1,0:T(8,128)}, u32[]{:S(2)}, u32[]{:S(2)}) async-start(f32[32,72,128]{2,1,0:T(8,128)} %bitcast.148), calls=%async_computation | async-start | bytes 2359296 | tf_op jit(solution)/shard_map/all_to_all | solution.py:849
  27.4 8.5 %copy-start.1 = (bf16[32,384,128]{2,1,0:T(8,128)(2,1)}, bf16[32,384,128]{2,1,0:T(8,128)(2,1)S(1)}, u32[]{:S(2)}) copy-start(bf16[32,384,128]{2,1,0:T(8,128)(2,1)S(1)} %pad_maximum_fusion.2.back) | copy-start | bytes 9437188
  36.0 2.3 %copy-start.3 = (f32[32,128,4]{2,1,0:T(8,128)S(1)}, f32[32,128,4]{2,1,0:T(8,128)}, u32[]{:S(2)}) copy-start(f32[32,128,4]{2,1,0:T(8,128)} %copy.28) | copy-start | bytes 196612
  36.3 3.0 %copy-start.2 = (bf16[32,384,128]{2,1,0:T(8,128)(2,1)}, bf16[32,384,128]{2,1,0:T(8,128)(2,1)S(1)}, u32[]{:S(2)}) copy-start(bf16[32,384,128]{2,1,0:T(8,128)(2,1)S(1)} %pad_maximum_fusion.1.mix) | copy-start | bytes 9437188
  40.7 2.7 %copy-start = (bf16[32,384,256]{2,1,0:T(8,128)(2,1)}, bf16[32,384,256]{2,1,0:T(8,128)(2,1)S(1)}, u32[]{:S(2)}) copy-start(bf16[32,384,256]{2,1,0:T(8,128)(2,1)S(1)} %pad_maximum_fusion.first) | copy-start | bytes 18874372

commit v8 on v7

--- a/solution.py
+++ b/solution.py
@@ -65,8 +65,6 @@
     cells = both[:targets] * 256.0 + both[targets:]
     for half in range(2):
         packed[pl.ds(64 + half, targets, stride=size), :] = cells[:, half * LANE : (half + 1) * LANE]
-    for extra in range(66, size):
-        packed[pl.ds(extra, targets, stride=size), :] = jnp.zeros((targets, LANE), f32)
 
     step = PACK_STEP
 
@@ -80,13 +78,13 @@
 
     @pl.loop(0, targets // PACK_SIDE)
     def _(i):
+        run = packed.at[pl.ds(pl.multiple_of(i * PACK_SIDE * size, 8), PACK_SIDE * size), :]
         for e in range(PACK_SIDE):
-            d = i * PACK_SIDE + e
-            start = pl.multiple_of(d * 256, 256)
+            start = pl.multiple_of((i * PACK_SIDE + e) * 256, 256)
             out = big[pl.ds(start, 64), :]
             for k in range(1, 4):
                 out = jnp.where(quarter == k, big[pl.ds(start + 64 * k, 64), :], out)
-            packed[pl.ds(pl.multiple_of(d * size, 8), 64), :] = out
+            run[e * size : e * size + 64, :] = out
 
 
 PACK_STEP = 64
@@ -99,7 +97,7 @@
     whole = pl.BlockSpec(memory_space=pltpu.VMEM)
     return pl.pallas_call(
         pack_kernel,
-        out_shape=jax.ShapeDtypeStruct((targets * 72, LANE), f32),
+        out_shape=jax.ShapeDtypeStruct((targets * 66, LANE), f32),
         in_specs=[pl.BlockSpec(memory_space=pltpu.SMEM), whole, whole, whole],
         out_specs=whole,
         scratch_shapes=[pltpu.VMEM((count, LANE), f32), pltpu.VMEM((total, LANE), f32)],
@@ -141,10 +139,11 @@
 SIDE = 1
 
 
-def forced_kernel(row_count, groups, places, got, quarters, background, decay, forced, moments, spread, field, sem, out_sem, *chains):
+def forced_kernel(row_count, groups, places, got, background, decay, forced, moments, spread, field, sem, out_sem, *chains):
     total = spread.shape[0]
     depth = chains[0].shape[0]
-    sources = got.shape[0]
+    sources = spread.shape[0] // 256
+    size = got.shape[0] // sources
     tiles = forced.shape[0]
     fetches = [
         pltpu.make_async_copy(
@@ -156,7 +155,7 @@
         fetch.start()
 
     row = lax.broadcasted_iota(jnp.int32, (8, LANE), 0)
-    picks = [(row == k).astype(f32).astype(bf16) for k in range(4)]
+    pick = (row == 0).astype(f32).astype(bf16)
     quarter = lax.broadcasted_iota(jnp.int32, (64, LANE), 1) // 32
     wanted = quarter.astype(f32)
 
@@ -170,23 +169,29 @@
         return out
 
     share = depth // sources
-    together = 2
+    together = 4
 
     @pl.loop(0, sources // together)
     def _(i):
+        run = got.at[pl.ds(pl.multiple_of(i * together * size, 8), together * size), :]
         for e in range(together):
             d = i * together + e
             at = pl.ds(pl.multiple_of(d * share, 8), share)
             for chain in chains:
                 chain[at, :] = jnp.zeros((share, LANE), f32)
-            part = turns(got[d, :64, :])
-            marks = quarters[d].astype(bf16)
-            for k in range(4):
+            part = turns(run[e * size : e * size + 64, :])
+            for half in range(2):
+                cell = run[e * size + 64 + half : e * size + 65 + half, :]
                 mark = lax.dot_general(
-                    marks, picks[k], (((0,), (0,)), ((), ())), preferred_element_type=f32
+                    jnp.broadcast_to(cell - 4.0 * jnp.floor(cell * 0.25), (8, LANE)).astype(bf16),
+                    pick,
+                    (((0,), (0,)), ((), ())),
+                    preferred_element_type=f32,
                 )
-                one = jnp.where(mark == wanted, repeat(part, k), 0.0)
-                spread[pl.ds(pl.multiple_of(d * 256 + k * 64, 64), 64), :] = one
+                for k in (2 * half, 2 * half + 1):
+                    first = (k % 2) * 64
+                    one = jnp.where(mark[first : first + 64] == wanted, repeat(part, k), 0.0)
+                    spread[pl.ds(pl.multiple_of(d * 256 + k * 64, 64), 64), :] = one
 
     step = 16
 
@@ -242,7 +247,7 @@
         pltpu.make_async_copy(field.at[ct], forced.at[ct], out_sem.at[ct]).wait()
 
 
-def force(places, got, quarters, background, decay, row_count, groups):
+def force(places, got, background, decay, row_count, groups):
     rows, columns = background.shape
     tiles = columns // LANE
     total = places.shape[0]
@@ -256,7 +261,6 @@
         ),
         in_specs=[
             pl.BlockSpec(memory_space=pltpu.SMEM),
-            whole,
             whole,
             pl.BlockSpec(memory_space=pl.ANY),
             whole,
@@ -272,7 +276,7 @@
         compiler_params=vmem(58),
         cost_estimate=cost(0, 16 << 20),
         name="force",
-    )(places, got, quarters, background, decay)
+    )(places, got, background, decay)
 
 
 def lon_weights(length, columns):
@@ -844,9 +848,8 @@
     ranks = route_ranks(owners, sub_count)
     row, column = obs_cell // lon_count, obs_cell % lon_count
     place = ((row // 4) * lon_count + column) * 4 + row % 4
-    lines = capacity // LANE
     message = pack(owners * capacity + ranks, place, obs_columns, sub_count)
-    got = lax.all_to_all(message.reshape(sub_count, -1, LANE), "sub", 0, 0, tiled=True)
+    got = lax.all_to_all(message.reshape(sub_count, 1, -1), "sub", 0, 0, tiled=True)
 
     vert_decay = jnp.exp(-1.0 / vert_length)
     coef = level_coefficients(vert_decay)
@@ -866,10 +869,8 @@
 
     ready = (got, weights, own_weights, decay, hub_lat, coef, vert_decay)
     got, weights, own_weights, decay, hub_lat, coef, vert_decay = lax.optimization_barrier(ready)
-    places = got[:, capacity // 4 : capacity // 4 + lines, :].reshape(-1).astype(jnp.int32)
-    quarters = (places & 3).astype(f32).reshape(sub_count, 4, capacity // 4)
-    quarters = jnp.pad(quarters, ((0, 0), (0, 4), (0, 0)))
-    forced, moments = force(places >> 2, got, quarters, tile_field, decay, row_count, groups)
+    places = got[:, 0, capacity * groups :].reshape(-1).astype(jnp.int32)
+    forced, moments = force(places >> 2, got.reshape(-1, LANE), tile_field, decay, row_count, groups)
     smooth, entering = exchange(
         forced,
         moments.reshape(sub_count, 4 * tiles, LANE),

time: 163 us -> 161 us (0.988)
  waiting for transfers between devices: 8.54 us -> 6.22 us
  Pallas kernels: 112 us -> 114 us
    all_to_all x1, waiting for transfers between devices: 8.54 us -> 6.22 us  [per_device(): lax.all_to_all(message.reshape(sub_count, 1, -1), 'sub', 0, 0, tiled=True)]
    pallas_call x1, Pallas kernels: 78.4 us -> 80.5 us  [exchange(): pl.pallas_call(functools.partial(exchange_kernel, row_count, variables),...]
where the time goes in v8:
time: 161 us
  Pallas kernels  114 us (71%)
  other arithmetic  14.6 us (9%)
  local copies, waits for them, and re-layouts  12.3 us (8%)
  starting transfers between devices  12.1 us (8%)
  waiting for transfers between devices  6.22 us (4%)
    pallas_call x1, Pallas kernels, exchange(): pl.pallas_call(functools.partial(exchange_kernel, row_count, variables),...  80.5 us
    pallas_call x1, Pallas kernels, force(): pl.pallas_call(functools.partial(forced_kernel, row_count, groups), out_s...  21.6 us
    all_to_all x1, starting transfers between devices, per_device(): lax.all_to_all(message.reshape(sub_count, 1, -1), 'sub', 0, 0, tiled=True)  12.1 us
    pallas_call x1, Pallas kernels, pack(): pl.pallas_call(pack_kernel, out_shape=jax.ShapeDtypeStruct((targets * 66,...  6.86 us
    all_to_all x1, waiting for transfers between devices, per_device(): lax.all_to_all(message.reshape(sub_count, 1, -1), 'sub', 0, 0, tiled=True)  6.22 us
    convert_element_type x3, other arithmetic, thirds(): high = high.astype(bf16)  5.23 us
    pallas_call x1, Pallas kernels, level_states(): pl.pallas_call(level_states_kernel, out_shape=jax.ShapeDtypeStruct(shape,...  5.05 us
    unnamed x16, local copies, waits for them, and re-layouts  4.13 us
  transfers between devices with their start and end apart: 1, of which 1 were waited for; matrix products, arithmetic and copies ran while one was open for 9% of the time, Pallas kernels for 0%

profile of v8, /device:TPU:1, one launch (start us, length us, event | category | flops | bytes accessed | tf_op | source)
XLA Modules:
  0.0 160.9 jit_solution(7825110119326395556)
XLA Ops:
  0.0 0.7 broadcast_multiply_fusion.1
  0.7 0.9 convert_reduce_fusion
  1.7 0.1 reduce_window_sum.11
  1.7 1.1 fusion.7
  2.8 0.0 copy-start.6
  2.8 1.3 bitcast_add_fusion.slot_row
  4.2 1.4 fusion.23
  5.5 0.6 bitcast_add_fusion.1.slots
  6.1 6.9 %pack.1 = f32[2112,128]{1,0:T(8,128)} custom-call(s32[4096]{0:T(1024)} %bitcast_add_fusion.1.slots, s32[1,4096]{1,0:T(1,128)} %bitcast_add_fusion.slot_row, s32[1,4096]{1,0:T(1,128)} %bitcast.156, f32[8,4,4096]{2,1,0:T(4,128)} %values.1), custom_call_target="tpu_custom_call" | custom-call | bytes 4194304 | tf_op jit(solution)/shard_map/pack/pallas_call | solution.py:98
  13.0 12.1 %all-to-all-start = ((f32[32,1,8448]{2,1,0:T(1,128)}), f32[32,1,8448]{2,1,0:T(1,128)}, u32[]{:S(2)}, u32[]{:S(2)}) async-start(f32[32,1,8448]{2,1,0:T(1,128)} %bitcast.150), calls=%async_computation | async-start | bytes 2162688 | tf_op jit(solution)/shard_map/all_to_all | solution.py:852
  25.2 0.1 copy.36
  25.3 0.3 slice_reduce_fusion.7
  25.6 0.1 fusion.11
  25.8 0.1 fusion.19
  26.0 0.1 divide_exponential_fusion.2
  26.0 0.4 reshape.1434
  26.4 0.6 reshape.1436.vert
  27.1 0.1 copy.37
  27.2 0.1 copy.29
  27.3 0.1 broadcast_in_dim_reshape.3
  27.4 0.1 copy.33
  27.5 0.1 copy.34
  27.5 0.6 pad.18.decay
  28.1 0.1 reshape.1435
  28.3 0.1 divide_exponential_fusion.6
  28.4 2.0 %copy.30 = f32[32,128,4]{2,1,0:T(8,128)} copy(f32[32,128,4]{1,0,2:T(8,128)S(1)} %pad_maximum_fusion.3) | data formatting | bytes 131072 | tf_op jit(solution)/shard_map/concatenate | solution.py:296
  30.3 0.1 add.321
  30.4 0.2 add_multiply_fusion.1
  30.6 0.6 reduce-precision_convert_fusion.1
  31.1 0.3 pad_maximum_fusion.2.back
  31.5 0.7 constant_dynamic-slice_fusion.2.own_back
  32.2 0.1 fusion.17
  32.4 3.6 %reduce-precision_convert_fusion.2 = (bf16[32,128,128]{2,1,0:T(8,128)(2,1)S(1)}, bf16[32,128,128]{2,1,0:T(8,128)(2,1)S(1)}, f32[32,128,128]{2,1,0:T(8,128)S(1)}) fusion(pred[128,128]{1,0:T(8,128)(4,1)S(1)} %get-tuple-element.60, f32[32]{0:T(128)S(1)} %exponential-minus-one_negate_fusion, f32[32]{0:T(128)S(1)} %broadcast_in_dim_reshape.3, ...), kind=kLoop, calls=%fused_computation.11 | loop fusion | flops 7340032 | bytes 4489856 | tf_op jit(solution)/shard_map/convert_element_type | solution.py:331
  36.0 0.0 copy-start.3
  36.0 0.3 pad_maximum_fusion.1.mix
  36.4 0.7 constant_dynamic-slice_fusion.3.own_mix
  37.0 1.3 copy-done.3
  38.3 1.0 reduce-precision_convert_fusion
  39.4 1.4 pad_maximum_fusion.first
  40.8 2.7 %copy-done = bf16[32,384,256]{2,1,0:T(8,128)(2,1)} copy-done((bf16[32,384,256]{2,1,0:T(8,128)(2,1)}, bf16[32,384,256]{2,1,0:T(8,128)(2,1)S(1)}, u32[]{:S(2)}) %copy-start) | copy-done | bytes 6291480
  43.4 0.7 constant_dynamic-slice_fusion.4.own_first
  44.1 6.2 %all-to-all-done = f32[32,1,8448]{2,1,0:T(1,128)} async-done(((f32[32,1,8448]{2,1,0:T(1,128)}), f32[32,1,8448]{2,1,0:T(1,128)}, u32[]{:S(2)}, u32[]{:S(2)}) %all-to-all-start) | async-done | bytes 1081376 | tf_op jit(solution)/shard_map/all_to_all | solution.py:852
  50.3 0.7 broadcast_in_dim.42.coef
  51.0 1.1 broadcast_in_dim.41.decay.table
  52.1 1.4 convert_shift-right-arithmetic_fusion
  53.5 21.6 %force.1 = (f32[12,768,128]{2,1,0:T(8,128)}, f32[1536,128]{1,0:T(8,128)}) custom-call(s32[8192]{0:T(1024)} %bitcast.155, f32[2112,128]{1,0:T(8,128)} %bitcast.16.got, f32[768,1536]{1,0:T(8,128)} %bitcast.148, f32[1536,128]{1,0:T(8,128)} %broadcast_in_dim.41.decay.table), custom_call_target="tpu_custom_call" | custom-call | bytes 16777216 | tf_op jit(solution)/shard_map/force/pallas_call | solution.py:256
  75.2 80.5 %exchange.1 = (f32[12,768,128]{2,1,0:T(8,128)}, f32[8,288,128]{2,1,0:T(8,128)}) custom-call(f32[12,768,128]{2,1,0:T(8,128)} %get-tuple-element.22.field, f32[32,48,128]{2,1,0:T(8,128)} %bitcast.152, f32[24,128]{1,0:T(8,128)} %pad.18.decay, f32[1536,128]{1,0:T(8,128)} %broadcast_in_dim.41.decay.table, bf16[32,384,256]{2,1,0:T(8,128)(2,1)} %copy-done, ...), custom_call_target="tpu_custom_call" | custom-call | flops 2717908992 | bytes 62914560 | tf_op jit(solution)/shard_map/exchange/pallas_call | solution.py:726
  155.7 5.1 %level_states.1 = f32[8,4,24,1536]{3,2,1,0:T(8,128)} custom-call(f32[12,8,4,24,128]{4,3,2,1,0:T(8,128)} %bitcast.149, f32[32]{0:T(128)} %reshape.1436.vert, f32[4,2,2,6,24,128]{5,4,3,2,1,0:T(8,128)} %bitcast.151), custom_call_target="tpu_custom_call" | custom-call | bytes 11534336 | tf_op jit(solution)/shard_map/level_states/pallas_call | solution.py:805
  (32 shorter events, 0.3 us)
Async XLA Ops:
  2.8 22.4 %copy-start.6 = (f32[8,4]{0,1:T(4,128)S(1)}, f32[8,4]{0,1:T(4,128)}, u32[]{:S(2)}) copy-start(f32[8,4]{0,1:T(4,128)} %param.13) | copy-start | bytes 388
  5.5 20.4 %copy-start.4 = (f32[8,4,768]{2,1,0:T(4,128)S(1)}, f32[8,4,768]{2,1,0:T(4,128)}, u32[]{:S(2)}) copy-start(f32[8,4,768]{2,1,0:T(4,128)} %param.11) | copy-start | bytes 294916
  13.0 14.2 %copy-start.5 = (f32[8,4]{0,1:T(4,128)S(1)}, f32[8,4]{0,1:T(4,128)}, u32[]{:S(2)}) copy-start(f32[8,4]{0,1:T(4,128)} %param.12) | copy-start | bytes 388
  13.0 37.3 %all-to-all-start = ((f32[32,1,8448]{2,1,0:T(1,128)}), f32[32,1,8448]{2,1,0:T(1,128)}, u32[]{:S(2)}, u32[]{:S(2)}) async-start(f32[32,1,8448]{2,1,0:T(1,128)} %bitcast.150), calls=%async_computation | async-start | bytes 2162688 | tf_op jit(solution)/shard_map/all_to_all | solution.py:852
  31.5 4.5 %copy-start.1 = (bf16[32,384,128]{2,1,0:T(8,128)(2,1)}, bf16[32,384,128]{2,1,0:T(8,128)(2,1)S(1)}, u32[]{:S(2)}) copy-start(bf16[32,384,128]{2,1,0:T(8,128)(2,1)S(1)} %pad_maximum_fusion.2.back) | copy-start | bytes 9437188
  36.0 2.3 %copy-start.3 = (f32[32,128,4]{2,1,0:T(8,128)S(1)}, f32[32,128,4]{2,1,0:T(8,128)}, u32[]{:S(2)}) copy-start(f32[32,128,4]{2,1,0:T(8,128)} %copy.30) | copy-start | bytes 196612
  36.4 3.0 %copy-start.2 = (bf16[32,384,128]{2,1,0:T(8,128)(2,1)}, bf16[32,384,128]{2,1,0:T(8,128)(2,1)S(1)}, u32[]{:S(2)}) copy-start(bf16[32,384,128]{2,1,0:T(8,128)(2,1)S(1)} %pad_maximum_fusion.1.mix) | copy-start | bytes 9437188
  40.8 2.7 %copy-start = (bf16[32,384,256]{2,1,0:T(8,128)(2,1)}, bf16[32,384,256]{2,1,0:T(8,128)(2,1)S(1)}, u32[]{:S(2)}) copy-start(bf16[32,384,256]{2,1,0:T(8,128)(2,1)S(1)} %pad_maximum_fusion.first) | copy-start | bytes 18874372

commit v9 on v8

--- a/solution.py
+++ b/solution.py
@@ -34,7 +34,7 @@
     return rank.reshape(count).astype(jnp.int32)
 
 
-def pack_kernel(slots, slot_row, place_row, values, packed, rows, big):
+def pack_kernel(lon_count, slots, slot_row, cell_row, values, packed, rows, big):
     levels, _, count = values.shape
     total = big.shape[0]
     targets = total // 256
@@ -48,7 +48,10 @@
         )
         rows[j * LANE : (j + 1) * LANE, :] = jnp.concatenate([part] * 4, axis=0).T
 
-    slot, place = slot_row[...], place_row[...]
+    slot, cell = slot_row[...], cell_row[...]
+    line = ((cell.astype(f32) + 0.5) * (1.0 / lon_count)).astype(jnp.int32)
+    column = cell - line * lon_count
+    place = (lax.shift_right_logical(line, 2) * lon_count + column) * 4 + (line & 3)
     owner, rank = lax.shift_right_logical(slot, 8), slot & 255
     mine = owner == lax.broadcasted_iota(jnp.int32, (targets, count), 0)
     spot = (rank == lax.broadcasted_iota(jnp.int32, (256, count), 0)).astype(f32).astype(bf16)
@@ -91,12 +94,12 @@
 PACK_SIDE = 8
 
 
-def pack(slots, place, values, targets):
+def pack(slots, cells, values, targets, lon_count):
     count = values.shape[2]
     total = targets * 256
     whole = pl.BlockSpec(memory_space=pltpu.VMEM)
     return pl.pallas_call(
-        pack_kernel,
+        functools.partial(pack_kernel, lon_count),
         out_shape=jax.ShapeDtypeStruct((targets * 66, LANE), f32),
         in_specs=[pl.BlockSpec(memory_space=pltpu.SMEM), whole, whole, whole],
         out_specs=whole,
@@ -104,7 +107,7 @@
         compiler_params=vmem(60),
         cost_estimate=cost(0, 4 << 20),
         name="pack",
-    )(slots, slots.reshape(1, count), place.reshape(1, count), values)
+    )(slots, slots.reshape(1, count), cells.reshape(1, count), values)
 
 
 def lat_sweeps(sets, decays, starts):
@@ -846,9 +849,7 @@
     capacity = 2 * owners.shape[0] // sub_count
 
     ranks = route_ranks(owners, sub_count)
-    row, column = obs_cell // lon_count, obs_cell % lon_count
-    place = ((row // 4) * lon_count + column) * 4 + row % 4
-    message = pack(owners * capacity + ranks, place, obs_columns, sub_count)
+    message = pack(owners * capacity + ranks, obs_cell, obs_columns, sub_count, lon_count)
     got = lax.all_to_all(message.reshape(sub_count, 1, -1), "sub", 0, 0, tiled=True)
 
     vert_decay = jnp.exp(-1.0 / vert_length)

time: 161 us -> 161 us (level); the launches traced: 161 us -> 159 us
    pallas_call x1, Pallas kernels: 80.5 us -> 78.8 us  [exchange(): pl.pallas_call(functools.partial(exchange_kernel, row_count, variables),...]
    add x3 -> x2, other arithmetic: 3.3 us -> 1.95 us  [per_device(): owners * capacity + ranks]
where the time goes in v9:
time: 161 us; the launch traced here: 159 us
  Pallas kernels  113 us (70%)
  other arithmetic  13.3 us (8%)
  local copies, waits for them, and re-layouts  12.3 us (8%)
  starting transfers between devices  12.1 us (8%)
  waiting for transfers between devices  6.22 us (4%)
    pallas_call x1, Pallas kernels, exchange(): pl.pallas_call(functools.partial(exchange_kernel, row_count, variables),...  78.8 us
    pallas_call x1, Pallas kernels, force(): pl.pallas_call(functools.partial(forced_kernel, row_count, groups), out_s...  22.3 us
    all_to_all x1, starting transfers between devices, per_device(): lax.all_to_all(message.reshape(sub_count, 1, -1), 'sub', 0, 0, tiled=True)  12.1 us
    pallas_call x1, Pallas kernels, pack(): pl.pallas_call(functools.partial(pack_kernel, lon_count), out_shape=jax.S...  6.86 us
    all_to_all x1, waiting for transfers between devices, per_device(): lax.all_to_all(message.reshape(sub_count, 1, -1), 'sub', 0, 0, tiled=True)  6.22 us
    convert_element_type x3, other arithmetic, thirds(): high = high.astype(bf16)  5.23 us
    pallas_call x1, Pallas kernels, level_states(): pl.pallas_call(level_states_kernel, out_shape=jax.ShapeDtypeStruct(shape,...  5.05 us
    unnamed x16, local copies, waits for them, and re-layouts  4.13 us
  transfers between devices with their start and end apart: 1, of which 1 were waited for; matrix products, arithmetic and copies ran while one was open for 9% of the time, Pallas kernels for 0%

profile of v9, /device:TPU:1, one launch (start us, length us, event | category | flops | bytes accessed | tf_op | source)
XLA Modules:
  0.0 158.5 jit_solution(14668406211391318702)
XLA Ops:
  0.0 0.7 broadcast_multiply_fusion.1
  0.7 0.9 convert_reduce_fusion
  1.7 0.1 reduce_window_sum.11
  1.7 1.1 fusion.7
  2.8 0.0 copy-start.6
  2.8 1.3 bitcast_add_fusion.slot_row
  4.2 0.6 bitcast_add_fusion.1.slots
  4.8 6.9 %pack.1 = f32[2112,128]{1,0:T(8,128)} custom-call(s32[4096]{0:T(1024)} %bitcast_add_fusion.1.slots, s32[1,4096]{1,0:T(1,128)} %bitcast_add_fusion.slot_row, s32[1,4096]{1,0:T(1,128)} %bitcast.161, f32[8,4,4096]{2,1,0:T(4,128)} %values.1), custom_call_target="tpu_custom_call" | custom-call | bytes 4194304 | tf_op jit(solution)/shard_map/pack/pallas_call | solution.py:101
  11.6 12.1 %all-to-all-start = ((f32[32,1,8448]{2,1,0:T(1,128)}), f32[32,1,8448]{2,1,0:T(1,128)}, u32[]{:S(2)}, u32[]{:S(2)}) async-start(f32[32,1,8448]{2,1,0:T(1,128)} %bitcast.150), calls=%async_computation | async-start | bytes 2162688 | tf_op jit(solution)/shard_map/all_to_all | solution.py:853
  23.9 0.1 copy.36
  24.0 0.3 slice_reduce_fusion.7
  24.3 0.1 fusion.11
  24.4 0.1 fusion.19
  24.6 0.0 copy-done.4
  24.6 0.1 divide_exponential_fusion.2
  24.7 0.4 reshape.1434
  25.1 0.6 reshape.1436.vert
  25.7 0.1 copy.37
  25.8 0.1 copy.29
  25.9 0.1 broadcast_in_dim_reshape.3
  26.0 0.1 copy.33
  26.1 0.1 copy.34
  26.2 0.6 pad.18.decay
  26.8 0.1 reshape.1435
  26.9 0.1 divide_exponential_fusion.6
  27.0 2.0 %copy.30 = f32[32,128,4]{2,1,0:T(8,128)} copy(f32[32,128,4]{1,0,2:T(8,128)S(1)} %pad_maximum_fusion.3) | data formatting | bytes 131072 | tf_op jit(solution)/shard_map/concatenate | solution.py:299
  29.0 0.1 add.299
  29.1 0.2 add_multiply_fusion.1
  29.2 0.6 reduce-precision_convert_fusion.1
  29.8 0.3 pad_maximum_fusion.2.back
  30.1 0.7 constant_dynamic-slice_fusion.2.own_back
  30.8 0.1 fusion.17
  31.0 3.6 %reduce-precision_convert_fusion.2 = (bf16[32,128,128]{2,1,0:T(8,128)(2,1)S(1)}, bf16[32,128,128]{2,1,0:T(8,128)(2,1)S(1)}, f32[32,128,128]{2,1,0:T(8,128)S(1)}) fusion(pred[128,128]{1,0:T(8,128)(4,1)S(1)} %get-tuple-element.60, f32[32]{0:T(128)S(1)} %exponential-minus-one_negate_fusion, f32[32]{0:T(128)S(1)} %broadcast_in_dim_reshape.3, ...), kind=kLoop, calls=%fused_computation.11 | loop fusion | flops 7340032 | bytes 4489856 | tf_op jit(solution)/shard_map/convert_element_type | solution.py:334
  34.7 0.0 copy-start.3
  34.7 0.3 pad_maximum_fusion.1.mix
  35.0 0.7 constant_dynamic-slice_fusion.3.own_mix
  35.7 1.3 copy-done.3
  37.0 1.0 reduce-precision_convert_fusion
  38.0 1.4 pad_maximum_fusion.first
  39.4 2.7 %copy-done = bf16[32,384,256]{2,1,0:T(8,128)(2,1)} copy-done((bf16[32,384,256]{2,1,0:T(8,128)(2,1)}, bf16[32,384,256]{2,1,0:T(8,128)(2,1)S(1)}, u32[]{:S(2)}) %copy-start) | copy-done | bytes 6291480
  42.1 0.7 constant_dynamic-slice_fusion.4.own_first
  42.8 6.2 %all-to-all-done = f32[32,1,8448]{2,1,0:T(1,128)} async-done(((f32[32,1,8448]{2,1,0:T(1,128)}), f32[32,1,8448]{2,1,0:T(1,128)}, u32[]{:S(2)}, u32[]{:S(2)}) %all-to-all-start) | async-done | bytes 1081376 | tf_op jit(solution)/shard_map/all_to_all | solution.py:853
  49.0 0.7 broadcast_in_dim.42.coef
  49.6 1.1 broadcast_in_dim.41.decay.table
  50.8 1.4 convert_shift-right-arithmetic_fusion
  52.2 22.3 %force.1 = (f32[12,768,128]{2,1,0:T(8,128)}, f32[1536,128]{1,0:T(8,128)}) custom-call(s32[8192]{0:T(1024)} %bitcast.155, f32[2112,128]{1,0:T(8,128)} %bitcast.16.got, f32[768,1536]{1,0:T(8,128)} %bitcast.148, f32[1536,128]{1,0:T(8,128)} %broadcast_in_dim.41.decay.table), custom_call_target="tpu_custom_call" | custom-call | bytes 16777216 | tf_op jit(solution)/shard_map/force/pallas_call | solution.py:259
  74.5 78.8 %exchange.1 = (f32[12,768,128]{2,1,0:T(8,128)}, f32[8,288,128]{2,1,0:T(8,128)}) custom-call(f32[12,768,128]{2,1,0:T(8,128)} %get-tuple-element.22.field, f32[32,48,128]{2,1,0:T(8,128)} %bitcast.152, f32[24,128]{1,0:T(8,128)} %pad.18.decay, f32[1536,128]{1,0:T(8,128)} %broadcast_in_dim.41.decay.table, bf16[32,384,256]{2,1,0:T(8,128)(2,1)} %copy-done, ...), custom_call_target="tpu_custom_call" | custom-call | flops 2717908992 | bytes 62914560 | tf_op jit(solution)/shard_map/exchange/pallas_call | solution.py:729
  153.3 5.1 %level_states.1 = f32[8,4,24,1536]{3,2,1,0:T(8,128)} custom-call(f32[12,8,4,24,128]{4,3,2,1,0:T(8,128)} %bitcast.149, f32[32]{0:T(128)} %reshape.1436.vert, f32[4,2,2,6,24,128]{5,4,3,2,1,0:T(8,128)} %bitcast.151), custom_call_target="tpu_custom_call" | custom-call | bytes 11534336 | tf_op jit(solution)/shard_map/level_states/pallas_call | solution.py:808
  (31 shorter events, 0.3 us)
Async XLA Ops:
  2.8 21.1 %copy-start.6 = (f32[8,4]{0,1:T(4,128)S(1)}, f32[8,4]{0,1:T(4,128)}, u32[]{:S(2)}) copy-start(f32[8,4]{0,1:T(4,128)} %param.13) | copy-start | bytes 388
  4.2 20.4 %copy-start.4 = (f32[8,4,768]{2,1,0:T(4,128)S(1)}, f32[8,4,768]{2,1,0:T(4,128)}, u32[]{:S(2)}) copy-start(f32[8,4,768]{2,1,0:T(4,128)} %param.11) | copy-start | bytes 294916
  11.6 14.2 %copy-start.5 = (f32[8,4]{0,1:T(4,128)S(1)}, f32[8,4]{0,1:T(4,128)}, u32[]{:S(2)}) copy-start(f32[8,4]{0,1:T(4,128)} %param.12) | copy-start | bytes 388
  11.6 37.3 %all-to-all-start = ((f32[32,1,8448]{2,1,0:T(1,128)}), f32[32,1,8448]{2,1,0:T(1,128)}, u32[]{:S(2)}, u32[]{:S(2)}) async-start(f32[32,1,8448]{2,1,0:T(1,128)} %bitcast.150), calls=%async_computation | async-start | bytes 2162688 | tf_op jit(solution)/shard_map/all_to_all | solution.py:853
  30.1 4.5 %copy-start.1 = (bf16[32,384,128]{2,1,0:T(8,128)(2,1)}, bf16[32,384,128]{2,1,0:T(8,128)(2,1)S(1)}, u32[]{:S(2)}) copy-start(bf16[32,384,128]{2,1,0:T(8,128)(2,1)S(1)} %pad_maximum_fusion.2.back) | copy-start | bytes 9437188
  34.7 2.3 %copy-start.3 = (f32[32,128,4]{2,1,0:T(8,128)S(1)}, f32[32,128,4]{2,1,0:T(8,128)}, u32[]{:S(2)}) copy-start(f32[32,128,4]{2,1,0:T(8,128)} %copy.30) | copy-start | bytes 196612
  35.0 3.0 %copy-start.2 = (bf16[32,384,128]{2,1,0:T(8,128)(2,1)}, bf16[32,384,128]{2,1,0:T(8,128)(2,1)S(1)}, u32[]{:S(2)}) copy-start(bf16[32,384,128]{2,1,0:T(8,128)(2,1)S(1)} %pad_maximum_fusion.1.mix) | copy-start | bytes 9437188
  39.4 2.7 %copy-start = (bf16[32,384,256]{2,1,0:T(8,128)(2,1)}, bf16[32,384,256]{2,1,0:T(8,128)(2,1)S(1)}, u32[]{:S(2)}) copy-start(bf16[32,384,256]{2,1,0:T(8,128)(2,1)S(1)} %pad_maximum_fusion.first) | copy-start | bytes 18874372
